TPU v7x, 32 devices: a whole 2x2x4 slice. The times are simulated.
32 devices in a mesh: dp: 8 (over z, y), tensor: 4 (over x, core).
Axes of the slice: x: 2, y: 2, z: 4, core: 2. Of those that a mesh axis runs over, the one named last changes fastest.
Arguments:
- tokens: bfloat16 [2048, 768], P('dp'), may hold values from -6 to 6
- segments: int32 [2048], P('dp'), may hold values from -1 to 255, as said below
- first_gain: float32 [768], replicated, may hold values from 0.1 to 1.9
- first_shift: float32 [768], replicated, may hold values from -1.75 to 1.75
- second_gain: float32 [768], replicated, may hold values from 0.1 to 1.9
- second_shift: float32 [768], replicated, may hold values from -1.75 to 1.75
- inlet: bfloat16 [768, 2304], P(None, 'tensor'), may hold values from -1 to 1
- offsets: float32 [12, 192], P('tensor'), may hold values from -3 to 3
- outlet: bfloat16 [768, 768], P('tensor'), may hold values from -1.25 to 1.25
- outlet_bias: float32 [768], replicated, may hold values from -1.75 to 1.75
- expand: bfloat16 [768, 3072], P(None, 'tensor'), may hold values from -0.21875 to 0.21875
- thresholds: float32 [3072], P('tensor'), may hold values from -3 to 3
- contract: bfloat16 [3072, 768], P('tensor'), may hold values from -0.109375 to 0.109375
- contract_bias: float32 [768], replicated, may hold values from -1.75 to 1.75
- cotangent: bfloat16 [2048, 768], P('dp'), may hold values from -6 to 6
Outputs:
- mixed: bfloat16 [2048, 768], P('dp')
- input_grad: bfloat16 [2048, 768], P('dp')
- inlet_grad: float32 [768, 2304], P('dp', 'tensor')
- offsets_grad: float32 [12, 192], P('tensor', 'dp')
- outlet_grad: float32 [768, 768], P('tensor', 'dp')
- expand_grad: float32 [768, 3072], P('dp', 'tensor')
- thresholds_grad: float32 [4, 768], P('tensor', 'dp')
- contract_grad: float32 [3072, 768], P('tensor', 'dp')
- bias_grad: float32 [768], P('dp')
- norm_grads: float32 [4, 768], P(None, 'dp')
Inputs may be any that keep to these rules, and one draw needn't show every extreme that they name: `segments`: within each device's 256 slots the used slots come first; their values start at 0 and rise by one from sequence to sequence; each sequence fills 1 to 128 consecutive slots; unused slots hold -1. Some device uses all its slots and holds a sequence of exactly 128 slots; some device uses half of them; some device uses all its slots as 256 sequences of one slot.
All inputs are finite; a program needn't handle non-finite values.
Results may differ from a plain program's by a relative error of at most 0.0067.
Values may be sent and summed in bfloat16 or wider, within the bound.
No kernel may reach another device: no remote copies, remote signals or barrier semaphores. Data moves between devices by JAX's collectives and lax.ppermute only.
A program may use at most 64 MiB of HBM per device.

v0:
```python
import math

import jax
import jax.numpy as jnp
from jax import lax
from jax.sharding import PartitionSpec as P

ROT = 16


EPS = 1e-05


def layer_norm(value, gain, shift):
    center = value - jnp.mean(value, axis=-1, keepdims=True)
    inverse = lax.rsqrt(jnp.mean(center * center, axis=-1, keepdims=True) + EPS)
    scaled = center * inverse
    return (scaled * gain + shift, scaled, inverse)


def norm_back(normed_grad, scaled, inverse, gain):
    lifted = normed_grad * gain
    return inverse * (
        lifted
        - jnp.mean(lifted, axis=-1, keepdims=True)
        - scaled * jnp.mean(lifted * scaled, axis=-1, keepdims=True)
    )


def positions_of(labels):
    index = jnp.arange(labels.shape[0], dtype=jnp.int32)
    before = jnp.concatenate([jnp.full((1,), -2, jnp.int32), labels[:-1]])
    first = jnp.where(labels != before, index, jnp.zeros_like(index))
    return index - lax.cummax(first, axis=0)


def rotary_tables(labels):
    angles_pos = positions_of(labels).astype(jnp.float32)
    freq = jnp.exp(jnp.arange(ROT // 2, dtype=jnp.float32) * (-2.0 * math.log(10000.0) / ROT))
    angle = angles_pos[:, None] * freq[None, :]
    return (jnp.cos(angle)[:, None, :], jnp.sin(angle)[:, None, :])


def rotate(field, cosine, sine, direction):
    half = cosine.shape[-1]
    first = field[..., :half]
    second = field[..., half : 2 * half]
    rest = field[..., 2 * half :]
    new_first = first * cosine - direction * second * sine
    new_second = second * cosine + direction * first * sine
    return jnp.concatenate([new_first, new_second, rest], axis=-1)


def gelu_pair(expanded):
    cumulative = 0.5 * (1.0 + lax.erf(expanded * (1.0 / math.sqrt(2.0))))
    density = jnp.exp(-0.5 * expanded * expanded) * (1.0 / math.sqrt(2.0 * math.pi))
    return (expanded * cumulative, cumulative + expanded * density)


def contract_rows(left, right):
    return lax.dot_general(
        left, right, (((0,), (0,)), ((), ())), preferred_element_type=jnp.float32
    )


def times_transposed(left, right):
    return lax.dot_general(
        left, right, (((1,), (1,)), ((), ())), preferred_element_type=jnp.float32
    )


def masked_scores(query_rows, keys, label_rows, label_keys, start):
    scores = (
        jnp.einsum("qhd,khd->hqk", query_rows, keys, preferred_element_type=jnp.float32) * 0.125
    )
    query_index = start + jnp.arange(query_rows.shape[0], dtype=jnp.int32)
    key_index = jnp.arange(keys.shape[0], dtype=jnp.int32)
    allowed = (label_rows[:, None] == label_keys[None, :]) & (
        key_index[None, :] <= query_index[:, None]
    )
    return jnp.where(allowed[None], scores, -jnp.inf)


def body(
    tokens,
    segments,
    first_gain,
    first_shift,
    second_gain,
    second_shift,
    inlet,
    offsets,
    outlet,
    outlet_bias,
    expand,
    thresholds,
    contract,
    contract_bias,
    cotangent,
):
    count = tokens.shape[0]
    heads = offsets.shape[0]
    head_size = offsets.shape[1] // 3
    residual = tokens.astype(jnp.float32)
    normed_full, scaled_one, inverse_one = layer_norm(residual, first_gain, first_shift)
    normed_one = normed_full.astype(jnp.bfloat16)
    normed_full, scaled_two, inverse_two = layer_norm(residual, second_gain, second_shift)
    normed_two = normed_full.astype(jnp.bfloat16)
    projected = (
        jnp.dot(normed_one, inlet, preferred_element_type=jnp.float32) + offsets.reshape(-1)
    ).reshape(count, heads, 3, head_size)
    cosine, sine = rotary_tables(segments)
    query = rotate(projected[:, :, 0], cosine, sine, 1.0).astype(jnp.bfloat16)
    key = rotate(projected[:, :, 1], cosine, sine, 1.0).astype(jnp.bfloat16)
    value = projected[:, :, 2].astype(jnp.bfloat16)
    width = min(512, count)
    start = 0
    end = start + width
    scores = masked_scores(query, key, segments, segments, start)
    peak = jnp.max(scores, axis=-1, keepdims=True)
    log_total = peak + jnp.log(jnp.sum(jnp.exp(scores - peak), axis=-1, keepdims=True))
    softmax = jnp.exp(scores - log_total).astype(jnp.bfloat16)
    pieces = jnp.einsum("hqk,khd->qhd", softmax, value, preferred_element_type=jnp.float32).astype(
        jnp.bfloat16
    )
    totals = [log_total]
    attended = pieces.reshape(count, heads * head_size)
    expanded = jnp.dot(normed_two, expand, preferred_element_type=jnp.float32) + thresholds
    active_full, slope = gelu_pair(expanded)
    active = active_full.astype(jnp.bfloat16)
    branch = jnp.dot(attended, outlet, preferred_element_type=jnp.float32) + jnp.dot(
        active, contract, preferred_element_type=jnp.float32
    )
    shift = outlet_bias + contract_bias
    summed = lax.psum(branch, "tensor")
    mixed = (residual + summed + shift).astype(jnp.bfloat16)
    live = (segments >= 0).astype(jnp.float32)
    grad_full = cotangent.astype(jnp.float32) * live[:, None]
    grad_out = grad_full.astype(jnp.bfloat16)
    bias_grad = jnp.sum(grad_full, axis=0)
    contract_grad = contract_rows(active, grad_out)
    outlet_grad = contract_rows(attended, grad_out)
    active_grad = times_transposed(grad_out, contract)
    expanded_grad = active_grad * slope
    expanded_back = expanded_grad.astype(jnp.bfloat16)
    expand_grad = contract_rows(normed_two, expanded_back)
    thresholds_grad = jnp.sum(expanded_grad, axis=0)[None, :]
    normed_two_grad = times_transposed(expanded_back, expand)
    attended_grad = (
        times_transposed(grad_out, outlet).astype(jnp.bfloat16).reshape(count, heads, head_size)
    )
    query_parts = []
    key_grad = jnp.zeros((count, heads, head_size), jnp.float32)
    value_grad = jnp.zeros((count, heads, head_size), jnp.float32)
    for number, start in enumerate(range(0, count, width)):
        end = start + width
        scores = masked_scores(query, key, segments, segments, start)
        weight_full = jnp.exp(scores - totals[number])
        softmax = weight_full.astype(jnp.bfloat16)
        prob_grad = jnp.einsum(
            "qhd,khd->hqk", attended_grad, value, preferred_element_type=jnp.float32
        )
        delta = jnp.sum(weight_full * prob_grad, axis=-1, keepdims=True)
        score_grad = (weight_full * (prob_grad - delta)).astype(jnp.bfloat16)
        query_parts.append(
            jnp.einsum("hqk,khd->qhd", score_grad, key, preferred_element_type=jnp.float32) * 0.125
        )
        key_grad = key_grad.at[:end].add(
            jnp.einsum("hqk,qhd->khd", score_grad, query, preferred_element_type=jnp.float32)
            * 0.125
        )
        value_grad = value_grad.at[:end].add(
            jnp.einsum("hqk,qhd->khd", softmax, attended_grad, preferred_element_type=jnp.float32)
        )
    query_grad = rotate(query_parts[0], cosine, sine, -1.0)
    key_grad = rotate(key_grad, cosine, sine, -1.0)
    inlet_full = jnp.stack([query_grad, key_grad, value_grad], axis=2).reshape(
        count, heads * 3 * head_size
    )
    inlet_back = inlet_full.astype(jnp.bfloat16)
    inlet_grad = contract_rows(normed_one, inlet_back)
    offsets_grad = jnp.sum(inlet_full, axis=0).reshape(heads, 3 * head_size)
    normed_one_grad = times_transposed(inlet_back, inlet)
    norm_terms = jnp.stack(
        [
            jnp.sum(normed_one_grad * scaled_one, axis=0),
            jnp.sum(normed_one_grad, axis=0),
            jnp.sum(normed_two_grad * scaled_two, axis=0),
            jnp.sum(normed_two_grad, axis=0),
        ]
    )
    local_grad = norm_back(normed_one_grad, scaled_one, inverse_one, first_gain) + norm_back(
        normed_two_grad, scaled_two, inverse_two, second_gain
    )
    summed_grad, norm_summed = lax.psum((local_grad, norm_terms), "tensor")
    input_grad = (grad_full + summed_grad).astype(jnp.bfloat16)
    (
        inlet_summed,
        outlet_summed,
        offsets_summed,
        norm_grads,
        expand_summed,
        contract_summed,
        thresholds_summed,
        bias_summed,
    ) = (
        lax.psum_scatter(inlet_grad, "dp", scatter_dimension=0, tiled=True),
        lax.psum_scatter(outlet_grad, "dp", scatter_dimension=1, tiled=True),
        lax.psum_scatter(offsets_grad, "dp", scatter_dimension=1, tiled=True),
        lax.psum_scatter(norm_summed, "dp", scatter_dimension=1, tiled=True),
        lax.psum_scatter(expand_grad, "dp", scatter_dimension=0, tiled=True),
        lax.psum_scatter(contract_grad, "dp", scatter_dimension=1, tiled=True),
        lax.psum_scatter(thresholds_grad, "dp", scatter_dimension=1, tiled=True),
        lax.psum_scatter(bias_grad, "dp", scatter_dimension=0, tiled=True),
    )
    return (
        mixed,
        input_grad,
        inlet_summed,
        offsets_summed,
        outlet_summed,
        expand_summed,
        thresholds_summed,
        contract_summed,
        bias_summed,
        norm_grads,
    )


def solution(mesh):
    placed = (
        P("dp", None),
        P("dp"),
        P(),
        P(),
        P(),
        P(),
        P(None, "tensor"),
        P("tensor", None),
        P("tensor", None),
        P(),
        P(None, "tensor"),
        P("tensor"),
        P("tensor", None),
        P(),
        P("dp", None),
    )
    return jax.shard_map(
        body,
        mesh=mesh,
        in_specs=placed,
        out_specs=(
            P("dp", None),
            P("dp", None),
            P("dp", "tensor"),
            P("tensor", "dp"),
            P("tensor", "dp"),
            P("dp", "tensor"),
            P("tensor", "dp"),
            P("tensor", "dp"),
            P("dp"),
            P(None, "dp"),
        ),
        check_vma=False,
    )
```

profile of v0, /device:TPU:0, one launch (start us, length us, event | category | flops | bytes accessed | tf_op | source)
XLA Modules:
  0.0 434.5 jit_solution(17160722668712963985)
XLA Ops:
  8.1 0.8 compare_convert_fusion
  8.8 1.1 convert_reduce_fusion
  10.0 1.2 fusion.25
  11.3 2.0 convolution_add_fusion.1
  13.3 1.3 fusion.65
  14.6 0.9 reshape_bitcast_fusion
  15.7 0.7 fusion.37
  16.4 0.1 fusion.48
  16.5 0.3 reduce-window.9
  16.8 0.1 slice.100
  16.9 0.1 slice_reduce_fusion
  17.0 0.1 fusion.49
  17.1 0.1 add.134
  17.2 0.4 convolution_convert_fusion
  17.6 1.7 convolution_add_fusion.2
  19.4 0.1 broadcast_multiply_fusion
  19.6 0.6 copy-done.23
  20.2 0.3 fusion.64
  20.6 0.1 exponential_reduce_fusion
  20.7 0.3 convolution_bitcast_fusion.1
  21.0 0.3 multiply_reduce_fusion
  21.3 0.2 multiply_convert_fusion
  21.5 0.3 fusion.1
  21.8 0.2 fusion.2
  22.2 0.5 copy-done.5
  22.8 0.1 copy-done.7
  22.8 0.3 copy-done.11
  23.2 0.4 copy-done.15
  23.6 0.5 fusion.40
  24.1 0.1 copy-done.29
  24.3 0.5 copy-done.45
  24.8 2.2 fusion.23
  27.0 1.0 copy.67
  28.0 0.0 all-reduce.6.cloned.1.call-start
  28.1 1.2 convolution_convert_fusion.1
  29.3 0.6 copy-done.17
  30.0 0.3 fusion.66
  30.4 1.4 convolution_add_fusion
  31.9 1.3 fusion.20
  33.3 0.8 copy-done.18
  34.1 1.3 convolution_bitcast_fusion
  35.5 2.0 fusion.55
  37.5 2.0 fusion.58
  39.6 0.9 copy-done.12
  40.6 2.1 fusion.38
  42.7 0.6 copy-done.46
  43.3 0.6 dynamic-slice.10
  45.2 0.2 fusion.35
  45.4 0.1 reshape.273
  45.5 35.2 %reduce-scatter.22.cloned.1.call-done = f32[96,1]{1,0:T(8,128)} async-done(((f32[768,1]{1,0:T(8,128)}), f32[96,1]{1,0:T(8,128)}) %reduce-scatter.22.cloned.1.call-update) | async-done | bytes 400
  80.6 1.4 copy.66
  82.0 63.1 %reduce-scatter.24.cloned.1.call-done = f32[96,4]{1,0:T(8,128)} async-done(((f32[768,4]{1,0:T(8,128)}), f32[96,4]{1,0:T(8,128)}) %reduce-scatter.24.cloned.1.call-update) | async-done | bytes 1552
  145.1 0.9 copy.68
  146.0 6.2 %psum.24 = f32[4,96]{1,0:T(4,128)} all-reduce(f32[4,96]{1,0:T(4,128)S(1)} %copy.68), channel_id=1, replica_groups=mesh['dp'=8,'tensor'=4] {'tensor'}, use_global_device_ids=true, to_apply=%region_27.28 | all-reduce | flops 384 | bytes 3072 | tf_op jit(solution)/shard_map/psum | solution.py:195
  152.2 2.1 fusion.32
  154.3 19.7 %all-reduce.2 = (f32[3,192]{1,0:T(4,128)S(1)}, f32[768]{0:T(1024)S(1)}) all-reduce(f32[3,192]{1,0:T(4,128)S(1)} %reshape.273, f32[768]{0:T(1024)S(1)} %get-tuple-element.68), channel_id=3, replica_groups=mesh['dp'=8,'tensor'=4] {'dp'}, use_global_device_ids=true, to_apply=%region_15.16.clone | all-reduce | flops 1344 | bytes 10752
  174.0 0.6 dynamic-slice.13
  174.6 0.6 constant_dynamic-slice_fusion
  175.3 0.9 fusion.27
  176.1 34.6 %reduce-scatter.20.cloned.1.call-done = f32[96,192]{1,0:T(8,128)} async-done(((f32[768,192]{1,0:T(8,128)}), f32[96,192]{1,0:T(8,128)}) %reduce-scatter.20.cloned.1.call-update) | async-done | bytes 73744
  210.7 1.6 copy.64
  212.4 69.0 %reduce-scatter.14.cloned.1.call-done = f32[96,576]{1,0:T(8,128)} async-done(((f32[768,576]{1,0:T(8,128)}), f32[96,576]{1,0:T(8,128)}) %reduce-scatter.14.cloned.1.call-update) | async-done | bytes 221200 | tf_op jit(solution)/shard_map/reduce_scatter | solution.py:207
  281.3 72.5 %reduce-scatter.18.cloned.1.call-done = f32[768,96]{0,1:T(8,128)} async-done(((f32[768,768]{0,1:T(8,128)}), f32[768,96]{0,1:T(8,128)}) %reduce-scatter.18.cloned.1.call-update) | async-done | bytes 294928 | tf_op jit(solution)/shard_map/reduce_scatter | solution.py:212
  353.8 73.2 %reduce-scatter.16.cloned.1.call-done = f32[96,768]{1,0:T(8,128)} async-done(((f32[768,768]{1,0:T(8,128)}), f32[96,768]{1,0:T(8,128)}) %reduce-scatter.16.cloned.1.call-update) | async-done | bytes 294928 | tf_op jit(solution)/shard_map/reduce_scatter | solution.py:211
  (125 shorter events, 0.9 us)
Async XLA Ops:
  8.0 5.2 %copy-start = (bf16[768,768]{1,0:T(8,128)(2,1)S(1)}, bf16[768,768]{1,0:T(8,128)(2,1)}, u32[]{:S(2)}) copy-start(bf16[768,768]{1,0:T(8,128)(2,1)} %param.35) | copy-start | bytes 3538948
  8.0 72.6 %reduce-scatter.22.cloned.1.call-start = ((), (), s32[]{:S(2)}) async-start(), calls=%async_computation.10 | async-start | bytes 442368
  8.8 8.3 %copy-start.33 = (f32[256]{0:T(256)}, f32[256]{0:T(256)S(1)}, u32[]{:S(2)}) copy-start(f32[256]{0:T(256)S(1)} %compare_convert_fusion) | copy-start | bytes 3076
  10.0 14.1 %copy-start.24 = (f32[256]{0:T(256)}, f32[256]{0:T(256)S(1)}, u32[]{:S(2)}) copy-start(f32[256]{0:T(256)S(1)} %broadcast_multiply_fusion.5) | copy-start | bytes 3076
  11.2 12.9 %copy-start.31 = (f32[256]{0:T(256)}, f32[256]{0:T(256)S(1)}, u32[]{:S(2)}) copy-start(f32[256]{0:T(256)S(1)} %add_rsqrt_fusion) | copy-start | bytes 3076
  11.2 2.0 copy-start.2
  13.3 2.4 copy-start.26
  13.3 3.8 copy-start.40
  13.3 3.9 copy-start.21
  14.6 2.9 copy-start.1
  14.6 2.9 copy-start.27
  14.6 2.9 copy-start.35
  15.6 129.5 %reduce-scatter.24.cloned.1.call-start = ((), (), s32[]{:S(2)}) async-start(), calls=%async_computation.11 | async-start | bytes 442368
  19.3 1.7 copy-start.16
  19.3 0.9 copy-start.23
  21.0 1.1 copy-start.9
  22.0 1.1 copy-start.11
  22.0 1.5 copy-start.15
  22.1 0.7 copy-start.5
  22.1 0.7 copy-start.7
  22.8 1.3 copy-start.13
  23.6 0.7 copy-start.29
  23.6 1.2 copy-start.45
  24.1 2.9 copy-start.3
  28.0 124.1 %all-reduce.6.cloned.1.call-start = ((), (), s32[]{:S(2)}) async-start(), calls=%async_computation.12 | async-start | bytes 3145728 | tf_op jit(solution)/shard_map/psum | solution.py:135
  28.1 1.9 copy-start.22
  29.3 0.7 copy-start.17
  30.3 1.5 copy-start.44
  30.3 1.5 copy-start.43
  30.3 1.5 copy-start.42
  30.3 1.5 copy-start.41
  30.3 1.5 copy-start.4
  30.3 1.5 copy-start.20
  30.3 1.5 copy-start.25
  30.3 1.5 copy-start.28
  30.4 1.5 copy-start.30
  30.4 1.5 copy-start.32
  33.2 0.9 copy-start.18
  33.2 0.9 copy-start.34
  33.3 2.2 copy-start.14
  33.3 2.2 copy-start.36
  33.3 177.4 %reduce-scatter.20.cloned.1.call-start = ((), (), s32[]{:S(2)}) async-start(), calls=%async_computation.9 | async-start | bytes 884736
  35.4 245.9 %reduce-scatter.14.cloned.1.call-start = ((), (), s32[]{:S(2)}) async-start(), calls=%async_computation.6 | async-start | bytes 2211840 | tf_op jit(solution)/shard_map/reduce_scatter | solution.py:207
  37.5 316.3 %reduce-scatter.18.cloned.1.call-start = ((), (), s32[]{:S(2)}) async-start(), calls=%async_computation.8 | async-start | bytes 2654208 | tf_op jit(solution)/shard_map/reduce_scatter | solution.py:212
  39.6 1.0 copy-start.12
  39.6 1.0 copy-start.37
  39.6 387.4 %reduce-scatter.16.cloned.1.call-start = ((), (), s32[]{:S(2)}) async-start(), calls=%async_computation.7 | async-start | bytes 2654208 | tf_op jit(solution)/shard_map/reduce_scatter | solution.py:211
  42.6 0.7 copy-start.46
  42.6 2.5 copy-start.6
  42.6 2.5 copy-start.8
  42.6 2.6 copy-start.10
  42.6 2.8 copy-start.38
  42.7 2.8 copy-start.39
  152.2 23.1 %copy-start.19 = (f32[256,768]{1,0:T(8,128)S(1)}, f32[256,768]{1,0:T(8,128)}, u32[]{:S(2)}) copy-start(f32[256,768]{1,0:T(8,128)} %get-tuple-element.64) | copy-start | bytes 2359300
Sparse Core Ops, SparseCore 0:
  15.7 64.8 reduce-scatter.21
  83.9 61.1 reduce-scatter.23
  148.4 62.2 reduce-scatter.19
  214.6 66.6 reduce-scatter.13
  285.3 68.4 reduce-scatter.17
  357.7 69.2 reduce-scatter.15
Sparse Core Ops, SparseCore 1:
  33.4 45.4 all-reduce.5
where the time goes:
time: 435 us; the launch traced here: 434 us
  waiting for transfers between devices  348 us (80%)
  blocking collectives  25.9 us (6%)
  matrix products  19.8 us (5%)
  between operations  17.6 us (4%)
  local copies, waits for them, and re-layouts  13.9 us (3%)
  other arithmetic  9.44 us (2%)
    unnamed x10, waiting for transfers between devices  133 us
    reduce_scatter x1, waiting for transfers between devices, body(): lax.psum_scatter(expand_grad, 'dp', scatter_dimension=0, tiled=True)  73.2 us
    reduce_scatter x1, waiting for transfers between devices, body(): lax.psum_scatter(contract_grad, 'dp', scatter_dimension=1, tiled=True)  72.5 us
    reduce_scatter x1, waiting for transfers between devices, body(): lax.psum_scatter(inlet_grad, 'dp', scatter_dimension=0, tiled=True)  69 us
    unnamed x1, blocking collectives  19.7 us
    unnamed x102, local copies, waits for them, and re-layouts  13.4 us
  transfers between devices with their start and end apart: 7, of which 6 were waited for; matrix products, arithmetic and copies ran while one was open for 7% of the time, Pallas kernels for 0%

commit v1 on v0

v1 whole, which is shorter than its diff:
```python
import functools
import math

import jax
import jax.numpy as jnp
from jax import lax
from jax.experimental import pallas as pl
from jax.experimental.pallas import tpu as pltpu
from jax.sharding import PartitionSpec as P

ROT = 16
EPS = 1e-05
F32 = jnp.float32
BF16 = jnp.bfloat16
VMEM_LIMIT = 40 * 1024 * 1024


def dot(a, b):
    return jnp.dot(a, b, preferred_element_type=F32)


def dot_t(a, b):
    return lax.dot_general(a, b, (((1,), (1,)), ((), ())), preferred_element_type=F32)


def dot_rows(a, b):
    return lax.dot_general(a, b, (((0,), (0,)), ((), ())), preferred_element_type=F32)


def norm_parts(tok):
    x = tok.astype(F32)
    center = x - jnp.mean(x, axis=-1, keepdims=True)
    inverse = lax.rsqrt(jnp.mean(center * center, axis=-1, keepdims=True) + EPS)
    return center * inverse, inverse


def label_tables(seg_row):
    n = seg_row.shape[1]
    across = jnp.broadcast_to(seg_row, (n, n))
    down = across.T
    row = lax.broadcasted_iota(jnp.int32, (n, n), 0)
    col = lax.broadcasted_iota(jnp.int32, (n, n), 1)
    same = across == down
    allowed = same & (col <= row)
    position = jnp.sum(jnp.where(same & (row <= col), 1.0, 0.0), axis=0, keepdims=True) - 1.0
    live = jnp.where(down[:, :1] >= 0.0, 1.0, 0.0)
    return allowed, live, position


def rope_tables(position, heads, size, width):
    half = ROT // 2
    index = lax.broadcasted_iota(jnp.int32, (half, 1), 0).astype(F32)
    angle = jnp.exp(index * (-2.0 * math.log(10000.0) / ROT)) * position
    cosine = jnp.concatenate([jnp.cos(angle)] * (128 // half), axis=0).T
    sine = jnp.concatenate([jnp.sin(angle)] * (128 // half), axis=0).T
    lane = lax.broadcasted_iota(jnp.int32, (1, width), 1)
    part, dim = lane // size, lane % size
    value = part >= 3 * heads
    for head in range(heads):
        value = value | (part == 3 * head + 2)
    turned = jnp.logical_not(value) & (dim < ROT)
    low = turned & (dim < half)
    high = turned & (dim >= half)
    blocks = width // 128
    cosine = jnp.concatenate([cosine] * blocks, axis=1)
    sine = jnp.concatenate([sine] * blocks, axis=1)
    return (
        jnp.where(turned, cosine, 1.0),
        jnp.where(low, sine, 0.0),
        jnp.where(high, sine, 0.0),
    )


def turn(field, tables, sign):
    cosine, low, high = tables
    width = field.shape[1]
    ahead = pltpu.roll(field, width - ROT // 2, 1)
    behind = pltpu.roll(field, ROT // 2, 1)
    return field * cosine + sign * (behind * high - ahead * low)


def gelu_pair(expanded):
    cumulative = 0.5 * (1.0 + lax.erf(expanded * (1.0 / math.sqrt(2.0))))
    density = jnp.exp(-0.5 * expanded * expanded) * (1.0 / math.sqrt(2.0 * math.pi))
    return expanded * cumulative, cumulative + expanded * density


def ffn_block(normed_two, grad_out, expand, thresholds, contract):
    expanded = dot(normed_two, expand) + thresholds
    active, slope = gelu_pair(expanded)
    grad = dot_t(grad_out, contract) * slope
    return active.astype(BF16), grad


def attention_block(normed_one, grad_out, allowed, position, inlet_t, offsets, outlet, heads, size):
    n = normed_one.shape[0]
    columns = inlet_t.shape[0]
    width = -(-columns // 128) * 128
    tables = rope_tables(position, heads, size, width)
    projected = dot_t(normed_one, inlet_t) + offsets
    if width > columns:
        projected = jnp.concatenate([projected, jnp.zeros((n, width - columns), F32)], axis=1)
    turned = turn(projected, tables, 1.0).astype(BF16)
    attended_grad = dot_t(grad_out, outlet).astype(BF16)
    attended, grads = [], []
    for head in range(heads):
        at = 3 * head * size
        query = turned[:, at : at + size]
        key = turned[:, at + size : at + 2 * size]
        value = turned[:, at + 2 * size : at + 3 * size]
        back = attended_grad[:, head * size : (head + 1) * size]
        scores = jnp.where(allowed, dot_t(query, key) * 0.125, -jnp.inf)
        raised = jnp.exp(scores - jnp.max(scores, axis=-1, keepdims=True))
        weight = raised / jnp.sum(raised, axis=-1, keepdims=True)
        softmax = weight.astype(BF16)
        attended.append(dot(softmax, value).astype(BF16))
        prob_grad = dot_t(back, value)
        delta = jnp.sum(weight * prob_grad, axis=-1, keepdims=True)
        score_grad = (weight * (prob_grad - delta)).astype(BF16)
        grads.append(dot(score_grad, key) * 0.125)
        grads.append(dot_rows(score_grad, query) * 0.125)
        grads.append(dot_rows(softmax, back))
    if width > columns:
        grads.append(jnp.zeros((n, width - columns), F32))
    inlet_full = turn(jnp.concatenate(grads, axis=1), tables, -1.0)
    return jnp.concatenate(attended, axis=1), inlet_full


def own_kernel(
    heads, size,
    tok_ref, cot_ref, seg_ref, norm_ref, inlet_ref, offsets_ref, outlet_ref, expand_ref, thr_ref, contract_ref,
    sums_ref, active_ref, back_ref, attended_ref, inlet_back_ref, small_ref,
):
    allowed, live, position = label_tables(seg_ref[...])
    scaled, inverse = norm_parts(tok_ref[...])
    gain_one, shift_one = norm_ref[0:1], norm_ref[1:2]
    gain_two, shift_two = norm_ref[2:3], norm_ref[3:4]
    normed_one = (scaled * gain_one + shift_one).astype(BF16)
    normed_two = (scaled * gain_two + shift_two).astype(BF16)
    grad_full = cot_ref[...].astype(F32) * live
    grad_out = grad_full.astype(BF16)
    active, expanded_grad = ffn_block(
        normed_two, grad_out, expand_ref[...], thr_ref[...], contract_ref[...]
    )
    expanded_back = expanded_grad.astype(BF16)
    attended, inlet_full = attention_block(
        normed_one, grad_out, allowed, position, inlet_ref[...], offsets_ref[...], outlet_ref[...], heads, size
    )
    columns = inlet_ref.shape[0]
    inlet_back = inlet_full.astype(BF16)[:, :columns]
    active_ref[...] = active
    back_ref[...] = expanded_back
    attended_ref[...] = attended
    inlet_back_ref[...] = inlet_back
    branch = dot(attended, outlet_ref[...]) + dot(active, contract_ref[...])
    one_grad = dot(inlet_back, inlet_ref[...])
    two_grad = dot_t(expanded_back, expand_ref[...])
    lifted = one_grad * gain_one + two_grad * gain_two
    local = inverse * (
        lifted
        - jnp.mean(lifted, axis=-1, keepdims=True)
        - scaled * jnp.mean(lifted * scaled, axis=-1, keepdims=True)
    )
    sums_ref[0] = branch.astype(BF16)
    sums_ref[1] = local.astype(BF16)
    small_ref[...] = jnp.zeros_like(small_ref)
    small_ref[0:1] = jnp.sum(one_grad * scaled, axis=0, keepdims=True)
    small_ref[1:2] = jnp.sum(one_grad, axis=0, keepdims=True)
    small_ref[2:3] = jnp.sum(two_grad * scaled, axis=0, keepdims=True)
    small_ref[3:4] = jnp.sum(two_grad, axis=0, keepdims=True)
    small_ref[4:5] = jnp.sum(grad_full, axis=0, keepdims=True)
    small_ref[5:6, : thr_ref.shape[1]] = jnp.sum(expanded_grad, axis=0, keepdims=True)
    small_ref[6:7, :columns] = jnp.sum(inlet_full, axis=0, keepdims=True)[:, :columns]


def slabs(source, who_ref, send, dests, block):
    if dests == 1:
        return source[...]
    first = who_ref[1]
    first = 1 - first if send else first
    rows = []
    for rest in range(dests // 4):
        start = (4 * rest + 2 * who_ref[0] + first) * block
        rows.append(source[pl.ds(pl.multiple_of(start, 8), block), :])
    return jnp.concatenate(rows, axis=0) if len(rows) > 1 else rows[0]


def partner_inputs(who_ref, got_ref, swap_ref, n):
    core = who_ref[2]
    got, swap = got_ref[0:n], swap_ref[0:n]
    tok = jnp.where(core == 0, got, swap)
    cot = jnp.where(core == 0, swap, got)
    return tok, cot, got_ref[n : n + 1, :n].astype(F32)


def ffn_kernel(
    dests,
    who_ref, got_ref, swap_ref, tok_ref, cot_ref, seg_ref, norm_ref, expand_ref, thr_ref, contract_ref, active_ref, back_ref,
    send_ref, keep_ref,
    left_ref,
):
    n = tok_ref.shape[0]
    tok, cot, seg = partner_inputs(who_ref, got_ref, swap_ref, n)
    live = jnp.where(jnp.broadcast_to(seg, (128, n)).T[:, :1] >= 0.0, 1.0, 0.0)
    live_own = jnp.where(jnp.broadcast_to(seg_ref[...], (128, n)).T[:, :1] >= 0.0, 1.0, 0.0)
    gain, shift = norm_ref[2:3], norm_ref[3:4]
    scaled, _ = norm_parts(tok)
    normed = (scaled * gain + shift).astype(BF16)
    scaled, _ = norm_parts(tok_ref[...])
    normed_own = (scaled * gain + shift).astype(BF16)
    grad_out = (cot.astype(F32) * live).astype(BF16)
    grad_own = (cot_ref[...].astype(F32) * live_own).astype(BF16)
    active, grad = ffn_block(normed, grad_out, expand_ref[...], thr_ref[...], contract_ref[...])
    right = (
        jnp.concatenate([back_ref[...], grad.astype(BF16)], axis=0),
        jnp.concatenate([active_ref[...], active], axis=0),
    )
    left = (
        jnp.concatenate([normed_own, normed], axis=0),
        jnp.concatenate([grad_own, grad_out], axis=0),
    )
    block = left_ref.shape[0] // dests
    half = dests // 4 * block
    for which in range(2):
        left_ref[...] = left[which].T
        rows = jnp.concatenate(
            [slabs(left_ref, who_ref, True, dests, block), slabs(left_ref, who_ref, False, dests, block)], axis=0
        )
        product = dot(rows, right[which])
        send_ref[which] = product[:half].astype(BF16)
        keep_ref[which] = product[half:]


def attention_kernel(
    heads, size, dests,
    who_ref, got_ref, swap_ref, tok_ref, cot_ref, seg_ref, norm_ref, inlet_ref, offsets_ref, outlet_ref, attended_ref, inlet_back_ref,
    send_ref, keep_ref,
    left_ref,
):
    n = tok_ref.shape[0]
    tok, cot, seg = partner_inputs(who_ref, got_ref, swap_ref, n)
    allowed, live, position = label_tables(seg)
    live_own = jnp.where(jnp.broadcast_to(seg_ref[...], (128, n)).T[:, :1] >= 0.0, 1.0, 0.0)
    gain, shift = norm_ref[0:1], norm_ref[1:2]
    scaled, _ = norm_parts(tok)
    normed = (scaled * gain + shift).astype(BF16)
    scaled, _ = norm_parts(tok_ref[...])
    normed_own = (scaled * gain + shift).astype(BF16)
    grad_out = (cot.astype(F32) * live).astype(BF16)
    grad_own = (cot_ref[...].astype(F32) * live_own).astype(BF16)
    attended, inlet_full = attention_block(
        normed, grad_out, allowed, position, inlet_ref[...], offsets_ref[...], outlet_ref[...], heads, size
    )
    columns = inlet_ref.shape[0]
    inlet_back = inlet_full.astype(BF16)[:, :columns]
    block = left_ref.shape[0] // dests
    half = dests // 4 * block
    products = []
    for left, right in (
        ((normed_own, normed), (inlet_back_ref[...], inlet_back)),
        ((grad_own, grad_out), (attended_ref[...], attended)),
    ):
        left_ref[...] = jnp.concatenate(left, axis=0).T
        rows = jnp.concatenate(
            [slabs(left_ref, who_ref, True, dests, block), slabs(left_ref, who_ref, False, dests, block)], axis=0
        )
        products.append(dot(rows, jnp.concatenate(right, axis=0)))
    product = jnp.concatenate(products, axis=1)
    send_ref[...] = product[:half].astype(BF16)
    keep_ref[...] = product[half:]


def call(kernel, outs, args, scratch=(), scalars=0):
    specs = [pl.BlockSpec(memory_space=pltpu.SMEM)] * scalars
    specs += [pl.BlockSpec(memory_space=pltpu.VMEM)] * (len(args) - scalars)
    return pl.pallas_call(
        kernel,
        out_shape=[jax.ShapeDtypeStruct(shape, dtype) for shape, dtype in outs],
        in_specs=specs,
        out_specs=[pl.BlockSpec(memory_space=pltpu.VMEM)] * len(outs),
        scratch_shapes=list(scratch),
        compiler_params=pltpu.CompilerParams(vmem_limit_bytes=VMEM_LIMIT),
    )(*args)


def swap(value, axis, count, bit):
    return lax.ppermute(value, axis, [(i, i ^ bit) for i in range(count)])


def finish(keep, got, me, n_dp):
    total = keep + got.astype(F32)
    bit = 4
    while bit < n_dp:
        lead = total.shape[:-3]
        split = total.reshape(lead + (-1, 2) + total.shape[-2:])
        low, high = split[..., 0, :, :], split[..., 1, :, :]
        up = (me & bit) != 0
        away = jnp.where(up, low, high).astype(BF16)
        total = jnp.where(up, high, low) + swap(away, "dp", n_dp, bit).astype(F32)
        bit *= 2
    return jnp.squeeze(total, axis=-3)


def body(n_dp, n_tensor, tokens, segments, first_gain, first_shift, second_gain, second_shift, inlet, offsets,
         outlet, outlet_bias, expand, thresholds, contract, contract_bias, cotangent):
    n, width = tokens.shape
    heads, size = offsets.shape[0], offsets.shape[1] // 3
    units = expand.shape[1]
    columns = inlet.shape[1]
    mine = outlet.shape[0]
    block = width // n_dp
    dests = n_dp
    me = lax.axis_index("dp")
    you = lax.axis_index("tensor")
    core = you & 1
    who = jnp.stack([(me >> 1) & 1, me & 1, core, you]).astype(jnp.int32)
    seg_row = segments.astype(F32)[None, :]
    norms = jnp.stack([first_gain, first_shift, second_gain, second_shift])
    inlet_t = inlet.T
    offsets_row = offsets.reshape(1, columns)
    thr_row = thresholds[None, :]

    labels = jnp.broadcast_to(
        jnp.pad(seg_row.astype(BF16), ((0, 0), (0, width - n))), (16, width)
    )
    payload = jnp.concatenate([jnp.where(core == 0, tokens, cotangent), labels], axis=0)
    got = swap(payload, "dp", n_dp, 2)
    other = swap(got, "tensor", n_tensor, 1)

    sums, active, back, attended, inlet_back, small = call(
        functools.partial(own_kernel, heads, size),
        [((2, n, width), BF16), ((n, units), BF16), ((n, units), BF16), ((n, mine), BF16), ((n, columns), BF16), ((8, width), F32)],
        [tokens, cotangent, seg_row, norms, inlet_t, offsets_row, outlet, expand, thr_row, contract],
    )
    half = dests // 4 * block
    ffn_send, ffn_keep = call(
        functools.partial(ffn_kernel, dests),
        [((2, half, units), BF16), ((2, half, units), F32)],
        [who, got, other, tokens, cotangent, seg_row, norms, expand, thr_row, contract, active, back],
        [pltpu.VMEM((width, 2 * n), BF16)],
        1,
    )
    att_send, att_keep = call(
        functools.partial(attention_kernel, heads, size, dests),
        [((half, columns + mine), BF16), ((half, columns + mine), F32)],
        [who, got, other, tokens, cotangent, seg_row, norms, inlet_t, offsets_row, outlet, attended, inlet_back],
        [pltpu.VMEM((width, 2 * n), BF16)],
        1,
    )
    ffn_got = swap(ffn_send, "dp", n_dp, 1)
    att_got = swap(att_send, "dp", n_dp, 1)
    ffn = finish(
        ffn_keep.reshape(2, -1, block, units), ffn_got.reshape(2, -1, block, units), me, n_dp
    )
    att = finish(
        att_keep.reshape(-1, block, columns + mine), att_got.reshape(-1, block, columns + mine), me, n_dp
    )

    first = jnp.where(core == 0, sums[0], sums[1]).astype(F32)
    part = first + swap(jnp.where(core == 0, sums[1], sums[0]), "tensor", n_tensor, 1).astype(F32)
    bit = 2
    while bit < n_tensor:
        part = part.astype(BF16)
        part = part.astype(F32) + swap(part, "tensor", n_tensor, bit).astype(F32)
        bit *= 2
    live = (segments >= 0).astype(F32)[:, None]
    base = jnp.where(
        core == 0,
        tokens.astype(F32) + (outlet_bias + contract_bias),
        cotangent.astype(F32) * live,
    )
    done = (base + part).astype(BF16)
    paired = swap(done, "tensor", n_tensor, 1)
    mixed = jnp.where(core == 0, done, paired)
    input_grad = jnp.where(core == 0, paired, done)

    by_dest = small[:6].reshape(6, n_dp, block).transpose(1, 0, 2)
    third = offsets.shape[1] // n_dp
    offs = small[6, :columns].reshape(heads, n_dp, third).transpose(1, 0, 2)
    offs = jnp.pad(offs, ((0, 0), (0, 8 - heads), (0, block - third)))
    tile = jnp.concatenate([by_dest, jnp.zeros((n_dp, 2, block), F32), offs], axis=1)
    here = (jnp.arange(n_tensor) == you)[None, :, None, None]
    everywhere = (jnp.arange(16) < 4)[None, None, :, None]
    tile = jnp.where(here | everywhere, tile[:, None], 0.0)
    tile = lax.all_to_all(tile.reshape(n_dp * n_tensor, 16, block), ("dp", "tensor"), 0, 0, tiled=True)
    tile = jnp.sum(tile, axis=0)
    return (
        mixed,
        input_grad,
        att[:, :columns],
        tile[8 : 8 + heads, :third],
        att[:, columns:].T,
        ffn[0],
        tile[5:6],
        ffn[1].T,
        tile[4],
        tile[0:4],
    )


def solution(mesh):
    placed = (
        P("dp", None), P("dp"), P(), P(), P(), P(), P(None, "tensor"), P("tensor", None), P("tensor", None),
        P(), P(None, "tensor"), P("tensor"), P("tensor", None), P(), P("dp", None),
    )
    return jax.shard_map(
        functools.partial(body, mesh.shape["dp"], mesh.shape["tensor"]),
        mesh=mesh,
        in_specs=placed,
        out_specs=(
            P("dp", None), P("dp", None), P("dp", "tensor"), P("tensor", "dp"), P("tensor", "dp"),
            P("dp", "tensor"), P("tensor", "dp"), P("tensor", "dp"), P("dp"), P(None, "dp"),
        ),
        check_vma=False,
    )
```

time: 435 us -> 92 us (0.21)
  waiting for transfers between devices: 348 us -> 30.3 us
  blocking collectives: 25.9 us -> 0 us
  matrix products: 19.8 us -> 0 us
  between operations: 17.6 us -> 0.98 us
  starting transfers between devices: 0.29 us -> 16 us
  Pallas kernels: 0 us -> 14.3 us
    reduce_scatter x3 -> x0, waiting for transfers between devices: 215 us -> none  [the longest x1 73.2 us: body(): lax.psum_scatter(expand_grad, 'dp', scatter_dimension=0, tiled=True)]
    unnamed x10 -> x0, waiting for transfers between devices: 133 us -> none
    ppermute x0 -> x9, waiting for transfers between devices: none -> 28.5 us  [swap(): return lax.ppermute(value, axis, [(i, i ^ bit) for i in range(count)])]
    unnamed x1 -> x0, blocking collectives: 19.7 us -> none
    dot_general x17 -> x0, matrix products: 18.5 us -> none  [the longest x3 6.06 us: contract_rows(): lax.dot_general(left, right, (((0,), (0,)), ((), ())), preferred_element_...]
    pallas_call x0 -> x3, Pallas kernels: none -> 14.3 us  [call(): pl.pallas_call(kernel, out_shape=[jax.ShapeDtypeStruct(shape, dtype) for...]
    ppermute x0 -> x9, starting transfers between devices: none -> 10.8 us  [swap(): return lax.ppermute(value, axis, [(i, i ^ bit) for i in range(count)])]
    psum x1 -> x0, blocking collectives: 6.22 us -> none  [body(): summed_grad, norm_summed = lax.psum((local_grad, norm_terms), 'tensor')]
  transfers between devices with their start and end apart: 7 -> 10, of which waited for: 6 -> 4; matrix products, arithmetic and copies ran while one was open for 7% -> 16% of each run, Pallas kernels for 0% -> 10%
where the time goes in v1:
time: 92 us; the launch traced here: 91.2 us
  waiting for transfers between devices  30.3 us (33%)
  local copies, waits for them, and re-layouts  17.6 us (19%)
  starting transfers between devices  16 us (17%)
  Pallas kernels  14.3 us (16%)
  other arithmetic  12 us (13%)
  between operations  0.98 us (1%)
    ppermute x9, waiting for transfers between devices, swap(): return lax.ppermute(value, axis, [(i, i ^ bit) for i in range(count)])  28.5 us
    pallas_call x3, Pallas kernels, call(): pl.pallas_call(kernel, out_shape=[jax.ShapeDtypeStruct(shape, dtype) for...  14.3 us
    ppermute x9, starting transfers between devices, swap(): return lax.ppermute(value, axis, [(i, i ^ bit) for i in range(count)])  10.8 us
    unnamed x45, local copies, waits for them, and re-layouts  9.83 us
    all_to_all x1, starting transfers between devices, body(): lax.all_to_all(tile.reshape(n_dp * n_tensor, 16, block), ('dp', 'tensor')...  5.15 us
    another operation x4, local copies, waits for them, and re-layouts, body(): norms = jnp.stack([first_gain, first_shift, second_gain, second_shift])  2.76 us
    convert_element_type x1, other arithmetic, body(): done = (base + part).astype(BF16)  2.13 us
    select_n x1, other arithmetic, body(): input_grad = jnp.where(core == 0, paired, done)  2.04 us
  transfers between devices with their start and end apart: 10, of which 4 were waited for; matrix products, arithmetic and copies ran while one was open for 16% of the time, Pallas kernels for 10%

profile of v1, /device:TPU:0, one launch (start us, length us, event | category | flops | bytes accessed | tf_op | source)
XLA Modules:
  0.0 91.2 jit_solution(10688001018413723512)
XLA Ops:
  0.6 0.7 convert_convert_fusion
  1.3 0.7 stack.33
  2.0 0.7 stack.32
  2.7 0.7 stack.31
  3.4 0.7 stack.30
  4.1 0.8 reshape.235.offsets_ref
  4.9 0.7 broadcast_in_dim.48.thr_ref
  5.6 0.0 copy-start
  5.6 1.0 %copy-done = bf16[256,768]{1,0:T(8,128)(2,1)S(1)} copy-done((bf16[256,768]{1,0:T(8,128)(2,1)S(1)}, bf16[256,768]{1,0:T(8,128)(2,1)}, u32[]{:S(2)}) %copy-start) | copy-done | bytes 393240
  6.6 1.0 %copy-done.2 = bf16[256,768]{1,0:T(8,128)(2,1)S(1)} copy-done((bf16[256,768]{1,0:T(8,128)(2,1)S(1)}, bf16[256,768]{1,0:T(8,128)(2,1)}, u32[]{:S(2)}) %copy-start.2) | copy-done | bytes 393240
  7.6 1.3 %copy-done.4 = bf16[768,768]{1,0:T(8,128)(2,1)S(1)} copy-done((bf16[768,768]{1,0:T(8,128)(2,1)S(1)}, bf16[768,768]{1,0:T(8,128)(2,1)}, u32[]{:S(2)}) %copy-start.4) | copy-done | bytes 1179672
  8.8 1.3 %copy-done.6 = bf16[768,768]{1,0:T(8,128)(2,1)S(1)} copy-done((bf16[768,768]{1,0:T(8,128)(2,1)S(1)}, bf16[768,768]{1,0:T(8,128)(2,1)}, u32[]{:S(2)}) %copy-start.6) | copy-done | bytes 1179672
  10.1 1.2 %copy-done.8 = bf16[768,576]{0,1:T(8,128)(2,1)S(1)} copy-done((bf16[768,576]{0,1:T(8,128)(2,1)S(1)}, bf16[768,576]{0,1:T(8,128)(2,1)}, u32[]{:S(2)}) %copy-start.8) | copy-done | bytes 884760
  11.3 1.0 %copy-done.10 = bf16[192,768]{1,0:T(8,128)(2,1)S(1)} copy-done((bf16[192,768]{1,0:T(8,128)(2,1)S(1)}, bf16[192,768]{1,0:T(8,128)(2,1)}, u32[]{:S(2)}) %copy-start.10) | copy-done | bytes 294936
  12.2 5.5 %shard_map.222 = (bf16[2,256,768]{2,1,0:T(8,128)(2,1)S(1)}, bf16[256,768]{1,0:T(8,128)(2,1)S(1)}, bf16[256,768]{1,0:T(8,128)(2,1)S(1)}, bf16[256,192]{1,0:T(8,12...) custom-call(bf16[256,768]{1,0:T(8,128)(2,1)S(1)} %copy-done, bf16[256,768]{1,0:T(8,128)(2,1)S(1)} %copy-done.2, ...), custom_call_target="tpu_custom_call" | custom-call | tf_op jit(solution)/shard_map/pallas_call | solution.py:276
  17.7 0.0 copy-start.12
  17.8 0.9 select_bitcast_fusion
  18.6 0.5 collective-permute-start
  19.2 0.0 copy-start.18
  19.2 0.0 copy-start.19
  19.3 0.8 pad_maximum_fusion
  20.1 2.7 %collective-permute-start.3 = (bf16[272,768]{1,0:T(8,128)(2,1)}, bf16[272,768]{1,0:T(8,128)(2,1)S(1)}, u32[]{:S(2)}, u32[]{:S(2)}) collective-permute-start(bf16[272,768]{1,0:T(8,128)(2,1)} %pad_maximum_fusion), channel_id=1, source_target_pairs={{0,8},{4,12},{8,0},{12,4},{16,24},{20,28},{24,16},{28,20},{1,9},{5... | collective-permute-start | bytes 1253384 | tf_op jit(solution)/shard_map/ppermute | solution.py:287
  22.8 0.1 reshape_squeeze.3
  22.8 0.1 reshape.236
  22.9 0.1 pad.11.clone
  23.0 0.1 select_maximum_fusion
  23.1 0.1 broadcast_or_fusion
  23.2 0.8 bitcast_select_fusion
  24.1 5.1 %all-to-all-start = ((f32[32,16,96]{2,1,0:T(8,128)}), f32[32,16,96]{2,1,0:T(8,128)}, u32[]{:S(2)}, u32[]{:S(2)}) async-start(f32[32,16,96]{2,1,0:T(8,128)} %bitcast_select_fusion), calls=%async_computation | async-start | bytes 524288 | tf_op jit(solution)/shard_map/all_to_all | solution.py:385
  29.3 0.1 pad_add_fusion.who_ref
  29.3 4.7 %collective-permute-done.3.got_ref = bf16[272,768]{1,0:T(8,128)(2,1)S(1)} collective-permute-done((bf16[272,768]{1,0:T(8,128)(2,1)}, bf16[272,768]{1,0:T(8,128)(2,1)S(1)}, u32[]{:S(2)}, u32[]{:S(2)}) %collective-permute-start.3) | collective-permute-done | bytes 417824 | tf_op jit(solution)/shard_map/ppermute | solution.py:287
  34.0 1.9 %fusion = bf16[256,768]{1,0:T(8,128)(2,1)} fusion(bf16[256,768]{1,0:T(8,128)(2,1)} %collective-permute-done, pred[]{:T(512)S(6)} %eq.18, bf16[2,256,768]{2,1,0:T(8,128)(2,1)S(1)} %get-tuple-element.20), kind=kLoop, calls=%fused_computation.2 | loop fusion | flops 983040 | bytes 1572865 | tf_op jit(solution)/shard_map/convert_element_type | solution.py:363
  35.9 2.6 %collective-permute-start.1 = (bf16[256,768]{1,0:T(8,128)(2,1)}, bf16[256,768]{1,0:T(8,128)(2,1)}, u32[]{:S(2)}, u32[]{:S(2)}) collective-permute-start(bf16[256,768]{1,0:T(8,128)(2,1)} %fusion), channel_id=1, source_target_pairs={{0,2},{1,3},{2,0},{3,1},{4,6},{5,7},{6,4},{7,5},{8,10},{9,11},{10,... | collective-permute-start | bytes 1179656 | tf_op jit(solution)/shard_map/ppermute | solution.py:287
  38.5 1.9 %all-to-all-done = f32[32,16,96]{2,1,0:T(8,128)} async-done(((f32[32,16,96]{2,1,0:T(8,128)}), f32[32,16,96]{2,1,0:T(8,128)}, u32[]{:S(2)}, u32[]{:S(2)}) %all-to-all-start) | async-done | bytes 196640 | tf_op jit(solution)/shard_map/all_to_all | solution.py:385
  40.4 1.0 %reduce_sum.9 = f32[16,96]{1,0:T(8,128)S(1)} reduce(f32[32,16,96]{2,1,0:T(8,128)} %all-to-all-done, f32[]{:T(128)} %constant.22.clone.1), dimensions={0}, to_apply=%region_0.1 | reduce | flops 47616 | bytes 202756 | tf_op jit(solution)/shard_map/reduce_sum | solution.py:386
  41.4 0.0 copy-start.11
  41.4 1.0 %copy-done.11 = bf16[192,768]{1,0:T(8,128)(2,1)S(1)} copy-done((bf16[192,768]{1,0:T(8,128)(2,1)S(1)}, bf16[192,768]{1,0:T(8,128)(2,1)}, u32[]{:S(2)}) %copy-start.11) | copy-done | bytes 294936
  42.4 1.0 %copy-done.17 = bf16[256,576]{1,0:T(8,128)(2,1)S(1)} copy-done((bf16[256,576]{1,0:T(8,128)(2,1)S(1)}, bf16[256,576]{1,0:T(8,128)(2,1)}, u32[]{:S(2)}) %copy-start.17) | copy-done | bytes 294936
  43.3 5.3 %shard_map.223 = (bf16[192,768]{1,0:T(8,128)(2,1)S(1)}, f32[192,768]{1,0:T(8,128)S(1)}) custom-call(s32[4]{0:T(128)S(1)} %pad_add_fusion.who_ref, bf16[272,768]{1,0:T(8,128)(2,1)S(1)} %collective-permute-done.3.got_ref, bf16[272,768]{1,0:T(8,128)(2,1)S(1)} %collective-permute-done.4.swap_ref, bf16[256,768]{1,0:T(8,128)(2,1)S(1)} %copy-done.1, ...), custom_call_target="tpu_custom_call" | custom-call | tf_op jit(solution)/shard_map/pallas_call | solution.py:276
  48.6 0.0 copy-start.5
  48.7 0.0 copy-start.13
  48.7 1.1 %collective-permute-start.5 = (bf16[192,768]{1,0:T(8,128)(2,1)S(1)}, bf16[192,768]{1,0:T(8,128)(2,1)S(1)}, u32[]{:S(2)}, u32[]{:S(2)}) collective-permute-start(bf16[192,768]{1,0:T(8,128)(2,1)S(1)} %get-tuple-element.24), channel_id=1, source_target_pairs={{0,4},{4,0},{8,12},{12,8},{16,20},{20,16},{24,28},{28,24},{1,5},{5... | collective-permute-start | bytes 884744 | tf_op jit(solution)/shard_map/ppermute | solution.py:287
  49.8 0.5 slice_bitcast_fusion.5
  50.3 0.6 slice.71
  50.9 0.6 slice.79
  51.5 2.1 %add_convert_fusion = bf16[256,768]{1,0:T(8,128)(2,1)} fusion(bf16[256,768]{1,0:T(8,128)(2,1)} %collective-permute-done.1, bf16[256,768]{1,0:T(8,128)(2,1)} %fusion, bf16[256,768]{1,0:T(8,128)(2,1)S(1)} %copy-done.3, bf16[256,768]{1,0:T(8,128)(2,1)S(1)} %copy-done.1, f32[256]{0:T(256)S(1)} %compare_convert_fusion, f32[768]{0:T(1024)S(1)} %add.56, pred[]{:T(512)S(6)} %eq.18), kind=kLoop, calls=%fused_computation.3 | loop fusion | flops 1966080 | bytes 1970177 | tf_op jit(solution)/shard_map/convert_element_type | solution.py:372
  53.6 0.0 collective-permute-start.2
  53.6 3.5 %shard_map.224 = (bf16[2,192,768]{2,1,0:T(8,128)(2,1)}, f32[2,192,768]{2,1,0:T(8,128)S(1)}) custom-call(s32[4]{0:T(128)S(1)} %pad_add_fusion.who_ref, bf16[272,768]{1,0:T(8,128)(2,1)S(1)} %collective-permute-done.3.got_ref, bf16[272,768]{1,0:T(8,128)(2,1)S(1)} %collective-permute-done.4.swap_ref, bf16[256,768]{1,0:T(8,128)(2,1)S(1)} %copy-done.1, ...), custom_call_target="tpu_custom_call" | custom-call | tf_op jit(solution)/shard_map/pallas_call | solution.py:276
  57.1 1.7 %collective-permute-start.7 = (bf16[2,192,768]{2,1,0:T(8,128)(2,1)}, bf16[2,192,768]{2,1,0:T(8,128)(2,1)}, u32[]{:S(2)}, u32[]{:S(2)}) collective-permute-start(bf16[2,192,768]{2,1,0:T(8,128)(2,1)} %get-tuple-element.29), channel_id=1, source_target_pairs={{0,4},{4,0},{8,12},{12,8},{16,20},{20,16},{24,28},{28,24},{1,5},{5... | collective-permute-start | bytes 1769480 | tf_op jit(solution)/shard_map/ppermute | solution.py:287
  58.9 0.1 convert_add_fusion.2
  59.0 0.2 copy.40
  59.2 0.2 copy.39
  59.4 0.6 collective-permute-start.6
  60.0 2.0 %broadcast_select_fusion.1 = (bf16[256,768]{1,0:T(8,128)(2,1)}, bf16[256,768]{1,0:T(8,128)(2,1)}) fusion(bf16[256,768]{1,0:T(8,128)(2,1)} %collective-permute-done.2, bf16[256,768]{1,0:T(8,128)(2,1)} %add_convert_fusion, pred[]{:T(512)S(6)} %eq.18), kind=kLoop, calls=%fused_computation.15 | loop fusion | flops 393216 | bytes 1572865 | tf_op jit(solution)/shard_map/jit(_where)/select_n | solution.py:375
  62.1 11.1 %collective-permute-done.7 = bf16[2,192,768]{2,1,0:T(8,128)(2,1)} collective-permute-done((bf16[2,192,768]{2,1,0:T(8,128)(2,1)}, bf16[2,192,768]{2,1,0:T(8,128)(2,1)}, u32[]{:S(2)}, u32[]{:S(2)}) %collective-permute-start.7) | collective-permute-done | bytes 589856 | tf_op jit(solution)/shard_map/ppermute | solution.py:287
  73.2 1.2 %convert_add_fusion = f32[2,192,768]{2,1,0:T(8,128)S(1)} fusion(f32[2,192,768]{2,1,0:T(8,128)S(1)} %get-tuple-element.28, bf16[2,192,768]{2,1,0:T(8,128)(2,1)} %collective-permute-done.7), kind=kLoop, calls=%fused_computation | loop fusion | flops 589824 | bytes 2949120 | tf_op jit(solution)/shard_map/add | solution.py:291
  74.3 0.1 fusion.2
  74.4 1.6 %collective-permute-start.8 = (bf16[2,1,96,768]{3,2,1,0:T(8,128)(2,1)S(1)}, bf16[2,1,96,768]{3,2,1,0:T(8,128)(2,1)S(1)}, u32[]{:S(2)}, u32[]{:S(2)}) collective-permute-start(bf16[2,1,96,768]{3,2,1,0:T(8,128)(2,1)S(1)} %fusion.2), channel_id=1, source_target_pairs={{0,16},{4,20},{8,24},{12,28},{16,0},{20,4},{24,8},{28,12},{1,17},{... | collective-permute-start | bytes 884744 | tf_op jit(solution)/shard_map/ppermute | solution.py:287
  76.0 0.1 fusion.1
  76.1 0.9 copy.38
  76.9 0.6 slice_bitcast_fusion.4
  77.6 12.7 %collective-permute-done.8 = bf16[2,1,96,768]{3,2,1,0:T(8,128)(2,1)S(1)} collective-permute-done((bf16[2,1,96,768]{3,2,1,0:T(8,128)(2,1)S(1)}, bf16[2,1,96,768]{3,2,1,0:T(8,128)(2,1)S(1)}, u32[]{:S(2)}, u32[]{:S(2)}) %collective-permute-start.8) | collective-permute-done | bytes 294944 | tf_op jit(solution)/shard_map/ppermute | solution.py:287
  90.2 0.1 bitcast_add_fusion
  90.3 0.8 slice_bitcast_fusion.2
  (50 shorter events, 0.3 us)
Async XLA Ops:
  5.6 1.0 %copy-start = (bf16[256,768]{1,0:T(8,128)(2,1)S(1)}, bf16[256,768]{1,0:T(8,128)(2,1)}, u32[]{:S(2)}) copy-start(bf16[256,768]{1,0:T(8,128)(2,1)} %tok_ref.5) | copy-start | bytes 1179652
  6.6 1.0 %copy-start.2 = (bf16[256,768]{1,0:T(8,128)(2,1)S(1)}, bf16[256,768]{1,0:T(8,128)(2,1)}, u32[]{:S(2)}) copy-start(bf16[256,768]{1,0:T(8,128)(2,1)} %cot_ref.5) | copy-start | bytes 1179652
  7.6 1.3 %copy-start.4 = (bf16[768,768]{1,0:T(8,128)(2,1)S(1)}, bf16[768,768]{1,0:T(8,128)(2,1)}, u32[]{:S(2)}) copy-start(bf16[768,768]{1,0:T(8,128)(2,1)} %expand_ref.3) | copy-start | bytes 3538948
  8.8 1.3 %copy-start.6 = (bf16[768,768]{1,0:T(8,128)(2,1)S(1)}, bf16[768,768]{1,0:T(8,128)(2,1)}, u32[]{:S(2)}) copy-start(bf16[768,768]{1,0:T(8,128)(2,1)} %contract_ref.3) | copy-start | bytes 3538948
  10.1 1.2 %copy-start.8 = (bf16[768,576]{0,1:T(8,128)(2,1)S(1)}, bf16[768,576]{0,1:T(8,128)(2,1)}, u32[]{:S(2)}) copy-start(bf16[768,576]{0,1:T(8,128)(2,1)} %param.21) | copy-start | bytes 2654212
  11.3 1.0 %copy-start.10 = (bf16[192,768]{1,0:T(8,128)(2,1)S(1)}, bf16[192,768]{1,0:T(8,128)(2,1)}, u32[]{:S(2)}) copy-start(bf16[192,768]{1,0:T(8,128)(2,1)} %outlet_ref.3) | copy-start | bytes 884740
  17.7 1.5 %copy-start.12 = (bf16[256,768]{1,0:T(8,128)(2,1)}, bf16[256,768]{1,0:T(8,128)(2,1)S(1)}, u32[]{:S(2)}) copy-start(bf16[256,768]{1,0:T(8,128)(2,1)S(1)} %get-tuple-element.26.active_ref) | copy-start | bytes 1179652
  17.7 1.5 %copy-start.14 = (bf16[256,768]{1,0:T(8,128)(2,1)}, bf16[256,768]{1,0:T(8,128)(2,1)S(1)}, u32[]{:S(2)}) copy-start(bf16[256,768]{1,0:T(8,128)(2,1)S(1)} %get-tuple-element.27.back_ref) | copy-start | bytes 1179652
  17.8 1.5 %copy-start.16 = (bf16[256,576]{1,0:T(8,128)(2,1)}, bf16[256,576]{1,0:T(8,128)(2,1)S(1)}, u32[]{:S(2)}) copy-start(bf16[256,576]{1,0:T(8,128)(2,1)S(1)} %get-tuple-element.22.inlet_back_ref) | copy-start | bytes 884740
  18.6 15.4 %collective-permute-start = (bf16[256,768]{1,0:T(8,128)(2,1)}, bf16[256,768]{1,0:T(8,128)(2,1)}, u32[]{:S(2)}, u32[]{:S(2)}) collective-permute-start(bf16[256,768]{1,0:T(8,128)(2,1)} %select_bitcast_fusion), channel_id=1, source_target_pairs={{0,1},{1,0},{2,3},{3,2},{4,5},{5,4},{6,7},{7,6},{8,9},{9,8},{10,11... | collective-permute-start | bytes 1179656 | tf_op jit(solution)/shard_map/ppermute | solution.py:287
  19.2 10.0 %copy-start.18 = (f32[768]{0:T(1024)S(1)}, f32[768]{0:T(1024)}, u32[]{:S(2)}) copy-start(f32[768]{0:T(1024)} %param.24) | copy-start | bytes 9220
  19.2 10.0 %copy-start.19 = (f32[768]{0:T(1024)S(1)}, f32[768]{0:T(1024)}, u32[]{:S(2)}) copy-start(f32[768]{0:T(1024)} %param.28) | copy-start | bytes 9220
  20.1 13.9 %collective-permute-start.3 = (bf16[272,768]{1,0:T(8,128)(2,1)}, bf16[272,768]{1,0:T(8,128)(2,1)S(1)}, u32[]{:S(2)}, u32[]{:S(2)}) collective-permute-start(bf16[272,768]{1,0:T(8,128)(2,1)} %pad_maximum_fusion), channel_id=1, source_target_pairs={{0,8},{4,12},{8,0},{12,4},{16,24},{20,28},{24,16},{28,20},{1,9},{5... | collective-permute-start | bytes 1253384 | tf_op jit(solution)/shard_map/ppermute | solution.py:287
  23.2 15.3 %copy-start.20 = (s32[256]{0:T(256)S(1)}, s32[256]{0:T(256)}, u32[]{:S(2)}) copy-start(s32[256]{0:T(256)} %param.16) | copy-start | bytes 3076
  24.1 17.3 %copy-start.1 = (bf16[256,768]{1,0:T(8,128)(2,1)S(1)}, bf16[256,768]{1,0:T(8,128)(2,1)}, u32[]{:S(2)}) copy-start(bf16[256,768]{1,0:T(8,128)(2,1)} %tok_ref.5) | copy-start | bytes 1179652
  24.1 17.3 %copy-start.3 = (bf16[256,768]{1,0:T(8,128)(2,1)S(1)}, bf16[256,768]{1,0:T(8,128)(2,1)}, u32[]{:S(2)}) copy-start(bf16[256,768]{1,0:T(8,128)(2,1)} %cot_ref.5) | copy-start | bytes 1179652
  24.1 17.3 %copy-start.9 = (bf16[768,576]{0,1:T(8,128)(2,1)S(1)}, bf16[768,576]{0,1:T(8,128)(2,1)}, u32[]{:S(2)}) copy-start(bf16[768,576]{0,1:T(8,128)(2,1)} %param.21) | copy-start | bytes 2654212
  24.1 16.3 %all-to-all-start = ((f32[32,16,96]{2,1,0:T(8,128)}), f32[32,16,96]{2,1,0:T(8,128)}, u32[]{:S(2)}, u32[]{:S(2)}) async-start(f32[32,16,96]{2,1,0:T(8,128)} %bitcast_select_fusion), calls=%async_computation | async-start | bytes 524288 | tf_op jit(solution)/shard_map/all_to_all | solution.py:385
  34.0 7.3 %collective-permute-start.4 = (bf16[272,768]{1,0:T(8,128)(2,1)S(1)}, bf16[272,768]{1,0:T(8,128)(2,1)S(1)}, u32[]{:S(2)}, u32[]{:S(2)}) collective-permute-start(bf16[272,768]{1,0:T(8,128)(2,1)S(1)} %collective-permute-done.3.got_ref), channel_id=1, source_target_pairs={{0,1},{1,0},{2,3},{3,2},{4,5},{5,4},{6,7},{7,6},{8,9},{9,8},{10,11... | collective-permute-start | bytes 1253384 | tf_op jit(solution)/shard_map/ppermute | solution.py:287
  35.9 15.6 %collective-permute-start.1 = (bf16[256,768]{1,0:T(8,128)(2,1)}, bf16[256,768]{1,0:T(8,128)(2,1)}, u32[]{:S(2)}, u32[]{:S(2)}) collective-permute-start(bf16[256,768]{1,0:T(8,128)(2,1)} %fusion), channel_id=1, source_target_pairs={{0,2},{1,3},{2,0},{3,1},{4,6},{5,7},{6,4},{7,5},{8,10},{9,11},{10,... | collective-permute-start | bytes 1179656 | tf_op jit(solution)/shard_map/ppermute | solution.py:287
  41.4 1.0 %copy-start.11 = (bf16[192,768]{1,0:T(8,128)(2,1)S(1)}, bf16[192,768]{1,0:T(8,128)(2,1)}, u32[]{:S(2)}) copy-start(bf16[192,768]{1,0:T(8,128)(2,1)} %outlet_ref.3) | copy-start | bytes 884740
  42.4 1.0 %copy-start.17 = (bf16[256,576]{1,0:T(8,128)(2,1)S(1)}, bf16[256,576]{1,0:T(8,128)(2,1)}, u32[]{:S(2)}) copy-start(bf16[256,576]{1,0:T(8,128)(2,1)} %copy-done.16) | copy-start | bytes 884740
  43.3 10.3 %copy-start.7 = (bf16[768,768]{1,0:T(8,128)(2,1)S(1)}, bf16[768,768]{1,0:T(8,128)(2,1)}, u32[]{:S(2)}) copy-start(bf16[768,768]{1,0:T(8,128)(2,1)} %contract_ref.3) | copy-start | bytes 3538948
  48.6 5.0 %copy-start.5 = (bf16[768,768]{1,0:T(8,128)(2,1)S(1)}, bf16[768,768]{1,0:T(8,128)(2,1)}, u32[]{:S(2)}) copy-start(bf16[768,768]{1,0:T(8,128)(2,1)} %expand_ref.3) | copy-start | bytes 3538948
  48.7 5.0 %copy-start.13 = (bf16[256,768]{1,0:T(8,128)(2,1)S(1)}, bf16[256,768]{1,0:T(8,128)(2,1)}, u32[]{:S(2)}) copy-start(bf16[256,768]{1,0:T(8,128)(2,1)} %copy-done.12) | copy-start | bytes 1179652
  48.7 4.9 %copy-start.15 = (bf16[256,768]{1,0:T(8,128)(2,1)S(1)}, bf16[256,768]{1,0:T(8,128)(2,1)}, u32[]{:S(2)}) copy-start(bf16[256,768]{1,0:T(8,128)(2,1)} %copy-done.14) | copy-start | bytes 1179652
  48.7 10.2 %collective-permute-start.5 = (bf16[192,768]{1,0:T(8,128)(2,1)S(1)}, bf16[192,768]{1,0:T(8,128)(2,1)S(1)}, u32[]{:S(2)}, u32[]{:S(2)}) collective-permute-start(bf16[192,768]{1,0:T(8,128)(2,1)S(1)} %get-tuple-element.24), channel_id=1, source_target_pairs={{0,4},{4,0},{8,12},{12,8},{16,20},{20,16},{24,28},{28,24},{1,5},{5... | collective-permute-start | bytes 884744 | tf_op jit(solution)/shard_map/ppermute | solution.py:287
  53.6 6.4 %collective-permute-start.2 = (bf16[256,768]{1,0:T(8,128)(2,1)}, bf16[256,768]{1,0:T(8,128)(2,1)}, u32[]{:S(2)}, u32[]{:S(2)}) collective-permute-start(bf16[256,768]{1,0:T(8,128)(2,1)} %add_convert_fusion), channel_id=1, source_target_pairs={{0,1},{1,0},{2,3},{3,2},{4,5},{5,4},{6,7},{7,6},{8,9},{9,8},{10,11... | collective-permute-start | bytes 1179656 | tf_op jit(solution)/shard_map/ppermute | solution.py:287
  57.1 16.0 %collective-permute-start.7 = (bf16[2,192,768]{2,1,0:T(8,128)(2,1)}, bf16[2,192,768]{2,1,0:T(8,128)(2,1)}, u32[]{:S(2)}, u32[]{:S(2)}) collective-permute-start(bf16[2,192,768]{2,1,0:T(8,128)(2,1)} %get-tuple-element.29), channel_id=1, source_target_pairs={{0,4},{4,0},{8,12},{12,8},{16,20},{20,16},{24,28},{28,24},{1,5},{5... | collective-permute-start | bytes 1769480 | tf_op jit(solution)/shard_map/ppermute | solution.py:287
  59.4 16.6 %collective-permute-start.6 = (bf16[1,96,768]{1,2,0:T(8,128)(2,1)S(1)}, bf16[1,96,768]{1,2,0:T(8,128)(2,1)S(1)}, u32[]{:S(2)}, u32[]{:S(2)}) collective-permute-start(bf16[1,96,768]{1,2,0:T(8,128)(2,1)S(1)} %fusion.3), channel_id=1, source_target_pairs={{0,16},{4,20},{8,24},{12,28},{16,0},{20,4},{24,8},{28,12},{1,17},{... | collective-permute-start | bytes 442376 | tf_op jit(solution)/shard_map/ppermute | solution.py:287
  74.4 15.8 %collective-permute-start.8 = (bf16[2,1,96,768]{3,2,1,0:T(8,128)(2,1)S(1)}, bf16[2,1,96,768]{3,2,1,0:T(8,128)(2,1)S(1)}, u32[]{:S(2)}, u32[]{:S(2)}) collective-permute-start(bf16[2,1,96,768]{3,2,1,0:T(8,128)(2,1)S(1)} %fusion.2), channel_id=1, source_target_pairs={{0,16},{4,20},{8,24},{12,28},{16,0},{20,4},{24,8},{28,12},{1,17},{... | collective-permute-start | bytes 884744 | tf_op jit(solution)/shard_map/ppermute | solution.py:287

commit v2 on v1

v2 whole, which is shorter than its diff:
```python
import functools
import math

import jax
import jax.numpy as jnp
from jax import lax
from jax.experimental import pallas as pl
from jax.experimental.pallas import tpu as pltpu
from jax.sharding import PartitionSpec as P


ROT = 16
EPS = 1e-05
F32 = jnp.float32
BF16 = jnp.bfloat16
MIB = 1024 * 1024
VMEM_LIMIT = 32 * MIB


def dot(a, b):
    return jnp.dot(a, b, preferred_element_type=F32)


def dot_t(a, b):
    return lax.dot_general(a, b, (((1,), (1,)), ((), ())), preferred_element_type=F32)


def dot_rows(a, b):
    return lax.dot_general(a, b, (((0,), (0,)), ((), ())), preferred_element_type=F32)


def norm_parts(tok):
    x = tok.astype(F32)
    center = x - jnp.mean(x, axis=-1, keepdims=True)
    inverse = lax.rsqrt(jnp.mean(center * center, axis=-1, keepdims=True) + EPS)
    return center * inverse, inverse


def label_tables(seg_row):
    n = seg_row.shape[1]
    across = jnp.broadcast_to(seg_row, (n, n))
    down = across.T
    row = lax.broadcasted_iota(jnp.int32, (n, n), 0)
    col = lax.broadcasted_iota(jnp.int32, (n, n), 1)
    same = across == down
    allowed = same & (col <= row)
    position = jnp.sum(jnp.where(same & (row <= col), 1.0, 0.0), axis=0, keepdims=True) - 1.0
    live = jnp.where(down[:, :1] >= 0.0, 1.0, 0.0)
    return allowed, live, position


def rope_tables(position, heads, size, width):
    half = ROT // 2
    index = lax.broadcasted_iota(jnp.int32, (half, 1), 0).astype(F32)
    angle = jnp.exp(index * (-2.0 * math.log(10000.0) / ROT)) * position
    cosine = jnp.concatenate([jnp.cos(angle)] * (128 // half), axis=0).T
    sine = jnp.concatenate([jnp.sin(angle)] * (128 // half), axis=0).T
    lane = lax.broadcasted_iota(jnp.int32, (1, width), 1)
    part, dim = lane // size, lane % size
    value = part >= 3 * heads
    for head in range(heads):
        value = value | (part == 3 * head + 2)
    turned = jnp.logical_not(value) & (dim < ROT)
    low = turned & (dim < half)
    high = turned & (dim >= half)
    blocks = width // 128
    cosine = jnp.concatenate([cosine] * blocks, axis=1)
    sine = jnp.concatenate([sine] * blocks, axis=1)
    return (
        jnp.where(turned, cosine, 1.0),
        jnp.where(low, sine, 0.0),
        jnp.where(high, sine, 0.0),
    )


def turn(field, tables, sign):
    cosine, low, high = tables
    width = field.shape[1]
    ahead = pltpu.roll(field, width - ROT // 2, 1)
    behind = pltpu.roll(field, ROT // 2, 1)
    return field * cosine + sign * (behind * high - ahead * low)


def gelu_pair(expanded):
    cumulative = 0.5 * (1.0 + lax.erf(expanded * (1.0 / math.sqrt(2.0))))
    density = jnp.exp(-0.5 * expanded * expanded) * (1.0 / math.sqrt(2.0 * math.pi))
    return expanded * cumulative, cumulative + expanded * density


def ffn_block(normed_two, grad_out, expand, thresholds, contract):
    expanded = dot(normed_two, expand) + thresholds
    active, slope = gelu_pair(expanded)
    grad = dot_t(grad_out, contract) * slope
    return active.astype(BF16), grad


def attention_block(normed_one, grad_out, allowed, position, inlet_t, offsets, outlet, heads, size):
    n = normed_one.shape[0]
    columns = inlet_t.shape[0]
    width = -(-columns // 128) * 128
    tables = rope_tables(position, heads, size, width)
    projected = dot_t(normed_one, inlet_t) + offsets
    if width > columns:
        projected = jnp.concatenate([projected, jnp.zeros((n, width - columns), F32)], axis=1)
    turned = turn(projected, tables, 1.0).astype(BF16)
    attended_grad = dot_t(grad_out, outlet).astype(BF16)
    attended, grads = [], []
    for head in range(heads):
        at = 3 * head * size
        query = turned[:, at : at + size]
        key = turned[:, at + size : at + 2 * size]
        value = turned[:, at + 2 * size : at + 3 * size]
        back = attended_grad[:, head * size : (head + 1) * size]
        scores = jnp.where(allowed, dot_t(query, key) * 0.125, -jnp.inf)
        raised = jnp.exp(scores - jnp.max(scores, axis=-1, keepdims=True))
        weight = raised / jnp.sum(raised, axis=-1, keepdims=True)
        softmax = weight.astype(BF16)
        attended.append(dot(softmax, value).astype(BF16))
        prob_grad = dot_t(back, value)
        delta = jnp.sum(weight * prob_grad, axis=-1, keepdims=True)
        score_grad = (weight * (prob_grad - delta)).astype(BF16)
        grads.append(dot(score_grad, key) * 0.125)
        grads.append(dot_rows(score_grad, query) * 0.125)
        grads.append(dot_rows(softmax, back))
    if width > columns:
        grads.append(jnp.zeros((n, width - columns), F32))
    inlet_full = turn(jnp.concatenate(grads, axis=1), tables, -1.0)
    return jnp.concatenate(attended, axis=1), inlet_full


def flat(ref):
    rows = [ref[i : i + 1, :] for i in range(ref.shape[0])]
    return jnp.concatenate(rows, axis=1) if len(rows) > 1 else rows[0]


def folded(value):
    size = value.shape[0]
    return value.reshape(size // 128, 128) if size % 128 == 0 else value.reshape(1, size)


def label_row(seg_ref):
    return flat(seg_ref).astype(F32)


def live_column(seg_row):
    down = jnp.broadcast_to(seg_row, (128, seg_row.shape[1])).T
    return jnp.where(down[:, :1] >= 0.0, 1.0, 0.0)


def gather_kernel(tok_ref, cot_ref, seg_ref, out_ref, sem):
    n = tok_ref.shape[0]

    @pl.when(core_bit() == 0)
    def _():
        pltpu.make_async_copy(tok_ref, out_ref.at[0:n], sem).start()

    @pl.when(core_bit() != 0)
    def _():
        pltpu.make_async_copy(cot_ref, out_ref.at[0:n], sem).start()

    width = out_ref.shape[1]
    row = label_row(seg_ref)
    row = jnp.concatenate([row, jnp.zeros((1, width - n), F32)], axis=1)
    out_ref[n : n + 16] = jnp.broadcast_to(row, (16, width)).astype(BF16)
    pltpu.make_async_copy(tok_ref, out_ref.at[0:n], sem).wait()


def own_kernel(
    heads, size, n_dp, n_tensor,
    tok_any, cot_any, seg_ref, gain_one_ref, shift_one_ref, gain_two_ref, shift_two_ref, offsets_ref, thr_ref,
    inlet_any, outlet_any, expand_any, contract_any,
    tok_ref, cot_ref, inlet_ref, outlet_ref, expand_ref, contract_ref,
    away_ref, keep_ref, active_ref, back_ref, attended_ref, inlet_back_ref, tile_ref,
    sems,
):
    copies = [
        pltpu.make_async_copy(a, b, sems.at[i])
        for i, (a, b) in enumerate(
            [(tok_any, tok_ref), (cot_any, cot_ref), (expand_any, expand_ref), (contract_any, contract_ref),
             (inlet_any, inlet_ref), (outlet_any, outlet_ref)]
        )
    ]
    for copy in copies:
        copy.start()
    seg_row = label_row(seg_ref)
    allowed, live, position = label_tables(seg_row)
    gain_one, shift_one = flat(gain_one_ref), flat(shift_one_ref)
    gain_two, shift_two = flat(gain_two_ref), flat(shift_two_ref)
    offsets = jnp.concatenate([offsets_ref[i : i + 1, :] for i in range(heads)], axis=1)
    thr = flat(thr_ref)
    copies[0].wait()
    scaled, inverse = norm_parts(tok_ref[...])
    normed_one = (scaled * gain_one + shift_one).astype(BF16)
    normed_two = (scaled * gain_two + shift_two).astype(BF16)
    copies[1].wait()
    grad_full = cot_ref[...].astype(F32) * live
    grad_out = grad_full.astype(BF16)
    copies[2].wait()
    copies[3].wait()
    active, expanded_grad = ffn_block(normed_two, grad_out, expand_ref[...], thr, contract_ref[...])
    expanded_back = expanded_grad.astype(BF16)
    copies[4].wait()
    copies[5].wait()
    attended, inlet_full = attention_block(
        normed_one, grad_out, allowed, position, inlet_ref[...], offsets, outlet_ref[...], heads, size
    )
    columns = inlet_ref.shape[0]
    inlet_back = inlet_full.astype(BF16)[:, :columns]
    active_ref[...] = active
    back_ref[...] = expanded_back
    attended_ref[...] = attended
    inlet_back_ref[...] = inlet_back
    branch = dot(attended, outlet_ref[...]) + dot(active, contract_ref[...])
    one_grad = dot(inlet_back, inlet_ref[...])
    two_grad = dot_t(expanded_back, expand_ref[...])
    lifted = one_grad * gain_one + two_grad * gain_two
    local = inverse * (
        lifted
        - jnp.mean(lifted, axis=-1, keepdims=True)
        - scaled * jnp.mean(lifted * scaled, axis=-1, keepdims=True)
    )
    core = core_bit()
    away_ref[...] = jnp.where(core == 0, local, branch).astype(BF16)
    keep_ref[...] = jnp.where(core == 0, branch, local)

    def total(field):
        return jnp.sum(field, axis=0, keepdims=True)

    everyone = jnp.concatenate(
        [total(one_grad * scaled), total(one_grad), total(two_grad * scaled), total(two_grad)], axis=0
    )
    bias = total(grad_full)
    hidden = total(expanded_grad)
    shares = total(inlet_full)
    block = tile_ref.shape[3]
    third = 3 * size // n_dp
    per_dp = hidden.shape[1] // n_dp
    tile_ref[...] = jnp.zeros_like(tile_ref)
    for d in range(n_dp):
        lanes = slice(d * block, (d + 1) * block)
        for t in range(n_tensor):
            tile_ref[d, t, 0:4] = everyone[:, lanes]

        def put(t, d=d, lanes=lanes):
            tile_ref[d, t, 4:5] = bias[:, lanes]
            tile_ref[d, t, 5:6, :per_dp] = hidden[:, d * per_dp : (d + 1) * per_dp]
            for head in range(heads):
                at = head * 3 * size + d * third
                tile_ref[d, t, 8 + head : 9 + head, :third] = shares[:, at : at + third]

        put(lax.axis_index("tensor"))


def gather_bit():
    return lax.axis_index("dp") // 2 % 2


def first_bit():
    return lax.axis_index("dp") % 2


def core_bit():
    return lax.axis_index("tensor") % 2


def spread_rows(left, left_ref, dests):
    width = left.shape[1]
    block = width // dests
    if block % 16 == 0:
        left_ref[...] = left.T
        rows = []
        for flip in (1, 0):
            first = first_bit() if flip == 0 else 1 - first_bit()
            for rest in range(dests // 4):
                start = (4 * rest + 2 * gather_bit() + first) * block
                rows.append(left_ref[pl.ds(pl.multiple_of(start, 16), block), :])
        return jnp.concatenate(rows, axis=0)
    half = dests // 4 * block
    row = lax.broadcasted_iota(jnp.int32, (2 * half, width), 0)
    col = lax.broadcasted_iota(jnp.int32, (2 * half, width), 1)
    kept = row >= half
    row = jnp.where(kept, row - half, row)
    first = jnp.where(kept, first_bit(), 1 - first_bit())
    want = row + (row // block) * 3 * block + (2 * gather_bit() + first) * block
    return dot_t(jnp.where(want == col, 1.0, 0.0).astype(BF16), left).astype(BF16)


def partner_inputs(got_ref, swap_ref, n):
    core = core_bit()
    got, swapped = got_ref[0:n], swap_ref[0:n]
    tok = jnp.where(core == 0, got, swapped)
    cot = jnp.where(core == 0, swapped, got)
    return tok, cot, got_ref[n : n + 1, :n].astype(F32)


def put_halves(product, send_ref, keep_ref):
    half = product.shape[0] // 2
    send_ref[...] = product[:half].astype(BF16)
    keep_ref[...] = product[half:]


def expand_kernel(
    dests,
    got_ref, swap_ref, tok_ref, gain_ref, shift_ref, expand_ref, thr_ref, contract_ref, back_ref,
    send_ref, keep_ref, active_ref,
    left_ref,
):
    n = tok_ref.shape[0]
    tok, cot, seg = partner_inputs(got_ref, swap_ref, n)
    gain, shift = flat(gain_ref), flat(shift_ref)
    scaled, _ = norm_parts(tok)
    normed = (scaled * gain + shift).astype(BF16)
    scaled, _ = norm_parts(tok_ref[...])
    normed_own = (scaled * gain + shift).astype(BF16)
    grad_out = (cot.astype(F32) * live_column(seg)).astype(BF16)
    active, grad = ffn_block(normed, grad_out, expand_ref[...], flat(thr_ref), contract_ref[...])
    active_ref[...] = active
    rows = spread_rows(jnp.concatenate([normed_own, normed], axis=0), left_ref, dests)
    put_halves(dot(rows, jnp.concatenate([back_ref[...], grad.astype(BF16)], axis=0)), send_ref, keep_ref)


def contract_kernel(
    dests,
    got_ref, swap_ref, cot_ref, seg_ref, own_ref, active_ref,
    send_ref, keep_ref,
    left_ref,
):
    n = cot_ref.shape[0]
    _, cot, seg = partner_inputs(got_ref, swap_ref, n)
    grad_out = (cot.astype(F32) * live_column(seg)).astype(BF16)
    grad_own = (cot_ref[...].astype(F32) * live_column(label_row(seg_ref))).astype(BF16)
    rows = spread_rows(jnp.concatenate([grad_own, grad_out], axis=0), left_ref, dests)
    put_halves(dot(rows, jnp.concatenate([own_ref[...], active_ref[...]], axis=0)), send_ref, keep_ref)


def attention_kernel(
    heads, size, dests,
    got_ref, swap_ref, tok_ref, cot_ref, seg_ref, gain_ref, shift_ref, inlet_ref, offsets_ref, outlet_ref, attended_ref, inlet_back_ref, after_ref,
    send_ref, keep_ref,
    left_ref,
):
    n = tok_ref.shape[0]
    tok, cot, seg = partner_inputs(got_ref, swap_ref, n)
    allowed, live, position = label_tables(seg)
    gain, shift = flat(gain_ref), flat(shift_ref)
    offsets = jnp.concatenate([offsets_ref[i : i + 1, :] for i in range(heads)], axis=1)
    scaled, _ = norm_parts(tok)
    normed = (scaled * gain + shift).astype(BF16)
    scaled, _ = norm_parts(tok_ref[...])
    normed_own = (scaled * gain + shift).astype(BF16)
    grad_out = (cot.astype(F32) * live).astype(BF16)
    grad_own = (cot_ref[...].astype(F32) * live_column(label_row(seg_ref))).astype(BF16)
    attended, inlet_full = attention_block(
        normed, grad_out, allowed, position, inlet_ref[...], offsets, outlet_ref[...], heads, size
    )
    columns = inlet_ref.shape[0]
    inlet_back = inlet_full.astype(BF16)[:, :columns]
    rows = spread_rows(jnp.concatenate([normed_own, normed], axis=0), left_ref, dests)
    first = dot(rows, jnp.concatenate([inlet_back_ref[...], inlet_back], axis=0))
    rows = spread_rows(jnp.concatenate([grad_own, grad_out], axis=0), left_ref, dests)
    second = dot(rows, jnp.concatenate([attended_ref[...], attended], axis=0))
    put_halves(jnp.concatenate([first, second], axis=1), send_ref, keep_ref)


def halve_kernel(step, keep_ref, got_ref, send_ref, left_ref):
    bit = jnp.where((lax.axis_index("dp") & step) != 0, 1, 0)
    for i in range(send_ref.shape[0]):
        away, stay = 2 * i + 1 - bit, 2 * i + bit
        send_ref[i] = (keep_ref[away] + got_ref[away].astype(F32)).astype(BF16)
        left_ref[i] = keep_ref[stay] + got_ref[stay].astype(F32)


def add_kernel(keep_ref, got_ref, out_ref):
    out_ref[...] = keep_ref[0] + got_ref[0].astype(F32)


def split_kernel(keep_ref, got_ref, inlet_ref, outlet_ref):
    total = keep_ref[0] + got_ref[0].astype(F32)
    columns = inlet_ref.shape[1]
    inlet_ref[...] = total[:, :columns]
    outlet_ref[...] = total[:, columns:].T


def part_kernel(keep_ref, got_ref, out_ref):
    out_ref[...] = (keep_ref[...].astype(F32) + got_ref[...].astype(F32)).astype(BF16)


def done_kernel(part_ref, got_ref, tok_ref, cot_ref, seg_ref, bias_ref, other_ref, out_ref):
    part = part_ref[...].astype(F32) + got_ref[...].astype(F32)
    shift = flat(bias_ref) + flat(other_ref)
    live = live_column(label_row(seg_ref))
    base = jnp.where(core_bit() == 0, tok_ref[...].astype(F32) + shift, cot_ref[...].astype(F32) * live)
    out_ref[...] = (base + part).astype(BF16)


def pair_kernel(own_ref, got_ref, mixed_ref, grad_ref):
    first = core_bit() == 0
    own, got = own_ref[...], got_ref[...]
    mixed_ref[...] = jnp.where(first, own, got)
    grad_ref[...] = jnp.where(first, got, own)


def small_kernel(heads, third, tile_ref, norms_ref, bias_ref, thr_ref, offsets_ref):
    total = tile_ref[0]
    for i in range(1, tile_ref.shape[0]):
        total = total + tile_ref[i]
    norms_ref[...] = total[0:4]
    bias_ref[...] = total[4:5]
    thr_ref[...] = total[5:6, : thr_ref.shape[1]]
    offsets_ref[...] = total[8 : 8 + heads, :third]


def call(kernel, outs, args, flops=0, scratch=(), limit=VMEM_LIMIT, places="", results=""):
    kinds = {"v": pl.BlockSpec(memory_space=pltpu.VMEM), "a": pl.BlockSpec(memory_space=pltpu.HBM), "d": pl.BlockSpec()}
    places = places or "v" * len(args)
    results = results or "v" * len(outs)
    moved = sum(math.prod(s) * jnp.dtype(t).itemsize for s, t in outs)
    moved += sum(math.prod(a.shape) * a.dtype.itemsize for a in args)
    args = [pltpu.with_memory_space_constraint(a, pltpu.HBM) if k == "a" else a for a, k in zip(args, places)]
    return pl.pallas_call(
        kernel,
        out_shape=[jax.ShapeDtypeStruct(shape, dtype) for shape, dtype in outs],
        in_specs=[kinds[k] for k in places],
        out_specs=[kinds[k] for k in results],
        scratch_shapes=list(scratch),
        compiler_params=pltpu.CompilerParams(vmem_limit_bytes=limit),
        cost_estimate=pl.CostEstimate(flops=int(flops), bytes_accessed=moved, transcendentals=0),
    )(*args)


def swap(value, axis, count, bit):
    return lax.ppermute(value, axis, [(i, i ^ bit) for i in range(count)])


def step(n_dp, n_tensor, tokens, segments, first_gain, first_shift, second_gain, second_shift, inlet, offsets,
         outlet, outlet_bias, expand, thresholds, contract, contract_bias, cotangent):
    n, width = tokens.shape
    heads, size = offsets.shape[0], offsets.shape[1] // 3
    units = expand.shape[1]
    columns = inlet.shape[1]
    mine = outlet.shape[0]
    block = width // n_dp
    seg = folded(segments)
    gain_one, shift_one, gain_two, shift_two = map(folded, (first_gain, first_shift, second_gain, second_shift))
    thr = folded(thresholds)

    payload, = call(
        gather_kernel, [((n + 16, width), BF16)], [tokens, cotangent, seg],
        scratch=[pltpu.SemaphoreType.DMA], places="aav",
    )
    got = swap(payload, "dp", n_dp, 2)
    other = swap(got, "tensor", n_tensor, 1)

    (tok, cot, inlet_v, outlet_v, expand_v, contract_v, away, keep, active, back, attended, inlet_back, tile) = call(
        functools.partial(own_kernel, heads, size, n_dp, n_tensor),
        [(tokens.shape, BF16), (cotangent.shape, BF16), ((columns, width), BF16), (outlet.shape, BF16), (expand.shape, BF16),
         (contract.shape, BF16), ((n, width), BF16), ((n, width), F32), ((n, units), BF16), ((n, units), BF16),
         ((n, mine), BF16), ((n, columns), BF16), ((n_dp, n_tensor, 16, block), F32)],
        [tokens, cotangent, seg, gain_one, shift_one, gain_two, shift_two, offsets, thr, inlet.T, outlet, expand, contract],
        flops=6e9, scratch=[pltpu.SemaphoreType.DMA((6,))], places="aavvvvvvvaaaa",
    )
    half = n_dp // 4 * block
    left = [pltpu.VMEM((width, 2 * n), BF16)]

    expand_send, expand_keep, active_near = call(
        functools.partial(expand_kernel, n_dp),
        [((half, units), BF16), ((half, units), F32), ((n, units), BF16)],
        [got, other, tok, gain_two, shift_two, expand_v, thr, contract_v, back],
        flops=3e9, scratch=left,
    )
    expand_got = swap(expand_send, "dp", n_dp, 1)
    contract_send, contract_keep = call(
        functools.partial(contract_kernel, n_dp),
        [((half, units), BF16), ((half, units), F32)],
        [got, other, cot, seg, active, active_near],
        flops=1e9, scratch=left,
    )
    contract_got = swap(contract_send, "dp", n_dp, 1)
    tail_send, tail_keep = call(
        functools.partial(attention_kernel, heads, size, n_dp),
        [((half, columns + mine), BF16), ((half, columns + mine), F32)],
        [got, other, tok, cot, seg, gain_one, shift_one, inlet_v, offsets, outlet_v, attended, inlet_back, contract_keep],
        flops=5e9, scratch=left,
    )
    tail_got = swap(tail_send, "dp", n_dp, 1)

    part = keep
    near = swap(away, "tensor", n_tensor, 1)
    part, = call(part_kernel, [((n, width), BF16)], [keep, near], flops=1e6)
    bit = 2
    while 2 * bit < n_tensor:
        part, = call(part_kernel, [((n, width), BF16)], [part, swap(part, "tensor", n_tensor, bit)])
        bit *= 2
    far = swap(part, "tensor", n_tensor, bit)
    done, = call(
        done_kernel, [((n, width), BF16)],
        [part, far, tok, cot, seg, folded(outlet_bias), folded(contract_bias)], flops=1e6,
    )
    paired = swap(done, "tensor", n_tensor, 1)
    mixed, input_grad = call(pair_kernel, [((n, width), BF16)] * 2, [done, paired], results="dd")

    tile = lax.all_to_all(tile.reshape(n_dp * n_tensor, 16, block), ("dp", "tensor"), 0, 0, tiled=True)
    third = offsets.shape[1] // n_dp
    norm_grads, bias_grad, thr_grad, offsets_grad = call(
        functools.partial(small_kernel, heads, third),
        [((4, block), F32), ((1, block), F32), ((1, units // n_dp), F32), ((heads, third), F32)], [tile], results="dddd",
    )

    def reduce(kept, arrived):
        columns_here = kept.shape[1]
        kept = kept.reshape(-1, block, columns_here)
        arrived = arrived.reshape(-1, block, columns_here)
        bit = 4
        while bit < n_dp:
            rest = kept.shape[0] // 2
            shape = (rest, block, columns_here)
            away, kept = call(
                functools.partial(halve_kernel, bit), [(shape, BF16), (shape, F32)], [kept, arrived],
                flops=1e6,
            )
            arrived = swap(away, "dp", n_dp, bit)
            bit *= 2
        return kept, arrived

    expand_grad, = call(add_kernel, [((block, units), F32)], reduce(expand_keep, expand_got), results="d")
    contract_grad, = call(add_kernel, [((block, units), F32)], reduce(contract_keep, contract_got), results="d")
    inlet_grad, outlet_grad = call(
        split_kernel, [((block, columns), F32), ((mine, block), F32)],
        reduce(tail_keep, tail_got), results="dd",
    )
    return (
        mixed, input_grad, inlet_grad, offsets_grad, outlet_grad, expand_grad, thr_grad, contract_grad.T,
        bias_grad.reshape(block), norm_grads,
    )


def solution(mesh):
    placed = (
        P("dp", None), P("dp"), P(), P(), P(), P(), P(None, "tensor"), P("tensor", None), P("tensor", None),
        P(), P(None, "tensor"), P("tensor"), P("tensor", None), P(), P("dp", None),
    )
    return jax.shard_map(
        functools.partial(step, mesh.shape["dp"], mesh.shape["tensor"]),
        mesh=mesh,
        in_specs=placed,
        out_specs=(
            P("dp", None), P("dp", None), P("dp", "tensor"), P("tensor", "dp"), P("tensor", "dp"),
            P("dp", "tensor"), P("tensor", "dp"), P("tensor", "dp"), P("dp"), P(None, "dp"),
        ),
        check_vma=False,
    )
```

time: 92 us -> 73.2 us (0.80)
  local copies, waits for them, and re-layouts: 17.6 us -> 0.79 us
  other arithmetic: 12 us -> 0 us
  Pallas kernels: 14.3 us -> 23.3 us
  starting transfers between devices: 16 us -> 20.9 us
  waiting for transfers between devices: 30.3 us -> 27.2 us
    unnamed x45 -> x26, local copies, waits for them, and re-layouts: 9.83 us -> 0.79 us
    pallas_call x3 -> x15, Pallas kernels: 14.3 us -> 23.3 us  [call(): pl.pallas_call(kernel, out_shape=[jax.ShapeDtypeStruct(shape, dtype) for...]
    ppermute x9 -> x11, starting transfers between devices: 10.8 us -> 16.9 us  [swap(): return lax.ppermute(value, axis, [(i, i ^ bit) for i in range(count)])]
    convert_element_type x6 -> x0, other arithmetic: 4.81 us -> none  [the longest x1 2.13 us: body(): done = (base + part).astype(BF16)]
    select_n x4 -> x0, other arithmetic: 3.81 us -> none  [the longest x1 2.04 us: body(): input_grad = jnp.where(core == 0, paired, done)]
    another operation x5 -> x0, local copies, waits for them, and re-layouts: 2.83 us -> none  [the longest x4 2.76 us: body(): norms = jnp.stack([first_gain, first_shift, second_gain, second_shift])]
    all_to_all x1, waiting for transfers between devices: 1.85 us -> 0.01 us  [step(): lax.all_to_all(tile.reshape(n_dp * n_tensor, 16, block), ('dp', 'tensor')...]
    transpose x2 -> x0, local copies, waits for them, and re-layouts: 1.5 us -> none  [the longest x1 0.85 us: body(): ffn[1]]
  transfers between devices with their start and end apart: 10 -> 12, of which waited for: 4 -> 7; matrix products, arithmetic and copies ran while one was open for 16% -> 0% of each run, Pallas kernels for 10% -> 29%
where the time goes in v2:
time: 73.2 us; the launch traced here: 73 us
  waiting for transfers between devices  27.2 us (37%)
  Pallas kernels  23.3 us (32%)
  starting transfers between devices  20.9 us (29%)
  between operations  0.82 us (1%)
  local copies, waits for them, and re-layouts  0.79 us (1%)
    ppermute x11, waiting for transfers between devices, swap(): return lax.ppermute(value, axis, [(i, i ^ bit) for i in range(count)])  27.2 us
    pallas_call x15, Pallas kernels, call(): pl.pallas_call(kernel, out_shape=[jax.ShapeDtypeStruct(shape, dtype) for...  23.3 us
    ppermute x11, starting transfers between devices, swap(): return lax.ppermute(value, axis, [(i, i ^ bit) for i in range(count)])  16.9 us
    all_to_all x1, starting transfers between devices, step(): lax.all_to_all(tile.reshape(n_dp * n_tensor, 16, block), ('dp', 'tensor')...  4.05 us
  transfers between devices with their start and end apart: 12, of which 7 were waited for; matrix products, arithmetic and copies ran while one was open for 0% of the time, Pallas kernels for 29%

profile of v2, /device:TPU:0, one launch (start us, length us, event | category | flops | bytes accessed | tf_op | source)
XLA Modules:
  0.0 73.0 jit_solution(17477609745611468250)
XLA Ops:
  0.6 0.0 copy-start.4
  0.7 0.0 copy-start.3
  0.7 0.7 %copy-done.3 = s32[256]{0:T(256)S(1)} copy-done((s32[256]{0:T(256)S(1)}, s32[256]{0:T(256)}, u32[]{:S(2)}) %copy-start.3) | copy-done | bytes 1048
  1.4 0.0 copy-start.7
  1.4 0.0 copy-start.8
  1.4 0.0 copy-start.9
  1.4 0.0 copy-start.10
  1.4 0.0 copy-start.11
  1.4 0.0 copy-start.12
  1.4 1.1 %shard_map.226 = bf16[272,768]{1,0:T(8,128)(2,1)S(1)} custom-call(bf16[256,768]{1,0:T(8,128)(2,1)} %tok_ref.1, bf16[256,768]{1,0:T(8,128)(2,1)} %cot_ref.1, s32[2,128]{1,0:T(2,128)S(1)} %bitcast.24), custom_call_target="tpu_custom_call" | custom-call | bytes 1205248 | tf_op jit(solution)/shard_map/pallas_call | solution.py:420
  2.5 3.1 %collective-permute-start.3 = (bf16[272,768]{1,0:T(8,128)(2,1)S(1)}, bf16[272,768]{1,0:T(8,128)(2,1)S(1)}, u32[]{:S(2)}, u32[]{:S(2)}) collective-permute-start(bf16[272,768]{1,0:T(8,128)(2,1)S(1)} %shard_map.226), channel_id=1, source_target_pairs={{0,8},{4,12},{8,0},{12,4},{16,24},{20,28},{24,16},{28,20},{1,9},{5... | collective-permute-start | bytes 1253384 | tf_op jit(solution)/shard_map/ppermute | solution.py:432
  5.6 9.6 %collective-permute-done.3.got_ref = bf16[272,768]{1,0:T(8,128)(2,1)S(1)} collective-permute-done((bf16[272,768]{1,0:T(8,128)(2,1)S(1)}, bf16[272,768]{1,0:T(8,128)(2,1)S(1)}, u32[]{:S(2)}, u32[]{:S(2)}) %collective-permute-start.3) | collective-permute-done | bytes 417824 | tf_op jit(solution)/shard_map/ppermute | solution.py:432
  15.3 0.0 collective-permute-start.4
  15.3 0.0 copy-done.4
  15.3 0.0 copy-done.7
  15.3 0.0 copy-done.8
  15.3 0.0 copy-done.9
  15.3 0.0 copy-done.10
  15.3 0.0 copy-done.11
  15.3 0.0 copy-done.12
  15.3 7.3 %shard_map.222 = (bf16[256,768]{1,0:T(8,128)(2,1)S(1)}, bf16[256,768]{1,0:T(8,128)(2,1)S(1)}, bf16[576,768]{1,0:T(8,128)(2,1)S(1)}, bf16[192,768]{1,0:T(8,128)(2...) custom-call(bf16[256,768]{1,0:T(8,128)(2,1)} %tok_ref.1, ...), custom_call_target="tpu_custom_call" | custom-call | flops 6000000000 | bytes 11225344 | tf_op jit(solution)/shard_map/pallas_call | solution.py:420
  22.7 0.0 copy-start.2
  22.7 0.6 collective-permute-start
  23.2 1.3 %collective-permute-done.got_ref = bf16[256,768]{1,0:T(8,128)(2,1)S(1)} collective-permute-done((bf16[256,768]{1,0:T(8,128)(2,1)S(1)}, bf16[256,768]{1,0:T(8,128)(2,1)S(1)}, u32[]{:S(2)}, u32[]{:S(2)}) %collective-permute-start) | collective-permute-done | bytes 393248 | tf_op jit(solution)/shard_map/ppermute | solution.py:432
  24.6 0.1 shard_map.223.part_ref
  24.7 1.7 %collective-permute-start.1 = (bf16[256,768]{1,0:T(8,128)(2,1)S(1)}, bf16[256,768]{1,0:T(8,128)(2,1)S(1)}, u32[]{:S(2)}, u32[]{:S(2)}) collective-permute-start(bf16[256,768]{1,0:T(8,128)(2,1)S(1)} %shard_map.223.part_ref), channel_id=1, source_target_pairs={{0,2},{1,3},{2,0},{3,1},{4,6},{5,7},{6,4},{7,5},{8,10},{9,11},{10,... | collective-permute-start | bytes 1179656 | tf_op jit(solution)/shard_map/ppermute | solution.py:432
  26.4 0.0 collective-permute-done.4.swap_ref
  26.4 2.4 %shard_map.227 = (bf16[192,768]{1,0:T(8,128)(2,1)}, f32[192,768]{1,0:T(8,128)S(1)}, bf16[256,768]{1,0:T(8,128)(2,1)S(1)}) custom-call(bf16[272,768]{1,0:T(8,128)(2,1)S(1)} %collective-permute-done.3.got_ref, bf16[272,768]{1,0:T(8,128)(2,1)S(1)} %collective-permute-done.4.swap_ref, bf16[256,768]{1,0:T(8,128)(2,1)S(1)} %get-tuple-element.46.tok_ref, ...), custom_call_target="tpu_custom_call" | custom-call | flops 3000000000 | bytes 5268480 | tf_op jit(solution)/shard_map/pallas_call | solution.py:420
  28.7 0.0 copy-done.2
  28.7 1.6 %shard_map.228 = (bf16[192,768]{1,0:T(8,128)(2,1)}, f32[192,768]{1,0:T(8,128)S(1)}) custom-call(bf16[272,768]{1,0:T(8,128)(2,1)S(1)} %collective-permute-done.3.got_ref, bf16[272,768]{1,0:T(8,128)(2,1)S(1)} %collective-permute-done.4.swap_ref, bf16[256,768]{1,0:T(8,128)(2,1)S(1)} %get-tuple-element.47.cot_ref, s32[2,128]{1,0:T(2,128)S(1)} %bitcast.26, ...), custom_call_target="tpu_custom_call" | custom-call | flops 1000000000 | bytes 2900992 | tf_op jit(solution)/shard_map/pallas_call | solution.py:420
  30.3 0.0 copy-start.5
  30.3 0.0 copy-start.6
  30.3 5.5 %shard_map.229 = (bf16[192,768]{1,0:T(8,128)(2,1)}, f32[192,768]{1,0:T(8,128)S(1)}) custom-call(bf16[272,768]{1,0:T(8,128)(2,1)S(1)} %collective-permute-done.3.got_ref, bf16[272,768]{1,0:T(8,128)(2,1)S(1)} %collective-permute-done.4.swap_ref, bf16[256,768]{1,0:T(8,128)(2,1)S(1)} %get-tuple-element.46.tok_ref, ...), custom_call_target="tpu_custom_call" | custom-call | flops 5000000000 | bytes 4678912 | tf_op jit(solution)/shard_map/pallas_call | solution.py:420
  35.9 1.5 %collective-permute-start.5 = (bf16[192,768]{1,0:T(8,128)(2,1)}, bf16[192,768]{1,0:T(8,128)(2,1)}, u32[]{:S(2)}, u32[]{:S(2)}) collective-permute-start(bf16[192,768]{1,0:T(8,128)(2,1)} %get-tuple-element.61), channel_id=1, source_target_pairs={{0,4},{4,0},{8,12},{12,8},{16,20},{20,16},{24,28},{28,24},{1,5},{5... | collective-permute-start | bytes 884744 | tf_op jit(solution)/shard_map/ppermute | solution.py:432
  37.4 0.5 collective-permute-start.9
  37.9 1.5 %collective-permute-start.7 = (bf16[192,768]{1,0:T(8,128)(2,1)}, bf16[192,768]{1,0:T(8,128)(2,1)S(1)}, u32[]{:S(2)}, u32[]{:S(2)}) collective-permute-start(bf16[192,768]{1,0:T(8,128)(2,1)} %get-tuple-element.69), channel_id=1, source_target_pairs={{0,4},{4,0},{8,12},{12,8},{16,20},{20,16},{24,28},{28,24},{1,5},{5... | collective-permute-start | bytes 884744 | tf_op jit(solution)/shard_map/ppermute | solution.py:432
  39.4 0.0 collective-permute-done.1.got_ref
  39.4 0.0 copy-done.5
  39.4 0.0 copy-done.6
  39.4 0.3 shard_map.224.own_ref
  39.8 0.1 collective-permute-start.2
  39.8 4.1 %all-to-all-start = ((f32[32,16,96]{2,1,0:T(8,128)}), f32[32,16,96]{2,1,0:T(8,128)S(1)}, u32[]{:S(2)}, u32[]{:S(2)}) async-start(f32[32,16,96]{2,1,0:T(8,128)} %bitcast.23), calls=%async_computation | async-start | bytes 524288 | tf_op jit(solution)/shard_map/all_to_all | solution.py:502
  43.9 2.1 %collective-permute-done.5 = bf16[192,768]{1,0:T(8,128)(2,1)} collective-permute-done((bf16[192,768]{1,0:T(8,128)(2,1)}, bf16[192,768]{1,0:T(8,128)(2,1)}, u32[]{:S(2)}, u32[]{:S(2)}) %collective-permute-start.5) | collective-permute-done | bytes 294944 | tf_op jit(solution)/shard_map/ppermute | solution.py:432
  46.1 1.0 %shard_map.230 = (bf16[1,96,768]{2,1,0:T(8,128)(2,1)S(1)}, f32[1,96,768]{2,1,0:T(8,128)S(1)}) custom-call(f32[2,96,768]{2,1,0:T(8,128)S(1)} %bitcast.20, bf16[2,96,768]{2,1,0:T(8,128)(2,1)} %bitcast.10.got_ref), custom_call_target="tpu_custom_call" | custom-call | flops 1000000 | bytes 1327104 | tf_op jit(solution)/shard_map/pallas_call | solution.py:420
  47.1 0.0 copy-start
  47.1 2.6 %collective-permute-start.6 = (bf16[1,96,768]{2,1,0:T(8,128)(2,1)S(1)}, bf16[1,96,768]{2,1,0:T(8,128)(2,1)S(1)}, u32[]{:S(2)}, u32[]{:S(2)}) collective-permute-start(bf16[1,96,768]{2,1,0:T(8,128)(2,1)S(1)} %get-tuple-element.63), channel_id=1, source_target_pairs={{0,16},{4,20},{8,24},{12,28},{16,0},{20,4},{24,8},{28,12},{1,17},{... | collective-permute-start | bytes 442376 | tf_op jit(solution)/shard_map/ppermute | solution.py:432
  49.7 4.7 %collective-permute-done.9 = bf16[192,768]{1,0:T(8,128)(2,1)S(1)} collective-permute-done((bf16[192,768]{1,0:T(8,128)(2,1)}, bf16[192,768]{1,0:T(8,128)(2,1)S(1)}, u32[]{:S(2)}, u32[]{:S(2)}) %collective-permute-start.9) | collective-permute-done | bytes 294944 | tf_op jit(solution)/shard_map/ppermute | solution.py:432
  54.5 2.6 %collective-permute-start.10 = (bf16[1,96,768]{2,1,0:T(8,128)(2,1)S(1)}, bf16[1,96,768]{2,1,0:T(8,128)(2,1)S(1)}, u32[]{:S(2)}, u32[]{:S(2)}) collective-permute-start(bf16[1,96,768]{2,1,0:T(8,128)(2,1)S(1)} %get-tuple-element.75), channel_id=1, source_target_pairs={{0,16},{4,20},{8,24},{12,28},{16,0},{20,4},{24,8},{28,12},{1,17},{... | collective-permute-start | bytes 442376 | tf_op jit(solution)/shard_map/ppermute | solution.py:432
  57.1 3.3 %collective-permute-done.7 = bf16[192,768]{1,0:T(8,128)(2,1)S(1)} collective-permute-done((bf16[192,768]{1,0:T(8,128)(2,1)}, bf16[192,768]{1,0:T(8,128)(2,1)S(1)}, u32[]{:S(2)}, u32[]{:S(2)}) %collective-permute-start.7) | collective-permute-done | bytes 294944 | tf_op jit(solution)/shard_map/ppermute | solution.py:432
  60.4 0.0 copy-done
  60.4 2.7 %collective-permute-start.8 = (bf16[1,96,768]{2,1,0:T(8,128)(2,1)S(1)}, bf16[1,96,768]{2,1,0:T(8,128)(2,1)S(1)}, u32[]{:S(2)}, u32[]{:S(2)}) collective-permute-start(bf16[1,96,768]{2,1,0:T(8,128)(2,1)S(1)} %get-tuple-element.71), channel_id=1, source_target_pairs={{0,16},{4,20},{8,24},{12,28},{16,0},{20,4},{24,8},{28,12},{1,17},{... | collective-permute-start | bytes 442376 | tf_op jit(solution)/shard_map/ppermute | solution.py:432
  63.1 0.0 copy-start.1
  63.1 0.0 all-to-all-done.tile_ref
  63.1 0.6 shard_map.232
  63.7 0.0 collective-permute-done.2.got_ref
  63.7 1.0 %shard_map.225 = (bf16[256,768]{1,0:T(8,128)(2,1)}, bf16[256,768]{1,0:T(8,128)(2,1)}) custom-call(bf16[256,768]{1,0:T(8,128)(2,1)S(1)} %shard_map.224.own_ref, bf16[256,768]{1,0:T(8,128)(2,1)S(1)} %collective-permute-done.2.got_ref), custom_call_target="tpu_custom_call" | custom-call | bytes 1572864 | tf_op jit(solution)/shard_map/pallas_call | solution.py:420
  64.7 0.0 collective-permute-done.6.got_ref
  64.7 0.0 copy-done.1
  64.7 0.8 %shard_map.231 = (f32[96,576]{1,0:T(8,128)}, f32[192,96]{1,0:T(8,128)}) custom-call(f32[1,96,768]{2,1,0:T(8,128)S(1)} %copy-done.1, bf16[1,96,768]{2,1,0:T(8,128)(2,1)S(1)} %collective-permute-done.6.got_ref), custom_call_target="tpu_custom_call" | custom-call | bytes 737280 | tf_op jit(solution)/shard_map/pallas_call | solution.py:420
  65.5 4.1 %collective-permute-done.10.got_ref = bf16[1,96,768]{2,1,0:T(8,128)(2,1)S(1)} collective-permute-done((bf16[1,96,768]{2,1,0:T(8,128)(2,1)S(1)}, bf16[1,96,768]{2,1,0:T(8,128)(2,1)S(1)}, u32[]{:S(2)}, u32[]{:S(2)}) %collective-permute-start.10) | collective-permute-done | bytes 147488 | tf_op jit(solution)/shard_map/ppermute | solution.py:432
  69.6 0.7 %shard_map.236 = f32[96,768]{1,0:T(8,128)} custom-call(f32[1,96,768]{2,1,0:T(8,128)S(1)} %get-tuple-element.74.keep_ref, bf16[1,96,768]{2,1,0:T(8,128)(2,1)S(1)} %collective-permute-done.10.got_ref), custom_call_target="tpu_custom_call" | custom-call | bytes 737280 | tf_op jit(solution)/shard_map/pallas_call | solution.py:420
  70.4 1.8 %collective-permute-done.8.got_ref = bf16[1,96,768]{2,1,0:T(8,128)(2,1)S(1)} collective-permute-done((bf16[1,96,768]{2,1,0:T(8,128)(2,1)S(1)}, bf16[1,96,768]{2,1,0:T(8,128)(2,1)S(1)}, u32[]{:S(2)}, u32[]{:S(2)}) %collective-permute-start.8) | collective-permute-done | bytes 147488 | tf_op jit(solution)/shard_map/ppermute | solution.py:432
  72.2 0.7 %shard_map.234 = f32[96,768]{1,0:T(8,128)} custom-call(f32[1,96,768]{2,1,0:T(8,128)S(1)} %get-tuple-element.70.keep_ref, bf16[1,96,768]{2,1,0:T(8,128)(2,1)S(1)} %collective-permute-done.8.got_ref), custom_call_target="tpu_custom_call" | custom-call | bytes 737280 | tf_op jit(solution)/shard_map/pallas_call | solution.py:420
  (2 shorter events, 0.1 us)
Async XLA Ops:
  0.6 14.6 %copy-start.4 = (s32[256]{0:T(256)S(1)}, s32[256]{0:T(256)}, u32[]{:S(2)}) copy-start(s32[256]{0:T(256)} %param.16) | copy-start | bytes 3076
  0.7 0.7 %copy-start.3 = (s32[256]{0:T(256)S(1)}, s32[256]{0:T(256)}, u32[]{:S(2)}) copy-start(s32[256]{0:T(256)} %param.16) | copy-start | bytes 3076
  1.4 13.9 %copy-start.7 = (f32[768]{0:T(1024)S(1)}, f32[768]{0:T(1024)}, u32[]{:S(2)}) copy-start(f32[768]{0:T(1024)} %param.19) | copy-start | bytes 9220
  1.4 13.9 %copy-start.8 = (f32[768]{0:T(1024)S(1)}, f32[768]{0:T(1024)}, u32[]{:S(2)}) copy-start(f32[768]{0:T(1024)} %param.20) | copy-start | bytes 9220
  1.4 13.9 %copy-start.9 = (f32[768]{0:T(1024)S(1)}, f32[768]{0:T(1024)}, u32[]{:S(2)}) copy-start(f32[768]{0:T(1024)} %param.26) | copy-start | bytes 9220
  1.4 13.9 %copy-start.10 = (f32[768]{0:T(1024)S(1)}, f32[768]{0:T(1024)}, u32[]{:S(2)}) copy-start(f32[768]{0:T(1024)} %param.17) | copy-start | bytes 9220
  1.4 13.9 %copy-start.11 = (f32[768]{0:T(1024)S(1)}, f32[768]{0:T(1024)}, u32[]{:S(2)}) copy-start(f32[768]{0:T(1024)} %param.18) | copy-start | bytes 9220
  1.4 13.9 %copy-start.12 = (f32[3,192]{1,0:T(4,128)S(1)}, f32[3,192]{1,0:T(4,128)}, u32[]{:S(2)}) copy-start(f32[3,192]{1,0:T(4,128)} %offsets_ref.3) | copy-start | bytes 6916
  2.5 12.8 %collective-permute-start.3 = (bf16[272,768]{1,0:T(8,128)(2,1)S(1)}, bf16[272,768]{1,0:T(8,128)(2,1)S(1)}, u32[]{:S(2)}, u32[]{:S(2)}) collective-permute-start(bf16[272,768]{1,0:T(8,128)(2,1)S(1)} %shard_map.226), channel_id=1, source_target_pairs={{0,8},{4,12},{8,0},{12,4},{16,24},{20,28},{24,16},{28,20},{1,9},{5... | collective-permute-start | bytes 1253384 | tf_op jit(solution)/shard_map/ppermute | solution.py:432
  15.3 11.1 %collective-permute-start.4 = (bf16[272,768]{1,0:T(8,128)(2,1)S(1)}, bf16[272,768]{1,0:T(8,128)(2,1)S(1)}, u32[]{:S(2)}, u32[]{:S(2)}) collective-permute-start(bf16[272,768]{1,0:T(8,128)(2,1)S(1)} %collective-permute-done.3.got_ref), channel_id=1, source_target_pairs={{0,1},{1,0},{2,3},{3,2},{4,5},{5,4},{6,7},{7,6},{8,9},{9,8},{10,11... | collective-permute-start | bytes 1253384 | tf_op jit(solution)/shard_map/ppermute | solution.py:432
  22.7 6.1 %copy-start.2 = (f32[8,4,16,96]{3,2,1,0:T(8,128)}, f32[8,4,16,96]{3,2,1,0:T(8,128)S(1)}, u32[]{:S(2)}) copy-start(f32[8,4,16,96]{3,2,1,0:T(8,128)S(1)} %get-tuple-element.65) | copy-start | bytes 589828
  22.7 1.9 %collective-permute-start = (bf16[256,768]{1,0:T(8,128)(2,1)S(1)}, bf16[256,768]{1,0:T(8,128)(2,1)S(1)}, u32[]{:S(2)}, u32[]{:S(2)}) collective-permute-start(bf16[256,768]{1,0:T(8,128)(2,1)S(1)} %get-tuple-element.45), channel_id=1, source_target_pairs={{0,1},{1,0},{2,3},{3,2},{4,5},{5,4},{6,7},{7,6},{8,9},{9,8},{10,11... | collective-permute-start | bytes 1179656 | tf_op jit(solution)/shard_map/ppermute | solution.py:432
  24.7 14.8 %collective-permute-start.1 = (bf16[256,768]{1,0:T(8,128)(2,1)S(1)}, bf16[256,768]{1,0:T(8,128)(2,1)S(1)}, u32[]{:S(2)}, u32[]{:S(2)}) collective-permute-start(bf16[256,768]{1,0:T(8,128)(2,1)S(1)} %shard_map.223.part_ref), channel_id=1, source_target_pairs={{0,2},{1,3},{2,0},{3,1},{4,6},{5,7},{6,4},{7,5},{8,10},{9,11},{10,... | collective-permute-start | bytes 1179656 | tf_op jit(solution)/shard_map/ppermute | solution.py:432
  30.3 9.1 %copy-start.5 = (f32[768]{0:T(1024)S(1)}, f32[768]{0:T(1024)}, u32[]{:S(2)}) copy-start(f32[768]{0:T(1024)} %param.24) | copy-start | bytes 9220
  30.3 9.1 %copy-start.6 = (f32[768]{0:T(1024)S(1)}, f32[768]{0:T(1024)}, u32[]{:S(2)}) copy-start(f32[768]{0:T(1024)} %param.28) | copy-start | bytes 9220
  35.9 10.2 %collective-permute-start.5 = (bf16[192,768]{1,0:T(8,128)(2,1)}, bf16[192,768]{1,0:T(8,128)(2,1)}, u32[]{:S(2)}, u32[]{:S(2)}) collective-permute-start(bf16[192,768]{1,0:T(8,128)(2,1)} %get-tuple-element.61), channel_id=1, source_target_pairs={{0,4},{4,0},{8,12},{12,8},{16,20},{20,16},{24,28},{28,24},{1,5},{5... | collective-permute-start | bytes 884744 | tf_op jit(solution)/shard_map/ppermute | solution.py:432
  37.4 17.1 %collective-permute-start.9 = (bf16[192,768]{1,0:T(8,128)(2,1)}, bf16[192,768]{1,0:T(8,128)(2,1)S(1)}, u32[]{:S(2)}, u32[]{:S(2)}) collective-permute-start(bf16[192,768]{1,0:T(8,128)(2,1)} %get-tuple-element.73), channel_id=1, source_target_pairs={{0,4},{4,0},{8,12},{12,8},{16,20},{20,16},{24,28},{28,24},{1,5},{5... | collective-permute-start | bytes 884744 | tf_op jit(solution)/shard_map/ppermute | solution.py:432
  37.9 22.5 %collective-permute-start.7 = (bf16[192,768]{1,0:T(8,128)(2,1)}, bf16[192,768]{1,0:T(8,128)(2,1)S(1)}, u32[]{:S(2)}, u32[]{:S(2)}) collective-permute-start(bf16[192,768]{1,0:T(8,128)(2,1)} %get-tuple-element.69), channel_id=1, source_target_pairs={{0,4},{4,0},{8,12},{12,8},{16,20},{20,16},{24,28},{28,24},{1,5},{5... | collective-permute-start | bytes 884744 | tf_op jit(solution)/shard_map/ppermute | solution.py:432
  39.8 23.9 %collective-permute-start.2 = (bf16[256,768]{1,0:T(8,128)(2,1)S(1)}, bf16[256,768]{1,0:T(8,128)(2,1)S(1)}, u32[]{:S(2)}, u32[]{:S(2)}) collective-permute-start(bf16[256,768]{1,0:T(8,128)(2,1)S(1)} %shard_map.224.own_ref), channel_id=1, source_target_pairs={{0,1},{1,0},{2,3},{3,2},{4,5},{5,4},{6,7},{7,6},{8,9},{9,8},{10,11... | collective-permute-start | bytes 1179656 | tf_op jit(solution)/shard_map/ppermute | solution.py:432
  39.8 23.2 %all-to-all-start = ((f32[32,16,96]{2,1,0:T(8,128)}), f32[32,16,96]{2,1,0:T(8,128)S(1)}, u32[]{:S(2)}, u32[]{:S(2)}) async-start(f32[32,16,96]{2,1,0:T(8,128)} %bitcast.23), calls=%async_computation | async-start | bytes 524288 | tf_op jit(solution)/shard_map/all_to_all | solution.py:502
  47.1 13.3 %copy-start = (f32[1,96,768]{2,1,0:T(8,128)}, f32[1,96,768]{2,1,0:T(8,128)S(1)}, u32[]{:S(2)}) copy-start(f32[1,96,768]{2,1,0:T(8,128)S(1)} %get-tuple-element.62.keep_ref) | copy-start | bytes 884740
  47.1 17.6 %collective-permute-start.6 = (bf16[1,96,768]{2,1,0:T(8,128)(2,1)S(1)}, bf16[1,96,768]{2,1,0:T(8,128)(2,1)S(1)}, u32[]{:S(2)}, u32[]{:S(2)}) collective-permute-start(bf16[1,96,768]{2,1,0:T(8,128)(2,1)S(1)} %get-tuple-element.63), channel_id=1, source_target_pairs={{0,16},{4,20},{8,24},{12,28},{16,0},{20,4},{24,8},{28,12},{1,17},{... | collective-permute-start | bytes 442376 | tf_op jit(solution)/shard_map/ppermute | solution.py:432
  54.5 15.1 %collective-permute-start.10 = (bf16[1,96,768]{2,1,0:T(8,128)(2,1)S(1)}, bf16[1,96,768]{2,1,0:T(8,128)(2,1)S(1)}, u32[]{:S(2)}, u32[]{:S(2)}) collective-permute-start(bf16[1,96,768]{2,1,0:T(8,128)(2,1)S(1)} %get-tuple-element.75), channel_id=1, source_target_pairs={{0,16},{4,20},{8,24},{12,28},{16,0},{20,4},{24,8},{28,12},{1,17},{... | collective-permute-start | bytes 442376 | tf_op jit(solution)/shard_map/ppermute | solution.py:432
  60.4 11.8 %collective-permute-start.8 = (bf16[1,96,768]{2,1,0:T(8,128)(2,1)S(1)}, bf16[1,96,768]{2,1,0:T(8,128)(2,1)S(1)}, u32[]{:S(2)}, u32[]{:S(2)}) collective-permute-start(bf16[1,96,768]{2,1,0:T(8,128)(2,1)S(1)} %get-tuple-element.71), channel_id=1, source_target_pairs={{0,16},{4,20},{8,24},{12,28},{16,0},{20,4},{24,8},{28,12},{1,17},{... | collective-permute-start | bytes 442376 | tf_op jit(solution)/shard_map/ppermute | solution.py:432
  63.1 1.6 %copy-start.1 = (f32[1,96,768]{2,1,0:T(8,128)S(1)}, f32[1,96,768]{2,1,0:T(8,128)}, u32[]{:S(2)}) copy-start(f32[1,96,768]{2,1,0:T(8,128)} %copy-done) | copy-start | bytes 884740

commit v3 on v2

--- a/solution.py
+++ b/solution.py
@@ -113,7 +113,7 @@
         back = attended_grad[:, head * size : (head + 1) * size]
         scores = jnp.where(allowed, dot_t(query, key) * 0.125, -jnp.inf)
         raised = jnp.exp(scores - jnp.max(scores, axis=-1, keepdims=True))
-        weight = raised / jnp.sum(raised, axis=-1, keepdims=True)
+        weight = raised * (1.0 / jnp.sum(raised, axis=-1, keepdims=True))
         softmax = weight.astype(BF16)
         attended.append(dot(softmax, value).astype(BF16))
         prob_grad = dot_t(back, value)
@@ -147,8 +147,10 @@
     return jnp.where(down[:, :1] >= 0.0, 1.0, 0.0)
 
 
-def gather_kernel(tok_ref, cot_ref, seg_ref, out_ref, sem):
+def gather_kernel(tok_ref, cot_ref, seg_any, out_ref, seg_ref, sem, seg_sem):
     n = tok_ref.shape[0]
+    labels = pltpu.make_async_copy(seg_any, seg_ref, seg_sem)
+    labels.start()
 
     @pl.when(core_bit() == 0)
     def _():
@@ -159,6 +161,7 @@
         pltpu.make_async_copy(cot_ref, out_ref.at[0:n], sem).start()
 
     width = out_ref.shape[1]
+    labels.wait()
     row = label_row(seg_ref)
     row = jnp.concatenate([row, jnp.zeros((1, width - n), F32)], axis=1)
     out_ref[n : n + 16] = jnp.broadcast_to(row, (16, width)).astype(BF16)
@@ -170,7 +173,7 @@
     tok_any, cot_any, seg_ref, gain_one_ref, shift_one_ref, gain_two_ref, shift_two_ref, offsets_ref, thr_ref,
     inlet_any, outlet_any, expand_any, contract_any,
     tok_ref, cot_ref, inlet_ref, outlet_ref, expand_ref, contract_ref,
-    away_ref, keep_ref, active_ref, back_ref, attended_ref, inlet_back_ref, tile_ref,
+    away_ref, keep_ref, active_ref, back_ref, attended_ref, inlet_back_ref, tile_ref, one_ref, two_ref, out_ref,
     sems,
 ):
     copies = [
@@ -195,6 +198,9 @@
     copies[1].wait()
     grad_full = cot_ref[...].astype(F32) * live
     grad_out = grad_full.astype(BF16)
+    put_left(normed_one, one_ref)
+    put_left(normed_two, two_ref)
+    put_left(grad_out, out_ref)
     copies[2].wait()
     copies[3].wait()
     active, expanded_grad = ffn_block(normed_two, grad_out, expand_ref[...], thr, contract_ref[...])
@@ -246,7 +252,7 @@
             tile_ref[d, t, 5:6, :per_dp] = hidden[:, d * per_dp : (d + 1) * per_dp]
             for head in range(heads):
                 at = head * 3 * size + d * third
-                tile_ref[d, t, 8 + head : 9 + head, :third] = shares[:, at : at + third]
+                tile_ref[d, t, 6:7, head * third : (head + 1) * third] = shares[:, at : at + third]
 
         put(lax.axis_index("tensor"))
 
@@ -263,17 +269,24 @@
     return lax.axis_index("tensor") % 2
 
 
-def spread_rows(left, left_ref, dests):
-    width = left.shape[1]
+def put_left(left, ref):
+    ref[...] = left.T if ref.shape[0] != left.shape[0] else left
+
+
+def left_shape(n, width, dests):
+    return (width, n) if width // dests % 16 == 0 and width != n else (n, width)
+
+
+def spread_rows(refs, dests):
+    _, width = sorted(refs[0].shape)
     block = width // dests
-    if block % 16 == 0:
-        left_ref[...] = left.T
+    if refs[0].shape[0] == width:
         rows = []
         for flip in (1, 0):
             first = first_bit() if flip == 0 else 1 - first_bit()
             for rest in range(dests // 4):
-                start = (4 * rest + 2 * gather_bit() + first) * block
-                rows.append(left_ref[pl.ds(pl.multiple_of(start, 16), block), :])
+                start = pl.multiple_of((4 * rest + 2 * gather_bit() + first) * block, 16)
+                rows.append(jnp.concatenate([ref[pl.ds(start, block), :] for ref in refs], axis=1))
         return jnp.concatenate(rows, axis=0)
     half = dests // 4 * block
     row = lax.broadcasted_iota(jnp.int32, (2 * half, width), 0)
@@ -282,6 +295,7 @@
     row = jnp.where(kept, row - half, row)
     first = jnp.where(kept, first_bit(), 1 - first_bit())
     want = row + (row // block) * 3 * block + (2 * gather_bit() + first) * block
+    left = jnp.concatenate([ref[...] for ref in refs], axis=0)
     return dot_t(jnp.where(want == col, 1.0, 0.0).astype(BF16), left).astype(BF16)
 
 
@@ -301,64 +315,51 @@
 
 def expand_kernel(
     dests,
-    got_ref, swap_ref, tok_ref, gain_ref, shift_ref, expand_ref, thr_ref, contract_ref, back_ref,
-    send_ref, keep_ref, active_ref,
+    got_ref, swap_ref, two_ref, gain_ref, shift_ref, expand_ref, thr_ref, contract_ref, back_ref,
+    send_ref, keep_ref, active_ref, grad_ref,
     left_ref,
 ):
-    n = tok_ref.shape[0]
+    n = back_ref.shape[0]
     tok, cot, seg = partner_inputs(got_ref, swap_ref, n)
-    gain, shift = flat(gain_ref), flat(shift_ref)
     scaled, _ = norm_parts(tok)
-    normed = (scaled * gain + shift).astype(BF16)
-    scaled, _ = norm_parts(tok_ref[...])
-    normed_own = (scaled * gain + shift).astype(BF16)
+    normed = (scaled * flat(gain_ref) + flat(shift_ref)).astype(BF16)
     grad_out = (cot.astype(F32) * live_column(seg)).astype(BF16)
+    grad_ref[...] = grad_out
+    put_left(normed, left_ref)
     active, grad = ffn_block(normed, grad_out, expand_ref[...], flat(thr_ref), contract_ref[...])
     active_ref[...] = active
-    rows = spread_rows(jnp.concatenate([normed_own, normed], axis=0), left_ref, dests)
-    put_halves(dot(rows, jnp.concatenate([back_ref[...], grad.astype(BF16)], axis=0)), send_ref, keep_ref)
-
-
-def contract_kernel(
-    dests,
-    got_ref, swap_ref, cot_ref, seg_ref, own_ref, active_ref,
+    right = jnp.concatenate([back_ref[...], grad.astype(BF16)], axis=0)
+    put_halves(dot(spread_rows((two_ref, left_ref), dests), right), send_ref, keep_ref)
+
+
+def contract_kernel(dests, grad_ref, out_ref, own_ref, active_ref, send_ref, keep_ref, left_ref):
+    put_left(grad_ref[...], left_ref)
+    right = jnp.concatenate([own_ref[...], active_ref[...]], axis=0)
+    put_halves(dot(spread_rows((out_ref, left_ref), dests), right), send_ref, keep_ref)
+
+
+def attention_kernel(
+    heads, size, dests,
+    got_ref, swap_ref, grad_ref, gain_ref, shift_ref, inlet_ref, offsets_ref, outlet_ref, attended_ref, inlet_back_ref,
+    one_ref, out_ref, near_ref,
     send_ref, keep_ref,
     left_ref,
 ):
-    n = cot_ref.shape[0]
-    _, cot, seg = partner_inputs(got_ref, swap_ref, n)
-    grad_out = (cot.astype(F32) * live_column(seg)).astype(BF16)
-    grad_own = (cot_ref[...].astype(F32) * live_column(label_row(seg_ref))).astype(BF16)
-    rows = spread_rows(jnp.concatenate([grad_own, grad_out], axis=0), left_ref, dests)
-    put_halves(dot(rows, jnp.concatenate([own_ref[...], active_ref[...]], axis=0)), send_ref, keep_ref)
-
-
-def attention_kernel(
-    heads, size, dests,
-    got_ref, swap_ref, tok_ref, cot_ref, seg_ref, gain_ref, shift_ref, inlet_ref, offsets_ref, outlet_ref, attended_ref, inlet_back_ref, after_ref,
-    send_ref, keep_ref,
-    left_ref,
-):
-    n = tok_ref.shape[0]
-    tok, cot, seg = partner_inputs(got_ref, swap_ref, n)
-    allowed, live, position = label_tables(seg)
-    gain, shift = flat(gain_ref), flat(shift_ref)
+    n = attended_ref.shape[0]
+    tok, _, seg = partner_inputs(got_ref, swap_ref, n)
+    allowed, _, position = label_tables(seg)
     offsets = jnp.concatenate([offsets_ref[i : i + 1, :] for i in range(heads)], axis=1)
     scaled, _ = norm_parts(tok)
-    normed = (scaled * gain + shift).astype(BF16)
-    scaled, _ = norm_parts(tok_ref[...])
-    normed_own = (scaled * gain + shift).astype(BF16)
-    grad_out = (cot.astype(F32) * live).astype(BF16)
-    grad_own = (cot_ref[...].astype(F32) * live_column(label_row(seg_ref))).astype(BF16)
+    normed = (scaled * flat(gain_ref) + flat(shift_ref)).astype(BF16)
+    put_left(normed, left_ref)
     attended, inlet_full = attention_block(
-        normed, grad_out, allowed, position, inlet_ref[...], offsets, outlet_ref[...], heads, size
-    )
-    columns = inlet_ref.shape[0]
-    inlet_back = inlet_full.astype(BF16)[:, :columns]
-    rows = spread_rows(jnp.concatenate([normed_own, normed], axis=0), left_ref, dests)
-    first = dot(rows, jnp.concatenate([inlet_back_ref[...], inlet_back], axis=0))
-    rows = spread_rows(jnp.concatenate([grad_own, grad_out], axis=0), left_ref, dests)
-    second = dot(rows, jnp.concatenate([attended_ref[...], attended], axis=0))
+        normed, grad_ref[...], allowed, position, inlet_ref[...], offsets, outlet_ref[...], heads, size
+    )
+    inlet_back = inlet_full.astype(BF16)[:, : inlet_ref.shape[0]]
+    right = jnp.concatenate([inlet_back_ref[...], inlet_back], axis=0)
+    first = dot(spread_rows((one_ref, left_ref), dests), right)
+    right = jnp.concatenate([attended_ref[...], attended], axis=0)
+    second = dot(spread_rows((out_ref, near_ref), dests), right)
     put_halves(jnp.concatenate([first, second], axis=1), send_ref, keep_ref)
 
 
@@ -407,7 +408,8 @@
     norms_ref[...] = total[0:4]
     bias_ref[...] = total[4:5]
     thr_ref[...] = total[5:6, : thr_ref.shape[1]]
-    offsets_ref[...] = total[8 : 8 + heads, :third]
+    for head in range(heads):
+        offsets_ref[head : head + 1] = total[6:7, head * third : (head + 1) * third]
 
 
 def call(kernel, outs, args, flops=0, scratch=(), limit=VMEM_LIMIT, places="", results=""):
@@ -444,42 +446,46 @@
     gain_one, shift_one, gain_two, shift_two = map(folded, (first_gain, first_shift, second_gain, second_shift))
     thr = folded(thresholds)
 
+    turned = left_shape(n, width, n_dp)
+
     payload, = call(
         gather_kernel, [((n + 16, width), BF16)], [tokens, cotangent, seg],
-        scratch=[pltpu.SemaphoreType.DMA], places="aav",
+        scratch=[pltpu.VMEM(seg.shape, seg.dtype), pltpu.SemaphoreType.DMA, pltpu.SemaphoreType.DMA], places="aaa",
     )
     got = swap(payload, "dp", n_dp, 2)
     other = swap(got, "tensor", n_tensor, 1)
 
-    (tok, cot, inlet_v, outlet_v, expand_v, contract_v, away, keep, active, back, attended, inlet_back, tile) = call(
+    (tok, cot, inlet_v, outlet_v, expand_v, contract_v, away, keep, active, back, attended, inlet_back, tile,
+     one_t, two_t, out_t) = call(
         functools.partial(own_kernel, heads, size, n_dp, n_tensor),
         [(tokens.shape, BF16), (cotangent.shape, BF16), ((columns, width), BF16), (outlet.shape, BF16), (expand.shape, BF16),
          (contract.shape, BF16), ((n, width), BF16), ((n, width), F32), ((n, units), BF16), ((n, units), BF16),
-         ((n, mine), BF16), ((n, columns), BF16), ((n_dp, n_tensor, 16, block), F32)],
+         ((n, mine), BF16), ((n, columns), BF16), ((n_dp, n_tensor, 8, block), F32),
+         (turned, BF16), (turned, BF16), (turned, BF16)],
         [tokens, cotangent, seg, gain_one, shift_one, gain_two, shift_two, offsets, thr, inlet.T, outlet, expand, contract],
         flops=6e9, scratch=[pltpu.SemaphoreType.DMA((6,))], places="aavvvvvvvaaaa",
     )
     half = n_dp // 4 * block
-    left = [pltpu.VMEM((width, 2 * n), BF16)]
-
-    expand_send, expand_keep, active_near = call(
+    left = [pltpu.VMEM(turned, BF16)]
+
+    expand_send, expand_keep, active_near, grad_near = call(
         functools.partial(expand_kernel, n_dp),
-        [((half, units), BF16), ((half, units), F32), ((n, units), BF16)],
-        [got, other, tok, gain_two, shift_two, expand_v, thr, contract_v, back],
+        [((half, units), BF16), ((half, units), F32), ((n, units), BF16), ((n, width), BF16)],
+        [got, other, two_t, gain_two, shift_two, expand_v, thr, contract_v, back],
         flops=3e9, scratch=left,
     )
     expand_got = swap(expand_send, "dp", n_dp, 1)
-    contract_send, contract_keep = call(
+    contract_send, contract_keep, near_t = call(
         functools.partial(contract_kernel, n_dp),
-        [((half, units), BF16), ((half, units), F32)],
-        [got, other, cot, seg, active, active_near],
-        flops=1e9, scratch=left,
+        [((half, units), BF16), ((half, units), F32), (turned, BF16)],
+        [grad_near, out_t, active, active_near],
+        flops=1e9,
     )
     contract_got = swap(contract_send, "dp", n_dp, 1)
     tail_send, tail_keep = call(
         functools.partial(attention_kernel, heads, size, n_dp),
         [((half, columns + mine), BF16), ((half, columns + mine), F32)],
-        [got, other, tok, cot, seg, gain_one, shift_one, inlet_v, offsets, outlet_v, attended, inlet_back, contract_keep],
+        [got, other, grad_near, gain_one, shift_one, inlet_v, offsets, outlet_v, attended, inlet_back, one_t, out_t, near_t],
         flops=5e9, scratch=left,
     )
     tail_got = swap(tail_send, "dp", n_dp, 1)
@@ -499,7 +505,7 @@
     paired = swap(done, "tensor", n_tensor, 1)
     mixed, input_grad = call(pair_kernel, [((n, width), BF16)] * 2, [done, paired], results="dd")
 
-    tile = lax.all_to_all(tile.reshape(n_dp * n_tensor, 16, block), ("dp", "tensor"), 0, 0, tiled=True)
+    tile = lax.all_to_all(tile.reshape(n_dp * n_tensor, 8, block), ("dp", "tensor"), 0, 0, tiled=True)
     third = offsets.shape[1] // n_dp
     norm_grads, bias_grad, thr_grad, offsets_grad = call(
         functools.partial(small_kernel, heads, third),

time: 73.2 us -> 69.2 us (0.945)
  waiting for transfers between devices: 27.2 us -> 23.1 us
    ppermute x11, waiting for transfers between devices: 27.2 us -> 20.6 us  [swap(): return lax.ppermute(value, axis, [(i, i ^ bit) for i in range(count)])]
    all_to_all x1, waiting for transfers between devices: 0.01 us -> 2.52 us  [step(): lax.all_to_all(tile.reshape(n_dp * n_tensor, 8, block), ('dp', 'tensor'),...]
  transfers between devices with their start and end apart: 12 -> 12, of which waited for: 7 -> 8; matrix products, arithmetic and copies ran while one was open for 0% -> 0% of each run, Pallas kernels for 29% -> 30%
where the time goes in v3:
time: 69.2 us; the launch traced here: 68.9 us
  waiting for transfers between devices  23.1 us (33%)
  Pallas kernels  22.7 us (33%)
  starting transfers between devices  21.2 us (31%)
  local copies, waits for them, and re-layouts  1 us (1%)
  between operations  0.84 us (1%)
    pallas_call x15, Pallas kernels, call(): pl.pallas_call(kernel, out_shape=[jax.ShapeDtypeStruct(shape, dtype) for...  22.7 us
    ppermute x11, waiting for transfers between devices, swap(): return lax.ppermute(value, axis, [(i, i ^ bit) for i in range(count)])  20.6 us
    ppermute x11, starting transfers between devices, swap(): return lax.ppermute(value, axis, [(i, i ^ bit) for i in range(count)])  17 us
    all_to_all x1, starting transfers between devices, step(): lax.all_to_all(tile.reshape(n_dp * n_tensor, 8, block), ('dp', 'tensor'),...  4.17 us
    all_to_all x1, waiting for transfers between devices, step(): lax.all_to_all(tile.reshape(n_dp * n_tensor, 8, block), ('dp', 'tensor'),...  2.52 us
  transfers between devices with their start and end apart: 12, of which 8 were waited for; matrix products, arithmetic and copies ran while one was open for 0% of the time, Pallas kernels for 30%

profile of v3, /device:TPU:0, one launch (start us, length us, event | category | flops | bytes accessed | tf_op | source)
XLA Modules:
  0.0 68.9 jit_solution(16325137560524087067)
XLA Ops:
  0.6 0.0 copy-start.2
  0.7 0.0 copy-start.10
  0.7 0.0 copy-start.7
  0.7 0.0 copy-start.6
  0.7 0.0 copy-start.5
  0.7 0.0 copy-start.9
  0.7 0.0 copy-start.8
  0.7 1.1 %shard_map.226 = bf16[272,768]{1,0:T(8,128)(2,1)S(1)} custom-call(bf16[256,768]{1,0:T(8,128)(2,1)} %tok_ref.1, bf16[256,768]{1,0:T(8,128)(2,1)} %cot_ref.1, s32[2,128]{1,0:T(2,128)} %bitcast.23), custom_call_target="tpu_custom_call" | custom-call | bytes 1205248 | tf_op jit(solution)/shard_map/pallas_call | solution.py:422
  1.8 3.1 %collective-permute-start.3 = (bf16[272,768]{1,0:T(8,128)(2,1)S(1)}, bf16[272,768]{1,0:T(8,128)(2,1)S(1)}, u32[]{:S(2)}, u32[]{:S(2)}) collective-permute-start(bf16[272,768]{1,0:T(8,128)(2,1)S(1)} %shard_map.226), channel_id=1, source_target_pairs={{0,8},{4,12},{8,0},{12,4},{16,24},{20,28},{24,16},{28,20},{1,9},{5... | collective-permute-start | bytes 1253384 | tf_op jit(solution)/shard_map/ppermute | solution.py:434
  4.9 9.6 %collective-permute-done.3.got_ref = bf16[272,768]{1,0:T(8,128)(2,1)S(1)} collective-permute-done((bf16[272,768]{1,0:T(8,128)(2,1)S(1)}, bf16[272,768]{1,0:T(8,128)(2,1)S(1)}, u32[]{:S(2)}, u32[]{:S(2)}) %collective-permute-start.3) | collective-permute-done | bytes 417824 | tf_op jit(solution)/shard_map/ppermute | solution.py:434
  14.6 0.0 collective-permute-start.4
  14.6 0.0 copy-done.2
  14.6 0.0 copy-done.10
  14.6 0.0 copy-done.7
  14.6 0.0 copy-done.6
  14.6 0.0 copy-done.5
  14.6 0.0 copy-done.9
  14.6 0.0 copy-done.8
  14.6 8.0 %shard_map.222 = (bf16[256,768]{1,0:T(8,128)(2,1)S(1)}, bf16[256,768]{1,0:T(8,128)(2,1)S(1)}, bf16[576,768]{1,0:T(8,128)(2,1)S(1)}, bf16[192,768]{1,0:T(8,128)(2...) custom-call(bf16[256,768]{1,0:T(8,128)(2,1)} %tok_ref.1, ...), custom_call_target="tpu_custom_call" | custom-call | flops 6000000000 | bytes 12306688 | tf_op jit(solution)/shard_map/pallas_call | solution.py:422
  22.6 0.6 collective-permute-start
  23.2 1.3 %collective-permute-done.got_ref = bf16[256,768]{1,0:T(8,128)(2,1)S(1)} collective-permute-done((bf16[256,768]{1,0:T(8,128)(2,1)S(1)}, bf16[256,768]{1,0:T(8,128)(2,1)S(1)}, u32[]{:S(2)}, u32[]{:S(2)}) %collective-permute-start) | collective-permute-done | bytes 393248 | tf_op jit(solution)/shard_map/ppermute | solution.py:434
  24.5 0.1 shard_map.223.part_ref
  24.6 1.7 %collective-permute-start.1 = (bf16[256,768]{1,0:T(8,128)(2,1)S(1)}, bf16[256,768]{1,0:T(8,128)(2,1)S(1)}, u32[]{:S(2)}, u32[]{:S(2)}) collective-permute-start(bf16[256,768]{1,0:T(8,128)(2,1)S(1)} %shard_map.223.part_ref), channel_id=1, source_target_pairs={{0,2},{1,3},{2,0},{3,1},{4,6},{5,7},{6,4},{7,5},{8,10},{9,11},{10,... | collective-permute-start | bytes 1179656 | tf_op jit(solution)/shard_map/ppermute | solution.py:434
  26.4 0.0 collective-permute-done.4.swap_ref
  26.4 2.1 %shard_map.227 = (bf16[192,768]{1,0:T(8,128)(2,1)}, f32[192,768]{1,0:T(8,128)S(1)}, bf16[256,768]{1,0:T(8,128)(2,1)S(1)}, bf16[256,768]{1,0:T(8,128)(2,1)S(1)}) custom-call(bf16[272,768]{1,0:T(8,128)(2,1)S(1)} %collective-permute-done.3.got_ref, bf16[272,768]{1,0:T(8,128)(2,1)S(1)} %collective-permute-done.4.swap_ref, ...), custom_call_target="tpu_custom_call" | custom-call | flops 3000000000 | bytes 5661696 | tf_op jit(solution)/shard_map/pallas_call | solution.py:422
  28.5 1.5 %collective-permute-start.7 = (bf16[192,768]{1,0:T(8,128)(2,1)}, bf16[192,768]{1,0:T(8,128)(2,1)S(1)}, u32[]{:S(2)}, u32[]{:S(2)}) collective-permute-start(bf16[192,768]{1,0:T(8,128)(2,1)} %get-tuple-element.78), channel_id=1, source_target_pairs={{0,4},{4,0},{8,12},{12,8},{16,20},{20,16},{24,28},{28,24},{1,5},{5... | collective-permute-start | bytes 884744 | tf_op jit(solution)/shard_map/ppermute | solution.py:434
  30.0 1.3 %shard_map.228 = (bf16[192,768]{1,0:T(8,128)(2,1)}, f32[192,768]{1,0:T(8,128)S(1)}, bf16[768,256]{1,0:T(8,128)(2,1)S(1)}) custom-call(bf16[256,768]{1,0:T(8,128)(2,1)S(1)} %get-tuple-element.59.grad_ref, bf16[768,256]{1,0:T(8,128)(2,1)S(1)} %get-tuple-element.65.out_ref, bf16[256,768]{1,0:T(8,128)(2,1)S(1)} %get-tuple-element.66.own_ref, ...), custom_call_target="tpu_custom_call" | custom-call | flops 1000000000 | bytes 2850816 | tf_op jit(solution)/shard_map/pallas_call | solution.py:422
  31.2 0.0 copy-start.3
  31.2 0.0 copy-start.4
  31.2 4.8 %shard_map.229 = (bf16[192,768]{1,0:T(8,128)(2,1)}, f32[192,768]{1,0:T(8,128)S(1)}) custom-call(bf16[272,768]{1,0:T(8,128)(2,1)S(1)} %collective-permute-done.3.got_ref, bf16[272,768]{1,0:T(8,128)(2,1)S(1)} %collective-permute-done.4.swap_ref, bf16[256,768]{1,0:T(8,128)(2,1)S(1)} %get-tuple-element.59.grad_ref, f32[6,128]{1,0:T(8,128)S(1)} %bitcast.35, ...), custom_call_target="tpu_custom_call" | custom-call | flops 5000000000 | bytes 4874496 | tf_op jit(solution)/shard_map/pallas_call | solution.py:422
  36.0 0.5 collective-permute-start.5
  36.5 1.5 %collective-permute-start.9 = (bf16[192,768]{1,0:T(8,128)(2,1)}, bf16[192,768]{1,0:T(8,128)(2,1)S(1)}, u32[]{:S(2)}, u32[]{:S(2)}) collective-permute-start(bf16[192,768]{1,0:T(8,128)(2,1)} %get-tuple-element.83), channel_id=1, source_target_pairs={{0,4},{4,0},{8,12},{12,8},{16,20},{20,16},{24,28},{28,24},{1,5},{5... | collective-permute-start | bytes 884744 | tf_op jit(solution)/shard_map/ppermute | solution.py:434
  38.0 0.0 collective-permute-done.1.got_ref
  38.0 0.0 copy-done.3
  38.0 0.0 copy-done.4
  38.1 0.3 shard_map.224.own_ref
  38.4 0.1 collective-permute-start.2
  38.5 4.2 %all-to-all-start = ((f32[32,8,96]{2,1,0:T(8,128)}), f32[32,8,96]{2,1,0:T(8,128)S(1)}, u32[]{:S(2)}, u32[]{:S(2)}) async-start(f32[32,8,96]{2,1,0:T(8,128)} %bitcast.11), calls=%async_computation | async-start | bytes 262144 | tf_op jit(solution)/shard_map/all_to_all | solution.py:508
  42.7 0.0 collective-permute-done.7
  42.7 0.1 shard_map.233
  42.7 0.0 copy-start
  42.7 2.7 %collective-permute-start.8 = (bf16[1,96,768]{2,1,0:T(8,128)(2,1)S(1)}, bf16[1,96,768]{2,1,0:T(8,128)(2,1)S(1)}, u32[]{:S(2)}, u32[]{:S(2)}) collective-permute-start(bf16[1,96,768]{2,1,0:T(8,128)(2,1)S(1)} %get-tuple-element.80), channel_id=1, source_target_pairs={{0,16},{4,20},{8,24},{12,28},{16,0},{20,4},{24,8},{28,12},{1,17},{... | collective-permute-start | bytes 442376 | tf_op jit(solution)/shard_map/ppermute | solution.py:434
  45.5 0.7 %collective-permute-done.5 = bf16[192,768]{1,0:T(8,128)(2,1)} collective-permute-done((bf16[192,768]{1,0:T(8,128)(2,1)}, bf16[192,768]{1,0:T(8,128)(2,1)}, u32[]{:S(2)}, u32[]{:S(2)}) %collective-permute-start.5) | collective-permute-done | bytes 294944 | tf_op jit(solution)/shard_map/ppermute | solution.py:434
  46.2 1.0 %shard_map.230 = (bf16[1,96,768]{2,1,0:T(8,128)(2,1)S(1)}, f32[1,96,768]{2,1,0:T(8,128)S(1)}) custom-call(f32[2,96,768]{2,1,0:T(8,128)S(1)} %bitcast.20, bf16[2,96,768]{2,1,0:T(8,128)(2,1)} %bitcast.10.got_ref), custom_call_target="tpu_custom_call" | custom-call | flops 1000000 | bytes 1327104 | tf_op jit(solution)/shard_map/pallas_call | solution.py:422
  47.2 2.8 %collective-permute-start.6 = (bf16[1,96,768]{2,1,0:T(8,128)(2,1)S(1)}, bf16[1,96,768]{2,1,0:T(8,128)(2,1)S(1)}, u32[]{:S(2)}, u32[]{:S(2)}) collective-permute-start(bf16[1,96,768]{2,1,0:T(8,128)(2,1)S(1)} %get-tuple-element.72), channel_id=1, source_target_pairs={{0,16},{4,20},{8,24},{12,28},{16,0},{20,4},{24,8},{28,12},{1,17},{... | collective-permute-start | bytes 442376 | tf_op jit(solution)/shard_map/ppermute | solution.py:434
  50.0 2.6 %collective-permute-done.9 = bf16[192,768]{1,0:T(8,128)(2,1)S(1)} collective-permute-done((bf16[192,768]{1,0:T(8,128)(2,1)}, bf16[192,768]{1,0:T(8,128)(2,1)S(1)}, u32[]{:S(2)}, u32[]{:S(2)}) %collective-permute-start.9) | collective-permute-done | bytes 294944 | tf_op jit(solution)/shard_map/ppermute | solution.py:434
  52.6 0.0 copy-done
  52.6 2.5 %collective-permute-start.10 = (bf16[1,96,768]{2,1,0:T(8,128)(2,1)S(1)}, bf16[1,96,768]{2,1,0:T(8,128)(2,1)S(1)}, u32[]{:S(2)}, u32[]{:S(2)}) collective-permute-start(bf16[1,96,768]{2,1,0:T(8,128)(2,1)S(1)} %get-tuple-element.85), channel_id=1, source_target_pairs={{0,16},{4,20},{8,24},{12,28},{16,0},{20,4},{24,8},{28,12},{1,17},{... | collective-permute-start | bytes 442376 | tf_op jit(solution)/shard_map/ppermute | solution.py:434
  55.1 2.5 %all-to-all-done.tile_ref = f32[32,8,96]{2,1,0:T(8,128)S(1)} async-done(((f32[32,8,96]{2,1,0:T(8,128)}), f32[32,8,96]{2,1,0:T(8,128)S(1)}, u32[]{:S(2)}, u32[]{:S(2)}) %all-to-all-start) | async-done | bytes 98336 | tf_op jit(solution)/shard_map/all_to_all | solution.py:508
  57.7 0.7 shard_map.232
  58.3 0.0 collective-permute-done.2.got_ref
  58.4 1.0 %shard_map.225 = (bf16[256,768]{1,0:T(8,128)(2,1)}, bf16[256,768]{1,0:T(8,128)(2,1)}) custom-call(bf16[256,768]{1,0:T(8,128)(2,1)S(1)} %shard_map.224.own_ref, bf16[256,768]{1,0:T(8,128)(2,1)S(1)} %collective-permute-done.2.got_ref), custom_call_target="tpu_custom_call" | custom-call | bytes 1572864 | tf_op jit(solution)/shard_map/pallas_call | solution.py:422
  59.3 3.1 %collective-permute-done.8.got_ref = bf16[1,96,768]{2,1,0:T(8,128)(2,1)S(1)} collective-permute-done((bf16[1,96,768]{2,1,0:T(8,128)(2,1)S(1)}, bf16[1,96,768]{2,1,0:T(8,128)(2,1)S(1)}, u32[]{:S(2)}, u32[]{:S(2)}) %collective-permute-start.8) | collective-permute-done | bytes 147488 | tf_op jit(solution)/shard_map/ppermute | solution.py:434
  62.4 0.0 copy-start.1
  62.4 1.0 %copy-done.1 = f32[1,96,768]{2,1,0:T(8,128)S(1)} copy-done((f32[1,96,768]{2,1,0:T(8,128)S(1)}, f32[1,96,768]{2,1,0:T(8,128)}, u32[]{:S(2)}) %copy-start.1) | copy-done | bytes 294936
  63.4 0.7 %shard_map.234 = f32[96,768]{1,0:T(8,128)} custom-call(f32[1,96,768]{2,1,0:T(8,128)S(1)} %copy-done.1, bf16[1,96,768]{2,1,0:T(8,128)(2,1)S(1)} %collective-permute-done.8.got_ref), custom_call_target="tpu_custom_call" | custom-call | bytes 737280 | tf_op jit(solution)/shard_map/pallas_call | solution.py:422
  64.1 1.5 %collective-permute-done.6.got_ref = bf16[1,96,768]{2,1,0:T(8,128)(2,1)S(1)} collective-permute-done((bf16[1,96,768]{2,1,0:T(8,128)(2,1)S(1)}, bf16[1,96,768]{2,1,0:T(8,128)(2,1)S(1)}, u32[]{:S(2)}, u32[]{:S(2)}) %collective-permute-start.6) | collective-permute-done | bytes 147488 | tf_op jit(solution)/shard_map/ppermute | solution.py:434
  65.6 0.8 %shard_map.231 = (f32[96,576]{1,0:T(8,128)}, f32[192,96]{1,0:T(8,128)}) custom-call(f32[1,96,768]{2,1,0:T(8,128)S(1)} %get-tuple-element.71.keep_ref, bf16[1,96,768]{2,1,0:T(8,128)(2,1)S(1)} %collective-permute-done.6.got_ref), custom_call_target="tpu_custom_call" | custom-call | bytes 737280 | tf_op jit(solution)/shard_map/pallas_call | solution.py:422
  66.4 1.8 %collective-permute-done.10.got_ref = bf16[1,96,768]{2,1,0:T(8,128)(2,1)S(1)} collective-permute-done((bf16[1,96,768]{2,1,0:T(8,128)(2,1)S(1)}, bf16[1,96,768]{2,1,0:T(8,128)(2,1)S(1)}, u32[]{:S(2)}, u32[]{:S(2)}) %collective-permute-start.10) | collective-permute-done | bytes 147488 | tf_op jit(solution)/shard_map/ppermute | solution.py:434
  68.2 0.7 %shard_map.236 = f32[96,768]{1,0:T(8,128)} custom-call(f32[1,96,768]{2,1,0:T(8,128)S(1)} %get-tuple-element.84.keep_ref, bf16[1,96,768]{2,1,0:T(8,128)(2,1)S(1)} %collective-permute-done.10.got_ref), custom_call_target="tpu_custom_call" | custom-call | bytes 737280 | tf_op jit(solution)/shard_map/pallas_call | solution.py:422
  (1 shorter events, 0.0 us)
Async XLA Ops:
  0.6 13.9 %copy-start.2 = (s32[256]{0:T(256)S(1)}, s32[256]{0:T(256)}, u32[]{:S(2)}) copy-start(s32[256]{0:T(256)} %param.16) | copy-start | bytes 3076
  0.7 13.9 %copy-start.10 = (f32[3,192]{1,0:T(4,128)S(1)}, f32[3,192]{1,0:T(4,128)}, u32[]{:S(2)}) copy-start(f32[3,192]{1,0:T(4,128)} %offsets_ref.3) | copy-start | bytes 6916
  0.7 13.9 %copy-start.7 = (f32[768]{0:T(1024)S(1)}, f32[768]{0:T(1024)}, u32[]{:S(2)}) copy-start(f32[768]{0:T(1024)} %param.26) | copy-start | bytes 9220
  0.7 13.9 %copy-start.6 = (f32[768]{0:T(1024)S(1)}, f32[768]{0:T(1024)}, u32[]{:S(2)}) copy-start(f32[768]{0:T(1024)} %param.20) | copy-start | bytes 9220
  0.7 13.9 %copy-start.5 = (f32[768]{0:T(1024)S(1)}, f32[768]{0:T(1024)}, u32[]{:S(2)}) copy-start(f32[768]{0:T(1024)} %param.19) | copy-start | bytes 9220
  0.7 13.9 %copy-start.9 = (f32[768]{0:T(1024)S(1)}, f32[768]{0:T(1024)}, u32[]{:S(2)}) copy-start(f32[768]{0:T(1024)} %param.18) | copy-start | bytes 9220
  0.7 13.9 %copy-start.8 = (f32[768]{0:T(1024)S(1)}, f32[768]{0:T(1024)}, u32[]{:S(2)}) copy-start(f32[768]{0:T(1024)} %param.17) | copy-start | bytes 9220
  1.8 12.8 %collective-permute-start.3 = (bf16[272,768]{1,0:T(8,128)(2,1)S(1)}, bf16[272,768]{1,0:T(8,128)(2,1)S(1)}, u32[]{:S(2)}, u32[]{:S(2)}) collective-permute-start(bf16[272,768]{1,0:T(8,128)(2,1)S(1)} %shard_map.226), channel_id=1, source_target_pairs={{0,8},{4,12},{8,0},{12,4},{16,24},{20,28},{24,16},{28,20},{1,9},{5... | collective-permute-start | bytes 1253384 | tf_op jit(solution)/shard_map/ppermute | solution.py:434
  14.6 11.8 %collective-permute-start.4 = (bf16[272,768]{1,0:T(8,128)(2,1)S(1)}, bf16[272,768]{1,0:T(8,128)(2,1)S(1)}, u32[]{:S(2)}, u32[]{:S(2)}) collective-permute-start(bf16[272,768]{1,0:T(8,128)(2,1)S(1)} %collective-permute-done.3.got_ref), channel_id=1, source_target_pairs={{0,1},{1,0},{2,3},{3,2},{4,5},{5,4},{6,7},{7,6},{8,9},{9,8},{10,11... | collective-permute-start | bytes 1253384 | tf_op jit(solution)/shard_map/ppermute | solution.py:434
  22.6 1.9 %collective-permute-start = (bf16[256,768]{1,0:T(8,128)(2,1)S(1)}, bf16[256,768]{1,0:T(8,128)(2,1)S(1)}, u32[]{:S(2)}, u32[]{:S(2)}) collective-permute-start(bf16[256,768]{1,0:T(8,128)(2,1)S(1)} %get-tuple-element.50), channel_id=1, source_target_pairs={{0,1},{1,0},{2,3},{3,2},{4,5},{5,4},{6,7},{7,6},{8,9},{9,8},{10,11... | collective-permute-start | bytes 1179656 | tf_op jit(solution)/shard_map/ppermute | solution.py:434
  24.6 13.4 %collective-permute-start.1 = (bf16[256,768]{1,0:T(8,128)(2,1)S(1)}, bf16[256,768]{1,0:T(8,128)(2,1)S(1)}, u32[]{:S(2)}, u32[]{:S(2)}) collective-permute-start(bf16[256,768]{1,0:T(8,128)(2,1)S(1)} %shard_map.223.part_ref), channel_id=1, source_target_pairs={{0,2},{1,3},{2,0},{3,1},{4,6},{5,7},{6,4},{7,5},{8,10},{9,11},{10,... | collective-permute-start | bytes 1179656 | tf_op jit(solution)/shard_map/ppermute | solution.py:434
  28.5 14.2 %collective-permute-start.7 = (bf16[192,768]{1,0:T(8,128)(2,1)}, bf16[192,768]{1,0:T(8,128)(2,1)S(1)}, u32[]{:S(2)}, u32[]{:S(2)}) collective-permute-start(bf16[192,768]{1,0:T(8,128)(2,1)} %get-tuple-element.78), channel_id=1, source_target_pairs={{0,4},{4,0},{8,12},{12,8},{16,20},{20,16},{24,28},{28,24},{1,5},{5... | collective-permute-start | bytes 884744 | tf_op jit(solution)/shard_map/ppermute | solution.py:434
  31.2 6.8 %copy-start.3 = (f32[768]{0:T(1024)S(1)}, f32[768]{0:T(1024)}, u32[]{:S(2)}) copy-start(f32[768]{0:T(1024)} %param.24) | copy-start | bytes 9220
  31.2 6.8 %copy-start.4 = (f32[768]{0:T(1024)S(1)}, f32[768]{0:T(1024)}, u32[]{:S(2)}) copy-start(f32[768]{0:T(1024)} %param.28) | copy-start | bytes 9220
  36.0 10.2 %collective-permute-start.5 = (bf16[192,768]{1,0:T(8,128)(2,1)}, bf16[192,768]{1,0:T(8,128)(2,1)}, u32[]{:S(2)}, u32[]{:S(2)}) collective-permute-start(bf16[192,768]{1,0:T(8,128)(2,1)} %get-tuple-element.70), channel_id=1, source_target_pairs={{0,4},{4,0},{8,12},{12,8},{16,20},{20,16},{24,28},{28,24},{1,5},{5... | collective-permute-start | bytes 884744 | tf_op jit(solution)/shard_map/ppermute | solution.py:434
  36.5 16.1 %collective-permute-start.9 = (bf16[192,768]{1,0:T(8,128)(2,1)}, bf16[192,768]{1,0:T(8,128)(2,1)S(1)}, u32[]{:S(2)}, u32[]{:S(2)}) collective-permute-start(bf16[192,768]{1,0:T(8,128)(2,1)} %get-tuple-element.83), channel_id=1, source_target_pairs={{0,4},{4,0},{8,12},{12,8},{16,20},{20,16},{24,28},{28,24},{1,5},{5... | collective-permute-start | bytes 884744 | tf_op jit(solution)/shard_map/ppermute | solution.py:434
  38.4 19.9 %collective-permute-start.2 = (bf16[256,768]{1,0:T(8,128)(2,1)S(1)}, bf16[256,768]{1,0:T(8,128)(2,1)S(1)}, u32[]{:S(2)}, u32[]{:S(2)}) collective-permute-start(bf16[256,768]{1,0:T(8,128)(2,1)S(1)} %shard_map.224.own_ref), channel_id=1, source_target_pairs={{0,1},{1,0},{2,3},{3,2},{4,5},{5,4},{6,7},{7,6},{8,9},{9,8},{10,11... | collective-permute-start | bytes 1179656 | tf_op jit(solution)/shard_map/ppermute | solution.py:434
  38.5 19.2 %all-to-all-start = ((f32[32,8,96]{2,1,0:T(8,128)}), f32[32,8,96]{2,1,0:T(8,128)S(1)}, u32[]{:S(2)}, u32[]{:S(2)}) async-start(f32[32,8,96]{2,1,0:T(8,128)} %bitcast.11), calls=%async_computation | async-start | bytes 262144 | tf_op jit(solution)/shard_map/all_to_all | solution.py:508
  42.7 9.9 %copy-start = (f32[1,96,768]{2,1,0:T(8,128)}, f32[1,96,768]{2,1,0:T(8,128)S(1)}, u32[]{:S(2)}) copy-start(f32[1,96,768]{2,1,0:T(8,128)S(1)} %get-tuple-element.79.keep_ref) | copy-start | bytes 884740
  42.7 19.7 %collective-permute-start.8 = (bf16[1,96,768]{2,1,0:T(8,128)(2,1)S(1)}, bf16[1,96,768]{2,1,0:T(8,128)(2,1)S(1)}, u32[]{:S(2)}, u32[]{:S(2)}) collective-permute-start(bf16[1,96,768]{2,1,0:T(8,128)(2,1)S(1)} %get-tuple-element.80), channel_id=1, source_target_pairs={{0,16},{4,20},{8,24},{12,28},{16,0},{20,4},{24,8},{28,12},{1,17},{... | collective-permute-start | bytes 442376 | tf_op jit(solution)/shard_map/ppermute | solution.py:434
  47.2 18.3 %collective-permute-start.6 = (bf16[1,96,768]{2,1,0:T(8,128)(2,1)S(1)}, bf16[1,96,768]{2,1,0:T(8,128)(2,1)S(1)}, u32[]{:S(2)}, u32[]{:S(2)}) collective-permute-start(bf16[1,96,768]{2,1,0:T(8,128)(2,1)S(1)} %get-tuple-element.72), channel_id=1, source_target_pairs={{0,16},{4,20},{8,24},{12,28},{16,0},{20,4},{24,8},{28,12},{1,17},{... | collective-permute-start | bytes 442376 | tf_op jit(solution)/shard_map/ppermute | solution.py:434
  52.6 15.5 %collective-permute-start.10 = (bf16[1,96,768]{2,1,0:T(8,128)(2,1)S(1)}, bf16[1,96,768]{2,1,0:T(8,128)(2,1)S(1)}, u32[]{:S(2)}, u32[]{:S(2)}) collective-permute-start(bf16[1,96,768]{2,1,0:T(8,128)(2,1)S(1)} %get-tuple-element.85), channel_id=1, source_target_pairs={{0,16},{4,20},{8,24},{12,28},{16,0},{20,4},{24,8},{28,12},{1,17},{... | collective-permute-start | bytes 442376 | tf_op jit(solution)/shard_map/ppermute | solution.py:434
  62.4 1.0 %copy-start.1 = (f32[1,96,768]{2,1,0:T(8,128)S(1)}, f32[1,96,768]{2,1,0:T(8,128)}, u32[]{:S(2)}) copy-start(f32[1,96,768]{2,1,0:T(8,128)} %copy-done) | copy-start | bytes 884740

commit v4 on v3

--- a/solution.py
+++ b/solution.py
@@ -241,34 +241,37 @@
     block = tile_ref.shape[3]
     third = 3 * size // n_dp
     per_dp = hidden.shape[1] // n_dp
-    tile_ref[...] = jnp.zeros_like(tile_ref)
     for d in range(n_dp):
         lanes = slice(d * block, (d + 1) * block)
+        local = hidden[:, d * per_dp : (d + 1) * per_dp]
+        if per_dp < block:
+            local = jnp.concatenate([local, jnp.zeros((1, block - per_dp), F32)], axis=1)
+        cut = [shares[:, h * 3 * size + d * third : h * 3 * size + (d + 1) * third] for h in range(heads)]
+        if heads * third < block:
+            cut.append(jnp.zeros((1, block - heads * third), F32))
+        mine = jnp.concatenate([bias[:, lanes], local, jnp.concatenate(cut, axis=1), jnp.zeros((1, block), F32)], axis=0)
         for t in range(n_tensor):
-            tile_ref[d, t, 0:4] = everyone[:, lanes]
-
-        def put(t, d=d, lanes=lanes):
-            tile_ref[d, t, 4:5] = bias[:, lanes]
-            tile_ref[d, t, 5:6, :per_dp] = hidden[:, d * per_dp : (d + 1) * per_dp]
-            for head in range(heads):
-                at = head * 3 * size + d * third
-                tile_ref[d, t, 6:7, head * third : (head + 1) * third] = shares[:, at : at + third]
-
-        put(lax.axis_index("tensor"))
-
-
-def gather_bit():
-    return lax.axis_index("dp") // 2 % 2
-
-
-def first_bit():
-    return lax.axis_index("dp") % 2
+            here = jnp.where(lax.axis_index("tensor") == t, mine, 0.0)
+            tile_ref[d, t] = jnp.concatenate([everyone[:, lanes], here], axis=0).astype(BF16)
+
+
+def bit_of(bit):
+    return lax.axis_index("dp") // bit % 2
 
 
 def core_bit():
     return lax.axis_index("tensor") % 2
 
 
+def other_bits(dests, first):
+    return [1 << i for i in range(12) if 1 << i < dests and 1 << i not in (2, first)]
+
+
+def dest_order(dests, first):
+    bits = other_bits(dests, first)
+    return [sum(bit for i, bit in enumerate(bits) if rest >> i & 1) for rest in range(1 << len(bits))]
+
+
 def put_left(left, ref):
     ref[...] = left.T if ref.shape[0] != left.shape[0] else left
 
@@ -277,24 +280,28 @@
     return (width, n) if width // dests % 16 == 0 and width != n else (n, width)
 
 
-def spread_rows(refs, dests):
+def spread_rows(refs, dests, first):
     _, width = sorted(refs[0].shape)
     block = width // dests
+    numbers = dest_order(dests, first)
     if refs[0].shape[0] == width:
         rows = []
         for flip in (1, 0):
-            first = first_bit() if flip == 0 else 1 - first_bit()
-            for rest in range(dests // 4):
-                start = pl.multiple_of((4 * rest + 2 * gather_bit() + first) * block, 16)
+            side = bit_of(first) if flip == 0 else 1 - bit_of(first)
+            for number in numbers:
+                start = pl.multiple_of((number + 2 * bit_of(2) + first * side) * block, 16)
                 rows.append(jnp.concatenate([ref[pl.ds(start, block), :] for ref in refs], axis=1))
         return jnp.concatenate(rows, axis=0)
-    half = dests // 4 * block
+    half = len(numbers) * block
     row = lax.broadcasted_iota(jnp.int32, (2 * half, width), 0)
     col = lax.broadcasted_iota(jnp.int32, (2 * half, width), 1)
     kept = row >= half
     row = jnp.where(kept, row - half, row)
-    first = jnp.where(kept, first_bit(), 1 - first_bit())
-    want = row + (row // block) * 3 * block + (2 * gather_bit() + first) * block
+    side = jnp.where(kept, bit_of(first), 1 - bit_of(first))
+    want = row + (2 * bit_of(2) + first * side) * block
+    for place, number in enumerate(numbers):
+        inside = (row >= place * block) & (row < (place + 1) * block)
+        want = want + jnp.where(inside, (number - place) * block, 0)
     left = jnp.concatenate([ref[...] for ref in refs], axis=0)
     return dot_t(jnp.where(want == col, 1.0, 0.0).astype(BF16), left).astype(BF16)
 
@@ -329,13 +336,17 @@
     active, grad = ffn_block(normed, grad_out, expand_ref[...], flat(thr_ref), contract_ref[...])
     active_ref[...] = active
     right = jnp.concatenate([back_ref[...], grad.astype(BF16)], axis=0)
-    put_halves(dot(spread_rows((two_ref, left_ref), dests), right), send_ref, keep_ref)
-
-
-def contract_kernel(dests, grad_ref, out_ref, own_ref, active_ref, send_ref, keep_ref, left_ref):
+    put_halves(dot(spread_rows((two_ref, left_ref), dests, 1), right), send_ref, keep_ref)
+
+
+def contract_kernel(
+    dests, firsts, grad_ref, out_ref, own_ref, active_ref, send_a_ref, keep_a_ref, send_b_ref, keep_b_ref, left_ref
+):
     put_left(grad_ref[...], left_ref)
     right = jnp.concatenate([own_ref[...], active_ref[...]], axis=0)
-    put_halves(dot(spread_rows((out_ref, left_ref), dests), right), send_ref, keep_ref)
+    split = send_a_ref.shape[1]
+    put_halves(dot(spread_rows((out_ref, left_ref), dests, firsts[0]), right[:, :split]), send_a_ref, keep_a_ref)
+    put_halves(dot(spread_rows((out_ref, left_ref), dests, firsts[1]), right[:, split:]), send_b_ref, keep_b_ref)
 
 
 def attention_kernel(
@@ -357,22 +368,26 @@
     )
     inlet_back = inlet_full.astype(BF16)[:, : inlet_ref.shape[0]]
     right = jnp.concatenate([inlet_back_ref[...], inlet_back], axis=0)
-    first = dot(spread_rows((one_ref, left_ref), dests), right)
+    first = dot(spread_rows((one_ref, left_ref), dests, 1), right)
     right = jnp.concatenate([attended_ref[...], attended], axis=0)
-    second = dot(spread_rows((out_ref, near_ref), dests), right)
+    second = dot(spread_rows((out_ref, near_ref), dests, 1), right)
     put_halves(jnp.concatenate([first, second], axis=1), send_ref, keep_ref)
 
 
 def halve_kernel(step, keep_ref, got_ref, send_ref, left_ref):
-    bit = jnp.where((lax.axis_index("dp") & step) != 0, 1, 0)
+    bit = bit_of(step)
     for i in range(send_ref.shape[0]):
         away, stay = 2 * i + 1 - bit, 2 * i + bit
         send_ref[i] = (keep_ref[away] + got_ref[away].astype(F32)).astype(BF16)
         left_ref[i] = keep_ref[stay] + got_ref[stay].astype(F32)
 
 
-def add_kernel(keep_ref, got_ref, out_ref):
-    out_ref[...] = keep_ref[0] + got_ref[0].astype(F32)
+def add_kernel(*refs):
+    out_ref, at = refs[-1], 0
+    for keep_ref, got_ref in zip(refs[:-1:2], refs[1:-1:2]):
+        columns = keep_ref.shape[2]
+        out_ref[:, at : at + columns] = keep_ref[0] + got_ref[0].astype(F32)
+        at += columns
 
 
 def split_kernel(keep_ref, got_ref, inlet_ref, outlet_ref):
@@ -402,9 +417,9 @@
 
 
 def small_kernel(heads, third, tile_ref, norms_ref, bias_ref, thr_ref, offsets_ref):
-    total = tile_ref[0]
+    total = tile_ref[0].astype(F32)
     for i in range(1, tile_ref.shape[0]):
-        total = total + tile_ref[i]
+        total = total + tile_ref[i].astype(F32)
     norms_ref[...] = total[0:4]
     bias_ref[...] = total[4:5]
     thr_ref[...] = total[5:6, : thr_ref.shape[1]]
@@ -460,7 +475,7 @@
         functools.partial(own_kernel, heads, size, n_dp, n_tensor),
         [(tokens.shape, BF16), (cotangent.shape, BF16), ((columns, width), BF16), (outlet.shape, BF16), (expand.shape, BF16),
          (contract.shape, BF16), ((n, width), BF16), ((n, width), F32), ((n, units), BF16), ((n, units), BF16),
-         ((n, mine), BF16), ((n, columns), BF16), ((n_dp, n_tensor, 8, block), F32),
+         ((n, mine), BF16), ((n, columns), BF16), ((n_dp, n_tensor, 8, block), BF16),
          (turned, BF16), (turned, BF16), (turned, BF16)],
         [tokens, cotangent, seg, gain_one, shift_one, gain_two, shift_two, offsets, thr, inlet.T, outlet, expand, contract],
         flops=6e9, scratch=[pltpu.SemaphoreType.DMA((6,))], places="aavvvvvvvaaaa",
@@ -475,13 +490,17 @@
         flops=3e9, scratch=left,
     )
     expand_got = swap(expand_send, "dp", n_dp, 1)
-    contract_send, contract_keep, near_t = call(
-        functools.partial(contract_kernel, n_dp),
-        [((half, units), BF16), ((half, units), F32), (turned, BF16)],
+    far_first = 4 if n_dp > 4 else 1
+    part_units = units // 2
+    early_send, early_keep, late_send, late_keep, near_t = call(
+        functools.partial(contract_kernel, n_dp, (far_first, 1)),
+        [((half, part_units), BF16), ((half, part_units), F32), ((half, units - part_units), BF16),
+         ((half, units - part_units), F32), (turned, BF16)],
         [grad_near, out_t, active, active_near],
         flops=1e9,
     )
-    contract_got = swap(contract_send, "dp", n_dp, 1)
+    early_got = swap(early_send, "dp", n_dp, far_first)
+    late_got = swap(late_send, "dp", n_dp, 1)
     tail_send, tail_keep = call(
         functools.partial(attention_kernel, heads, size, n_dp),
         [((half, columns + mine), BF16), ((half, columns + mine), F32)],
@@ -512,27 +531,27 @@
         [((4, block), F32), ((1, block), F32), ((1, units // n_dp), F32), ((heads, third), F32)], [tile], results="dddd",
     )
 
-    def reduce(kept, arrived):
+    def reduce(kept, arrived, first):
         columns_here = kept.shape[1]
         kept = kept.reshape(-1, block, columns_here)
         arrived = arrived.reshape(-1, block, columns_here)
-        bit = 4
-        while bit < n_dp:
+        for bit in other_bits(n_dp, first):
             rest = kept.shape[0] // 2
             shape = (rest, block, columns_here)
             away, kept = call(
-                functools.partial(halve_kernel, bit), [(shape, BF16), (shape, F32)], [kept, arrived],
-                flops=1e6,
+                functools.partial(halve_kernel, bit), [(shape, BF16), (shape, F32)], [kept, arrived], flops=1e6
             )
             arrived = swap(away, "dp", n_dp, bit)
-            bit *= 2
-        return kept, arrived
-
-    expand_grad, = call(add_kernel, [((block, units), F32)], reduce(expand_keep, expand_got), results="d")
-    contract_grad, = call(add_kernel, [((block, units), F32)], reduce(contract_keep, contract_got), results="d")
+        return [kept, arrived]
+
+    expand_grad, = call(add_kernel, [((block, units), F32)], reduce(expand_keep, expand_got, 1), results="d")
+    contract_grad, = call(
+        add_kernel, [((block, units), F32)],
+        reduce(early_keep, early_got, far_first) + reduce(late_keep, late_got, 1), results="d",
+    )
     inlet_grad, outlet_grad = call(
         split_kernel, [((block, columns), F32), ((mine, block), F32)],
-        reduce(tail_keep, tail_got), results="dd",
+        reduce(tail_keep, tail_got, 1), results="dd",
     )
     return (
         mixed, input_grad, inlet_grad, offsets_grad, outlet_grad, expand_grad, thr_grad, contract_grad.T,

time: 69.2 us -> 69 us (level)
  waiting for transfers between devices: 23.1 us -> 28.5 us
  Pallas kernels: 22.7 us -> 19.8 us
  starting transfers between devices: 21.2 us -> 19.7 us
  local copies, waits for them, and re-layouts: 1 us -> 0.04 us
    all_to_all x1, waiting for transfers between devices: 2.52 us -> 9.18 us  [step(): lax.all_to_all(tile.reshape(n_dp * n_tensor, 8, block), ('dp', 'tensor'),...]
    pallas_call x15 -> x16, Pallas kernels: 22.7 us -> 19.8 us  [call(): pl.pallas_call(kernel, out_shape=[jax.ShapeDtypeStruct(shape, dtype) for...]
    ppermute x11 -> x13, waiting for transfers between devices: 20.6 us -> 19.3 us  [swap(): return lax.ppermute(value, axis, [(i, i ^ bit) for i in range(count)])]
    all_to_all x1, starting transfers between devices: 4.17 us -> 2.84 us  [step(): lax.all_to_all(tile.reshape(n_dp * n_tensor, 8, block), ('dp', 'tensor'),...]
    unnamed x22 -> x18, local copies, waits for them, and re-layouts: 1 us -> 0.04 us
    ppermute x11 -> x13, starting transfers between devices: 17 us -> 16.8 us  [swap(): return lax.ppermute(value, axis, [(i, i ^ bit) for i in range(count)])]
  transfers between devices with their start and end apart: 12 -> 14, of which waited for: 8 -> 6; matrix products, arithmetic and copies ran while one was open for 0% -> 0% of each run, Pallas kernels for 30% -> 26%
where the time goes in v4:
time: 69 us; the launch traced here: 68.8 us
  waiting for transfers between devices  28.5 us (41%)
  Pallas kernels  19.8 us (29%)
  starting transfers between devices  19.7 us (29%)
  between operations  0.86 us (1%)
    pallas_call x16, Pallas kernels, call(): pl.pallas_call(kernel, out_shape=[jax.ShapeDtypeStruct(shape, dtype) for...  19.8 us
    ppermute x13, waiting for transfers between devices, swap(): return lax.ppermute(value, axis, [(i, i ^ bit) for i in range(count)])  19.3 us
    ppermute x13, starting transfers between devices, swap(): return lax.ppermute(value, axis, [(i, i ^ bit) for i in range(count)])  16.8 us
    all_to_all x1, waiting for transfers between devices, step(): lax.all_to_all(tile.reshape(n_dp * n_tensor, 8, block), ('dp', 'tensor'),...  9.18 us
    all_to_all x1, starting transfers between devices, step(): lax.all_to_all(tile.reshape(n_dp * n_tensor, 8, block), ('dp', 'tensor'),...  2.84 us
  transfers between devices with their start and end apart: 14, of which 6 were waited for; matrix products, arithmetic and copies ran while one was open for 0% of the time, Pallas kernels for 26%

profile of v4, /device:TPU:0, one launch (start us, length us, event | category | flops | bytes accessed | tf_op | source)
XLA Modules:
  0.0 68.8 jit_solution(8408396511118105814)
XLA Ops:
  0.6 0.0 copy-start
  0.7 0.0 copy-start.8
  0.7 0.0 copy-start.5
  0.7 0.0 copy-start.4
  0.7 0.0 copy-start.3
  0.7 0.0 copy-start.7
  0.7 0.0 copy-start.6
  0.7 1.1 %shard_map.226 = bf16[272,768]{1,0:T(8,128)(2,1)S(1)} custom-call(bf16[256,768]{1,0:T(8,128)(2,1)} %tok_ref.1, bf16[256,768]{1,0:T(8,128)(2,1)} %cot_ref.1, s32[2,128]{1,0:T(2,128)} %bitcast.28), custom_call_target="tpu_custom_call" | custom-call | bytes 1205248 | tf_op jit(solution)/shard_map/pallas_call | solution.py:437
  1.8 3.1 %collective-permute-start.3 = (bf16[272,768]{1,0:T(8,128)(2,1)S(1)}, bf16[272,768]{1,0:T(8,128)(2,1)S(1)}, u32[]{:S(2)}, u32[]{:S(2)}) collective-permute-start(bf16[272,768]{1,0:T(8,128)(2,1)S(1)} %shard_map.226), channel_id=1, source_target_pairs={{0,8},{4,12},{8,0},{12,4},{16,24},{20,28},{24,16},{28,20},{1,9},{5... | collective-permute-start | bytes 1253384 | tf_op jit(solution)/shard_map/ppermute | solution.py:449
  4.9 9.6 %collective-permute-done.3.got_ref = bf16[272,768]{1,0:T(8,128)(2,1)S(1)} collective-permute-done((bf16[272,768]{1,0:T(8,128)(2,1)S(1)}, bf16[272,768]{1,0:T(8,128)(2,1)S(1)}, u32[]{:S(2)}, u32[]{:S(2)}) %collective-permute-start.3) | collective-permute-done | bytes 417824 | tf_op jit(solution)/shard_map/ppermute | solution.py:449
  14.6 0.0 collective-permute-start.4
  14.6 0.0 copy-done
  14.6 0.0 copy-done.8
  14.6 0.0 copy-done.5
  14.6 0.0 copy-done.4
  14.6 0.0 copy-done.3
  14.6 0.0 copy-done.7
  14.6 0.0 copy-done.6
  14.6 8.0 %shard_map.222 = (bf16[256,768]{1,0:T(8,128)(2,1)S(1)}, bf16[256,768]{1,0:T(8,128)(2,1)S(1)}, bf16[576,768]{1,0:T(8,128)(2,1)S(1)}, bf16[192,768]{1,0:T(8,128)(2...) custom-call(bf16[256,768]{1,0:T(8,128)(2,1)} %tok_ref.1, ...), custom_call_target="tpu_custom_call" | custom-call | flops 6000000000 | bytes 12257536 | tf_op jit(solution)/shard_map/pallas_call | solution.py:437
  22.6 0.6 collective-permute-start
  23.2 1.3 %collective-permute-done.got_ref = bf16[256,768]{1,0:T(8,128)(2,1)S(1)} collective-permute-done((bf16[256,768]{1,0:T(8,128)(2,1)S(1)}, bf16[256,768]{1,0:T(8,128)(2,1)S(1)}, u32[]{:S(2)}, u32[]{:S(2)}) %collective-permute-start) | collective-permute-done | bytes 393248 | tf_op jit(solution)/shard_map/ppermute | solution.py:449
  24.5 0.1 shard_map.223.part_ref
  24.6 1.7 %collective-permute-start.1 = (bf16[256,768]{1,0:T(8,128)(2,1)S(1)}, bf16[256,768]{1,0:T(8,128)(2,1)S(1)}, u32[]{:S(2)}, u32[]{:S(2)}) collective-permute-start(bf16[256,768]{1,0:T(8,128)(2,1)S(1)} %shard_map.223.part_ref), channel_id=1, source_target_pairs={{0,2},{1,3},{2,0},{3,1},{4,6},{5,7},{6,4},{7,5},{8,10},{9,11},{10,... | collective-permute-start | bytes 1179656 | tf_op jit(solution)/shard_map/ppermute | solution.py:449
  26.4 0.0 collective-permute-done.4.swap_ref
  26.4 1.4 %shard_map.227 = (bf16[192,768]{1,0:T(8,128)(2,1)S(1)}, f32[192,768]{1,0:T(8,128)S(1)}, bf16[256,768]{1,0:T(8,128)(2,1)S(1)}, bf16[256,768]{1,0:T(8,128)(2,1)S(1)}) custom-call(bf16[272,768]{1,0:T(8,128)(2,1)S(1)} %collective-permute-done.3.got_ref, bf16[272,768]{1,0:T(8,128)(2,1)S(1)} %collective-permute-done.4.swap_ref, ...), custom_call_target="tpu_custom_call" | custom-call | flops 3000000000 | bytes 5661696 | tf_op jit(solution)/shard_map/pallas_call | solution.py:437
  27.8 1.6 %collective-permute-start.7 = (bf16[192,768]{1,0:T(8,128)(2,1)S(1)}, bf16[192,768]{1,0:T(8,128)(2,1)S(1)}, u32[]{:S(2)}, u32[]{:S(2)}) collective-permute-start(bf16[192,768]{1,0:T(8,128)(2,1)S(1)} %get-tuple-element.82), channel_id=1, source_target_pairs={{0,4},{4,0},{8,12},{12,8},{16,20},{20,16},{24,28},{28,24},{1,5},{5... | collective-permute-start | bytes 884744 | tf_op jit(solution)/shard_map/ppermute | solution.py:449
  29.4 0.6 shard_map.228
  30.0 0.0 copy-start.1
  30.0 0.0 copy-start.2
  30.0 4.1 %shard_map.229 = (bf16[192,768]{1,0:T(8,128)(2,1)S(1)}, f32[192,768]{1,0:T(8,128)S(1)}) custom-call(bf16[272,768]{1,0:T(8,128)(2,1)S(1)} %collective-permute-done.3.got_ref, bf16[272,768]{1,0:T(8,128)(2,1)S(1)} %collective-permute-done.4.swap_ref, bf16[256,768]{1,0:T(8,128)(2,1)S(1)} %get-tuple-element.63.grad_ref, f32[6,128]{1,0:T(8,128)S(1)} %bitcast.40, ...), custom_call_target="tpu_custom_call" | custom-call | flops 5000000000 | bytes 4874496 | tf_op jit(solution)/shard_map/pallas_call | solution.py:437
  34.2 0.6 collective-permute-start.5
  34.7 1.4 %collective-permute-done.1.got_ref = bf16[256,768]{1,0:T(8,128)(2,1)S(1)} collective-permute-done((bf16[256,768]{1,0:T(8,128)(2,1)S(1)}, bf16[256,768]{1,0:T(8,128)(2,1)S(1)}, u32[]{:S(2)}, u32[]{:S(2)}) %collective-permute-start.1) | collective-permute-done | bytes 393248 | tf_op jit(solution)/shard_map/ppermute | solution.py:449
  36.1 0.0 copy-done.1
  36.1 0.0 copy-done.2
  36.1 0.3 shard_map.224.own_ref
  36.4 0.1 collective-permute-start.2
  36.5 2.8 %collective-permute-start.9 = (bf16[192,384]{1,0:T(8,128)(2,1)S(1)}, bf16[192,384]{1,0:T(8,128)(2,1)S(1)}, u32[]{:S(2)}, u32[]{:S(2)}) collective-permute-start(bf16[192,384]{1,0:T(8,128)(2,1)S(1)} %get-tuple-element.87), channel_id=1, source_target_pairs={{0,16},{4,20},{8,24},{12,28},{16,0},{20,4},{24,8},{28,12},{1,17},{... | collective-permute-start | bytes 442376 | tf_op jit(solution)/shard_map/ppermute | solution.py:449
  39.3 1.5 %collective-permute-start.11 = (bf16[192,384]{1,0:T(8,128)(2,1)S(1)}, bf16[192,384]{1,0:T(8,128)(2,1)S(1)}, u32[]{:S(2)}, u32[]{:S(2)}) collective-permute-start(bf16[192,384]{1,0:T(8,128)(2,1)S(1)} %get-tuple-element.91), channel_id=1, source_target_pairs={{0,4},{4,0},{8,12},{12,8},{16,20},{20,16},{24,28},{28,24},{1,5},{5... | collective-permute-start | bytes 442376 | tf_op jit(solution)/shard_map/ppermute | solution.py:449
  40.9 0.0 collective-permute-done.7
  40.9 0.4 collective-permute-start.8
  41.3 2.8 %collective-permute-done.5 = bf16[192,768]{1,0:T(8,128)(2,1)S(1)} collective-permute-done((bf16[192,768]{1,0:T(8,128)(2,1)S(1)}, bf16[192,768]{1,0:T(8,128)(2,1)S(1)}, u32[]{:S(2)}, u32[]{:S(2)}) %collective-permute-start.5) | collective-permute-done | bytes 294944 | tf_op jit(solution)/shard_map/ppermute | solution.py:449
  44.2 2.7 %collective-permute-start.6 = (bf16[1,96,768]{2,1,0:T(8,128)(2,1)S(1)}, bf16[1,96,768]{2,1,0:T(8,128)(2,1)S(1)}, u32[]{:S(2)}, u32[]{:S(2)}) collective-permute-start(bf16[1,96,768]{2,1,0:T(8,128)(2,1)S(1)} %get-tuple-element.76), channel_id=1, source_target_pairs={{0,16},{4,20},{8,24},{12,28},{16,0},{20,4},{24,8},{28,12},{1,17},{... | collective-permute-start | bytes 442376 | tf_op jit(solution)/shard_map/ppermute | solution.py:449
  46.8 2.8 %all-to-all-start = ((bf16[32,8,96]{2,1,0:T(8,128)(2,1)}), bf16[32,8,96]{2,1,0:T(8,128)(2,1)S(1)}, u32[]{:S(2)}, u32[]{:S(2)}) async-start(bf16[32,8,96]{2,1,0:T(8,128)(2,1)} %bitcast.11), calls=%async_computation | async-start | bytes 131072 | tf_op jit(solution)/shard_map/all_to_all | solution.py:527
  49.7 4.1 %collective-permute-done.9 = bf16[192,384]{1,0:T(8,128)(2,1)S(1)} collective-permute-done((bf16[192,384]{1,0:T(8,128)(2,1)S(1)}, bf16[192,384]{1,0:T(8,128)(2,1)S(1)}, u32[]{:S(2)}, u32[]{:S(2)}) %collective-permute-start.9) | collective-permute-done | bytes 147488 | tf_op jit(solution)/shard_map/ppermute | solution.py:449
  53.8 1.7 %collective-permute-start.10 = (bf16[1,96,384]{2,1,0:T(8,128)(2,1)S(1)}, bf16[1,96,384]{2,1,0:T(8,128)(2,1)S(1)}, u32[]{:S(2)}, u32[]{:S(2)}) collective-permute-start(bf16[1,96,384]{2,1,0:T(8,128)(2,1)S(1)} %get-tuple-element.89), channel_id=1, source_target_pairs={{0,4},{4,0},{8,12},{12,8},{16,20},{20,16},{24,28},{28,24},{1,5},{5... | collective-permute-start | bytes 221192 | tf_op jit(solution)/shard_map/ppermute | solution.py:449
  55.6 0.0 collective-permute-done.11
  55.6 0.1 collective-permute-start.12
  55.7 9.2 %all-to-all-done.tile_ref = bf16[32,8,96]{2,1,0:T(8,128)(2,1)S(1)} async-done(((bf16[32,8,96]{2,1,0:T(8,128)(2,1)}), bf16[32,8,96]{2,1,0:T(8,128)(2,1)S(1)}, u32[]{:S(2)}, u32[]{:S(2)}) %all-to-all-start) | async-done | bytes 49184 | tf_op jit(solution)/shard_map/all_to_all | solution.py:527
  64.9 0.7 shard_map.232
  65.6 0.0 collective-permute-done.10.refs_1_
  65.6 0.0 collective-permute-done.12.refs_3_
  65.6 0.7 %shard_map.237 = f32[96,768]{1,0:T(8,128)} custom-call(f32[1,96,384]{2,1,0:T(8,128)S(1)} %get-tuple-element.88.refs_0_, bf16[1,96,384]{2,1,0:T(8,128)(2,1)S(1)} %collective-permute-done.10.refs_1_, f32[1,96,384]{2,1,0:T(8,128)S(1)} %get-tuple-element.92.refs_2_, bf16[1,96,384]{2,1,0:T(8,128)(2,1)S(1)} %collective-permute-done.12.refs_3_), custom_call_target="tpu_custom_call" | custom-call | bytes 737280 | tf_op jit(solution)/shard_map/pallas_call | solution.py:437
  66.3 0.0 collective-permute-done.2.got_ref
  66.3 1.0 %shard_map.225 = (bf16[256,768]{1,0:T(8,128)(2,1)}, bf16[256,768]{1,0:T(8,128)(2,1)}) custom-call(bf16[256,768]{1,0:T(8,128)(2,1)S(1)} %shard_map.224.own_ref, bf16[256,768]{1,0:T(8,128)(2,1)S(1)} %collective-permute-done.2.got_ref), custom_call_target="tpu_custom_call" | custom-call | bytes 1572864 | tf_op jit(solution)/shard_map/pallas_call | solution.py:437
  67.3 0.0 collective-permute-done.8.refs_1_
  67.3 0.7 %shard_map.234 = f32[96,768]{1,0:T(8,128)} custom-call(f32[1,96,768]{2,1,0:T(8,128)S(1)} %get-tuple-element.83.refs_0_, bf16[1,96,768]{2,1,0:T(8,128)(2,1)S(1)} %collective-permute-done.8.refs_1_), custom_call_target="tpu_custom_call" | custom-call | bytes 737280 | tf_op jit(solution)/shard_map/pallas_call | solution.py:437
  68.0 0.0 collective-permute-done.6.got_ref
  68.0 0.8 %shard_map.231 = (f32[96,576]{1,0:T(8,128)}, f32[192,96]{1,0:T(8,128)}) custom-call(f32[1,96,768]{2,1,0:T(8,128)S(1)} %get-tuple-element.75.keep_ref, bf16[1,96,768]{2,1,0:T(8,128)(2,1)S(1)} %collective-permute-done.6.got_ref), custom_call_target="tpu_custom_call" | custom-call | bytes 737280 | tf_op jit(solution)/shard_map/pallas_call | solution.py:437
  (4 shorter events, 0.2 us)
Async XLA Ops:
  0.6 13.9 %copy-start = (s32[256]{0:T(256)S(1)}, s32[256]{0:T(256)}, u32[]{:S(2)}) copy-start(s32[256]{0:T(256)} %param.16) | copy-start | bytes 3076
  0.7 13.9 %copy-start.8 = (f32[3,192]{1,0:T(4,128)S(1)}, f32[3,192]{1,0:T(4,128)}, u32[]{:S(2)}) copy-start(f32[3,192]{1,0:T(4,128)} %offsets_ref.3) | copy-start | bytes 6916
  0.7 13.9 %copy-start.5 = (f32[768]{0:T(1024)S(1)}, f32[768]{0:T(1024)}, u32[]{:S(2)}) copy-start(f32[768]{0:T(1024)} %param.26) | copy-start | bytes 9220
  0.7 13.9 %copy-start.4 = (f32[768]{0:T(1024)S(1)}, f32[768]{0:T(1024)}, u32[]{:S(2)}) copy-start(f32[768]{0:T(1024)} %param.20) | copy-start | bytes 9220
  0.7 13.9 %copy-start.3 = (f32[768]{0:T(1024)S(1)}, f32[768]{0:T(1024)}, u32[]{:S(2)}) copy-start(f32[768]{0:T(1024)} %param.19) | copy-start | bytes 9220
  0.7 13.9 %copy-start.7 = (f32[768]{0:T(1024)S(1)}, f32[768]{0:T(1024)}, u32[]{:S(2)}) copy-start(f32[768]{0:T(1024)} %param.18) | copy-start | bytes 9220
  0.7 13.9 %copy-start.6 = (f32[768]{0:T(1024)S(1)}, f32[768]{0:T(1024)}, u32[]{:S(2)}) copy-start(f32[768]{0:T(1024)} %param.17) | copy-start | bytes 9220
  1.8 12.8 %collective-permute-start.3 = (bf16[272,768]{1,0:T(8,128)(2,1)S(1)}, bf16[272,768]{1,0:T(8,128)(2,1)S(1)}, u32[]{:S(2)}, u32[]{:S(2)}) collective-permute-start(bf16[272,768]{1,0:T(8,128)(2,1)S(1)} %shard_map.226), channel_id=1, source_target_pairs={{0,8},{4,12},{8,0},{12,4},{16,24},{20,28},{24,16},{28,20},{1,9},{5... | collective-permute-start | bytes 1253384 | tf_op jit(solution)/shard_map/ppermute | solution.py:449
  14.6 11.8 %collective-permute-start.4 = (bf16[272,768]{1,0:T(8,128)(2,1)S(1)}, bf16[272,768]{1,0:T(8,128)(2,1)S(1)}, u32[]{:S(2)}, u32[]{:S(2)}) collective-permute-start(bf16[272,768]{1,0:T(8,128)(2,1)S(1)} %collective-permute-done.3.got_ref), channel_id=1, source_target_pairs={{0,1},{1,0},{2,3},{3,2},{4,5},{5,4},{6,7},{7,6},{8,9},{9,8},{10,11... | collective-permute-start | bytes 1253384 | tf_op jit(solution)/shard_map/ppermute | solution.py:449
  22.6 1.9 %collective-permute-start = (bf16[256,768]{1,0:T(8,128)(2,1)S(1)}, bf16[256,768]{1,0:T(8,128)(2,1)S(1)}, u32[]{:S(2)}, u32[]{:S(2)}) collective-permute-start(bf16[256,768]{1,0:T(8,128)(2,1)S(1)} %get-tuple-element.54), channel_id=1, source_target_pairs={{0,1},{1,0},{2,3},{3,2},{4,5},{5,4},{6,7},{7,6},{8,9},{9,8},{10,11... | collective-permute-start | bytes 1179656 | tf_op jit(solution)/shard_map/ppermute | solution.py:449
  24.6 11.5 %collective-permute-start.1 = (bf16[256,768]{1,0:T(8,128)(2,1)S(1)}, bf16[256,768]{1,0:T(8,128)(2,1)S(1)}, u32[]{:S(2)}, u32[]{:S(2)}) collective-permute-start(bf16[256,768]{1,0:T(8,128)(2,1)S(1)} %shard_map.223.part_ref), channel_id=1, source_target_pairs={{0,2},{1,3},{2,0},{3,1},{4,6},{5,7},{6,4},{7,5},{8,10},{9,11},{10,... | collective-permute-start | bytes 1179656 | tf_op jit(solution)/shard_map/ppermute | solution.py:449
  27.8 13.1 %collective-permute-start.7 = (bf16[192,768]{1,0:T(8,128)(2,1)S(1)}, bf16[192,768]{1,0:T(8,128)(2,1)S(1)}, u32[]{:S(2)}, u32[]{:S(2)}) collective-permute-start(bf16[192,768]{1,0:T(8,128)(2,1)S(1)} %get-tuple-element.82), channel_id=1, source_target_pairs={{0,4},{4,0},{8,12},{12,8},{16,20},{20,16},{24,28},{28,24},{1,5},{5... | collective-permute-start | bytes 884744 | tf_op jit(solution)/shard_map/ppermute | solution.py:449
  30.0 6.1 %copy-start.1 = (f32[768]{0:T(1024)S(1)}, f32[768]{0:T(1024)}, u32[]{:S(2)}) copy-start(f32[768]{0:T(1024)} %param.24) | copy-start | bytes 9220
  30.0 6.1 %copy-start.2 = (f32[768]{0:T(1024)S(1)}, f32[768]{0:T(1024)}, u32[]{:S(2)}) copy-start(f32[768]{0:T(1024)} %param.28) | copy-start | bytes 9220
  34.2 9.9 %collective-permute-start.5 = (bf16[192,768]{1,0:T(8,128)(2,1)S(1)}, bf16[192,768]{1,0:T(8,128)(2,1)S(1)}, u32[]{:S(2)}, u32[]{:S(2)}) collective-permute-start(bf16[192,768]{1,0:T(8,128)(2,1)S(1)} %get-tuple-element.74), channel_id=1, source_target_pairs={{0,4},{4,0},{8,12},{12,8},{16,20},{20,16},{24,28},{28,24},{1,5},{5... | collective-permute-start | bytes 884744 | tf_op jit(solution)/shard_map/ppermute | solution.py:449
  36.4 29.9 %collective-permute-start.2 = (bf16[256,768]{1,0:T(8,128)(2,1)S(1)}, bf16[256,768]{1,0:T(8,128)(2,1)S(1)}, u32[]{:S(2)}, u32[]{:S(2)}) collective-permute-start(bf16[256,768]{1,0:T(8,128)(2,1)S(1)} %shard_map.224.own_ref), channel_id=1, source_target_pairs={{0,1},{1,0},{2,3},{3,2},{4,5},{5,4},{6,7},{7,6},{8,9},{9,8},{10,11... | collective-permute-start | bytes 1179656 | tf_op jit(solution)/shard_map/ppermute | solution.py:449
  36.5 17.3 %collective-permute-start.9 = (bf16[192,384]{1,0:T(8,128)(2,1)S(1)}, bf16[192,384]{1,0:T(8,128)(2,1)S(1)}, u32[]{:S(2)}, u32[]{:S(2)}) collective-permute-start(bf16[192,384]{1,0:T(8,128)(2,1)S(1)} %get-tuple-element.87), channel_id=1, source_target_pairs={{0,16},{4,20},{8,24},{12,28},{16,0},{20,4},{24,8},{28,12},{1,17},{... | collective-permute-start | bytes 442376 | tf_op jit(solution)/shard_map/ppermute | solution.py:449
  39.3 16.2 %collective-permute-start.11 = (bf16[192,384]{1,0:T(8,128)(2,1)S(1)}, bf16[192,384]{1,0:T(8,128)(2,1)S(1)}, u32[]{:S(2)}, u32[]{:S(2)}) collective-permute-start(bf16[192,384]{1,0:T(8,128)(2,1)S(1)} %get-tuple-element.91), channel_id=1, source_target_pairs={{0,4},{4,0},{8,12},{12,8},{16,20},{20,16},{24,28},{28,24},{1,5},{5... | collective-permute-start | bytes 442376 | tf_op jit(solution)/shard_map/ppermute | solution.py:449
  40.9 26.3 %collective-permute-start.8 = (bf16[1,96,768]{2,1,0:T(8,128)(2,1)S(1)}, bf16[1,96,768]{2,1,0:T(8,128)(2,1)S(1)}, u32[]{:S(2)}, u32[]{:S(2)}) collective-permute-start(bf16[1,96,768]{2,1,0:T(8,128)(2,1)S(1)} %get-tuple-element.84), channel_id=1, source_target_pairs={{0,16},{4,20},{8,24},{12,28},{16,0},{20,4},{24,8},{28,12},{1,17},{... | collective-permute-start | bytes 442376 | tf_op jit(solution)/shard_map/ppermute | solution.py:449
  44.2 23.8 %collective-permute-start.6 = (bf16[1,96,768]{2,1,0:T(8,128)(2,1)S(1)}, bf16[1,96,768]{2,1,0:T(8,128)(2,1)S(1)}, u32[]{:S(2)}, u32[]{:S(2)}) collective-permute-start(bf16[1,96,768]{2,1,0:T(8,128)(2,1)S(1)} %get-tuple-element.76), channel_id=1, source_target_pairs={{0,16},{4,20},{8,24},{12,28},{16,0},{20,4},{24,8},{28,12},{1,17},{... | collective-permute-start | bytes 442376 | tf_op jit(solution)/shard_map/ppermute | solution.py:449
  46.8 18.1 %all-to-all-start = ((bf16[32,8,96]{2,1,0:T(8,128)(2,1)}), bf16[32,8,96]{2,1,0:T(8,128)(2,1)S(1)}, u32[]{:S(2)}, u32[]{:S(2)}) async-start(bf16[32,8,96]{2,1,0:T(8,128)(2,1)} %bitcast.11), calls=%async_computation | async-start | bytes 131072 | tf_op jit(solution)/shard_map/all_to_all | solution.py:527
  53.8 11.7 %collective-permute-start.10 = (bf16[1,96,384]{2,1,0:T(8,128)(2,1)S(1)}, bf16[1,96,384]{2,1,0:T(8,128)(2,1)S(1)}, u32[]{:S(2)}, u32[]{:S(2)}) collective-permute-start(bf16[1,96,384]{2,1,0:T(8,128)(2,1)S(1)} %get-tuple-element.89), channel_id=1, source_target_pairs={{0,4},{4,0},{8,12},{12,8},{16,20},{20,16},{24,28},{28,24},{1,5},{5... | collective-permute-start | bytes 221192 | tf_op jit(solution)/shard_map/ppermute | solution.py:449
  55.6 9.9 %collective-permute-start.12 = (bf16[1,96,384]{2,1,0:T(8,128)(2,1)S(1)}, bf16[1,96,384]{2,1,0:T(8,128)(2,1)S(1)}, u32[]{:S(2)}, u32[]{:S(2)}) collective-permute-start(bf16[1,96,384]{2,1,0:T(8,128)(2,1)S(1)} %get-tuple-element.93), channel_id=1, source_target_pairs={{0,16},{4,20},{8,24},{12,28},{16,0},{20,4},{24,8},{28,12},{1,17},{... | collective-permute-start | bytes 221192 | tf_op jit(solution)/shard_map/ppermute | solution.py:449

commit v5 on v4

--- a/solution.py
+++ b/solution.py
@@ -164,16 +164,16 @@
     labels.wait()
     row = label_row(seg_ref)
     row = jnp.concatenate([row, jnp.zeros((1, width - n), F32)], axis=1)
-    out_ref[n : n + 16] = jnp.broadcast_to(row, (16, width)).astype(BF16)
+    out_ref[n : n + 8] = jnp.broadcast_to(row, (8, width)).astype(BF16)
     pltpu.make_async_copy(tok_ref, out_ref.at[0:n], sem).wait()
 
 
 def own_kernel(
-    heads, size, n_dp, n_tensor,
+    heads, size, n_dp,
     tok_any, cot_any, seg_ref, gain_one_ref, shift_one_ref, gain_two_ref, shift_two_ref, offsets_ref, thr_ref,
     inlet_any, outlet_any, expand_any, contract_any,
     tok_ref, cot_ref, inlet_ref, outlet_ref, expand_ref, contract_ref,
-    away_ref, keep_ref, active_ref, back_ref, attended_ref, inlet_back_ref, tile_ref, one_ref, two_ref, out_ref,
+    away_ref, keep_ref, active_ref, back_ref, attended_ref, inlet_back_ref, tile_away_ref, tile_keep_ref, one_ref, two_ref, out_ref,
     sems,
 ):
     copies = [
@@ -238,10 +238,11 @@
     bias = total(grad_full)
     hidden = total(expanded_grad)
     shares = total(inlet_full)
-    block = tile_ref.shape[3]
+    block = tile_keep_ref.shape[2]
     third = 3 * size // n_dp
     per_dp = hidden.shape[1] // n_dp
-    for d in range(n_dp):
+
+    def tile(d):
         lanes = slice(d * block, (d + 1) * block)
         local = hidden[:, d * per_dp : (d + 1) * per_dp]
         if per_dp < block:
@@ -249,10 +250,15 @@
         cut = [shares[:, h * 3 * size + d * third : h * 3 * size + (d + 1) * third] for h in range(heads)]
         if heads * third < block:
             cut.append(jnp.zeros((1, block - heads * third), F32))
-        mine = jnp.concatenate([bias[:, lanes], local, jnp.concatenate(cut, axis=1), jnp.zeros((1, block), F32)], axis=0)
-        for t in range(n_tensor):
-            here = jnp.where(lax.axis_index("tensor") == t, mine, 0.0)
-            tile_ref[d, t] = jnp.concatenate([everyone[:, lanes], here], axis=0).astype(BF16)
+        return jnp.concatenate(
+            [everyone[:, lanes], bias[:, lanes], local, jnp.concatenate(cut, axis=1), jnp.zeros((1, block), F32)], axis=0
+        )
+
+    upper = bit_of(1) == 1
+    for place, number in enumerate(rest_order(n_dp)):
+        low, high = tile(number), tile(number + 1)
+        tile_away_ref[place] = jnp.where(upper, low, high).astype(BF16)
+        tile_keep_ref[place] = jnp.where(upper, high, low)
 
 
 def bit_of(bit):
@@ -265,6 +271,10 @@
 
 def other_bits(dests, first):
     return [1 << i for i in range(12) if 1 << i < dests and 1 << i not in (2, first)]
+
+
+def rest_order(dests):
+    return list(range(0, dests, 2))
 
 
 def dest_order(dests, first):
@@ -321,7 +331,7 @@
 
 
 def expand_kernel(
-    dests,
+    dests, first,
     got_ref, swap_ref, two_ref, gain_ref, shift_ref, expand_ref, thr_ref, contract_ref, back_ref,
     send_ref, keep_ref, active_ref, grad_ref,
     left_ref,
@@ -336,17 +346,13 @@
     active, grad = ffn_block(normed, grad_out, expand_ref[...], flat(thr_ref), contract_ref[...])
     active_ref[...] = active
     right = jnp.concatenate([back_ref[...], grad.astype(BF16)], axis=0)
-    put_halves(dot(spread_rows((two_ref, left_ref), dests, 1), right), send_ref, keep_ref)
-
-
-def contract_kernel(
-    dests, firsts, grad_ref, out_ref, own_ref, active_ref, send_a_ref, keep_a_ref, send_b_ref, keep_b_ref, left_ref
-):
+    put_halves(dot(spread_rows((two_ref, left_ref), dests, first), right), send_ref, keep_ref)
+
+
+def contract_kernel(dests, grad_ref, out_ref, own_ref, active_ref, send_ref, keep_ref, left_ref):
     put_left(grad_ref[...], left_ref)
     right = jnp.concatenate([own_ref[...], active_ref[...]], axis=0)
-    split = send_a_ref.shape[1]
-    put_halves(dot(spread_rows((out_ref, left_ref), dests, firsts[0]), right[:, :split]), send_a_ref, keep_a_ref)
-    put_halves(dot(spread_rows((out_ref, left_ref), dests, firsts[1]), right[:, split:]), send_b_ref, keep_b_ref)
+    put_halves(dot(spread_rows((out_ref, left_ref), dests, 1), right), send_ref, keep_ref)
 
 
 def attention_kernel(
@@ -382,12 +388,8 @@
         left_ref[i] = keep_ref[stay] + got_ref[stay].astype(F32)
 
 
-def add_kernel(*refs):
-    out_ref, at = refs[-1], 0
-    for keep_ref, got_ref in zip(refs[:-1:2], refs[1:-1:2]):
-        columns = keep_ref.shape[2]
-        out_ref[:, at : at + columns] = keep_ref[0] + got_ref[0].astype(F32)
-        at += columns
+def add_kernel(keep_ref, got_ref, out_ref):
+    out_ref[...] = keep_ref[0] + got_ref[0].astype(F32)
 
 
 def split_kernel(keep_ref, got_ref, inlet_ref, outlet_ref):
@@ -416,15 +418,17 @@
     grad_ref[...] = jnp.where(first, got, own)
 
 
-def small_kernel(heads, third, tile_ref, norms_ref, bias_ref, thr_ref, offsets_ref):
-    total = tile_ref[0].astype(F32)
-    for i in range(1, tile_ref.shape[0]):
-        total = total + tile_ref[i].astype(F32)
-    norms_ref[...] = total[0:4]
+def small_kernel(heads, third, keep_ref, got_ref, norms_ref, bias_ref, thr_ref, offsets_ref):
+    total = keep_ref[0] + got_ref[0].astype(F32)
+    norms_ref[...] = total
     bias_ref[...] = total[4:5]
     thr_ref[...] = total[5:6, : thr_ref.shape[1]]
     for head in range(heads):
         offsets_ref[head : head + 1] = total[6:7, head * third : (head + 1) * third]
+
+
+def rows_kernel(own_ref, got_ref, out_ref):
+    out_ref[...] = (own_ref[...] + got_ref[...])[: out_ref.shape[0]]
 
 
 def call(kernel, outs, args, flops=0, scratch=(), limit=VMEM_LIMIT, places="", results=""):
@@ -464,18 +468,18 @@
     turned = left_shape(n, width, n_dp)
 
     payload, = call(
-        gather_kernel, [((n + 16, width), BF16)], [tokens, cotangent, seg],
+        gather_kernel, [((n + 8, width), BF16)], [tokens, cotangent, seg],
         scratch=[pltpu.VMEM(seg.shape, seg.dtype), pltpu.SemaphoreType.DMA, pltpu.SemaphoreType.DMA], places="aaa",
     )
     got = swap(payload, "dp", n_dp, 2)
     other = swap(got, "tensor", n_tensor, 1)
 
-    (tok, cot, inlet_v, outlet_v, expand_v, contract_v, away, keep, active, back, attended, inlet_back, tile,
+    (tok, cot, inlet_v, outlet_v, expand_v, contract_v, away, keep, active, back, attended, inlet_back, tile_away, tile_keep,
      one_t, two_t, out_t) = call(
-        functools.partial(own_kernel, heads, size, n_dp, n_tensor),
+        functools.partial(own_kernel, heads, size, n_dp),
         [(tokens.shape, BF16), (cotangent.shape, BF16), ((columns, width), BF16), (outlet.shape, BF16), (expand.shape, BF16),
          (contract.shape, BF16), ((n, width), BF16), ((n, width), F32), ((n, units), BF16), ((n, units), BF16),
-         ((n, mine), BF16), ((n, columns), BF16), ((n_dp, n_tensor, 8, block), BF16),
+         ((n, mine), BF16), ((n, columns), BF16), ((n_dp // 2, 8, block), BF16), ((n_dp // 2, 8, block), F32),
          (turned, BF16), (turned, BF16), (turned, BF16)],
         [tokens, cotangent, seg, gain_one, shift_one, gain_two, shift_two, offsets, thr, inlet.T, outlet, expand, contract],
         flops=6e9, scratch=[pltpu.SemaphoreType.DMA((6,))], places="aavvvvvvvaaaa",
@@ -483,24 +487,21 @@
     half = n_dp // 4 * block
     left = [pltpu.VMEM(turned, BF16)]
 
+    far_first = 4 if n_dp > 4 else 1
     expand_send, expand_keep, active_near, grad_near = call(
-        functools.partial(expand_kernel, n_dp),
+        functools.partial(expand_kernel, n_dp, far_first),
         [((half, units), BF16), ((half, units), F32), ((n, units), BF16), ((n, width), BF16)],
         [got, other, two_t, gain_two, shift_two, expand_v, thr, contract_v, back],
         flops=3e9, scratch=left,
     )
-    expand_got = swap(expand_send, "dp", n_dp, 1)
-    far_first = 4 if n_dp > 4 else 1
-    part_units = units // 2
-    early_send, early_keep, late_send, late_keep, near_t = call(
-        functools.partial(contract_kernel, n_dp, (far_first, 1)),
-        [((half, part_units), BF16), ((half, part_units), F32), ((half, units - part_units), BF16),
-         ((half, units - part_units), F32), (turned, BF16)],
+    expand_got = swap(expand_send, "dp", n_dp, far_first)
+    contract_send, contract_keep, near_t = call(
+        functools.partial(contract_kernel, n_dp),
+        [((half, units), BF16), ((half, units), F32), (turned, BF16)],
         [grad_near, out_t, active, active_near],
         flops=1e9,
     )
-    early_got = swap(early_send, "dp", n_dp, far_first)
-    late_got = swap(late_send, "dp", n_dp, 1)
+    contract_got = swap(contract_send, "dp", n_dp, 1)
     tail_send, tail_keep = call(
         functools.partial(attention_kernel, heads, size, n_dp),
         [((half, columns + mine), BF16), ((half, columns + mine), F32)],
@@ -524,31 +525,38 @@
     paired = swap(done, "tensor", n_tensor, 1)
     mixed, input_grad = call(pair_kernel, [((n, width), BF16)] * 2, [done, paired], results="dd")
 
-    tile = lax.all_to_all(tile.reshape(n_dp * n_tensor, 8, block), ("dp", "tensor"), 0, 0, tiled=True)
-    third = offsets.shape[1] // n_dp
-    norm_grads, bias_grad, thr_grad, offsets_grad = call(
-        functools.partial(small_kernel, heads, third),
-        [((4, block), F32), ((1, block), F32), ((1, units // n_dp), F32), ((heads, third), F32)], [tile], results="dddd",
-    )
+    def halve(bit, kept, arrived):
+        shape = (kept.shape[0] // 2,) + kept.shape[1:]
+        return call(functools.partial(halve_kernel, bit), [(shape, BF16), (shape, F32)], [kept, arrived], flops=1e6)
 
     def reduce(kept, arrived, first):
-        columns_here = kept.shape[1]
-        kept = kept.reshape(-1, block, columns_here)
-        arrived = arrived.reshape(-1, block, columns_here)
+        kept = kept.reshape(-1, block, kept.shape[1])
+        arrived = arrived.reshape(kept.shape)
         for bit in other_bits(n_dp, first):
-            rest = kept.shape[0] // 2
-            shape = (rest, block, columns_here)
-            away, kept = call(
-                functools.partial(halve_kernel, bit), [(shape, BF16), (shape, F32)], [kept, arrived], flops=1e6
-            )
+            away, kept = halve(bit, kept, arrived)
             arrived = swap(away, "dp", n_dp, bit)
         return [kept, arrived]
 
-    expand_grad, = call(add_kernel, [((block, units), F32)], reduce(expand_keep, expand_got, 1), results="d")
-    contract_grad, = call(
-        add_kernel, [((block, units), F32)],
-        reduce(early_keep, early_got, far_first) + reduce(late_keep, late_got, 1), results="d",
-    )
+    kept, arrived = tile_keep, swap(tile_away, "dp", n_dp, 1)
+    bit = 2
+    while bit < n_dp:
+        away, kept = halve(bit, kept, arrived)
+        arrived = swap(away, "dp", n_dp, bit)
+        bit *= 2
+    third = offsets.shape[1] // n_dp
+    norms, bias_grad, thr_grad, offsets_grad = call(
+        functools.partial(small_kernel, heads, third),
+        [((8, block), F32), ((1, block), F32), ((1, units // n_dp), F32), ((heads, third), F32)], [kept, arrived],
+        results="vddd",
+    )
+    bit = 1
+    while 2 * bit < n_tensor:
+        norms, = call(rows_kernel, [((8, block), F32)], [norms, swap(norms, "tensor", n_tensor, bit)])
+        bit *= 2
+    norm_grads, = call(rows_kernel, [((4, block), F32)], [norms, swap(norms, "tensor", n_tensor, bit)], results="d")
+
+    expand_grad, = call(add_kernel, [((block, units), F32)], reduce(expand_keep, expand_got, far_first), results="d")
+    contract_grad, = call(add_kernel, [((block, units), F32)], reduce(contract_keep, contract_got, 1), results="d")
     inlet_grad, outlet_grad = call(
         split_kernel, [((block, columns), F32), ((mine, block), F32)],
         reduce(tail_keep, tail_got, 1), results="dd",

time: 69 us -> 72.7 us (1.054)
  waiting for transfers between devices: 28.5 us -> 34 us
  starting transfers between devices: 19.7 us -> 18 us
    ppermute x13 -> x16, waiting for transfers between devices: 19.3 us -> 34 us  [swap(): return lax.ppermute(value, axis, [(i, i ^ bit) for i in range(count)])]
    all_to_all x1 -> x0, waiting for transfers between devices: 9.18 us -> none  [step(): lax.all_to_all(tile.reshape(n_dp * n_tensor, 8, block), ('dp', 'tensor'),...]
    all_to_all x1 -> x0, starting transfers between devices: 2.84 us -> none  [step(): lax.all_to_all(tile.reshape(n_dp * n_tensor, 8, block), ('dp', 'tensor'),...]
    ppermute x13 -> x16, starting transfers between devices: 16.8 us -> 18 us  [swap(): return lax.ppermute(value, axis, [(i, i ^ bit) for i in range(count)])]
    pallas_call x16 -> x19, Pallas kernels: 19.8 us -> 19.7 us  [call(): pl.pallas_call(kernel, out_shape=[jax.ShapeDtypeStruct(shape, dtype) for...]
  transfers between devices with their start and end apart: 14 -> 16, of which waited for: 6 -> 9; matrix products, arithmetic and copies ran while one was open for 0% -> 0% of each run, Pallas kernels for 26% -> 25%
where the time goes in v5:
time: 72.7 us; the launch traced here: 72.5 us
  waiting for transfers between devices  34 us (47%)
  Pallas kernels  19.7 us (27%)
  starting transfers between devices  18 us (25%)
  between operations  0.85 us (1%)
    ppermute x16, waiting for transfers between devices, swap(): return lax.ppermute(value, axis, [(i, i ^ bit) for i in range(count)])  34 us
    pallas_call x19, Pallas kernels, call(): pl.pallas_call(kernel, out_shape=[jax.ShapeDtypeStruct(shape, dtype) for...  19.7 us
    ppermute x16, starting transfers between devices, swap(): return lax.ppermute(value, axis, [(i, i ^ bit) for i in range(count)])  18 us
  transfers between devices with their start and end apart: 16, of which 9 were waited for; matrix products, arithmetic and copies ran while one was open for 0% of the time, Pallas kernels for 25%

profile of v5, /device:TPU:0, one launch (start us, length us, event | category | flops | bytes accessed | tf_op | source)
XLA Modules:
  0.0 72.5 jit_solution(14743278877751639575)
XLA Ops:
  0.6 0.0 copy-start
  0.7 0.0 copy-start.8
  0.7 0.0 copy-start.5
  0.7 0.0 copy-start.4
  0.7 0.0 copy-start.3
  0.7 0.0 copy-start.7
  0.7 0.0 copy-start.6
  0.7 1.1 %shard_map.226 = bf16[264,768]{1,0:T(8,128)(2,1)S(1)} custom-call(bf16[256,768]{1,0:T(8,128)(2,1)} %tok_ref.1, bf16[256,768]{1,0:T(8,128)(2,1)} %cot_ref.1, s32[2,128]{1,0:T(2,128)} %bitcast.23), custom_call_target="tpu_custom_call" | custom-call | bytes 1192960 | tf_op jit(solution)/shard_map/pallas_call | solution.py:441
  1.8 3.1 %collective-permute-start.3 = (bf16[264,768]{1,0:T(8,128)(2,1)S(1)}, bf16[264,768]{1,0:T(8,128)(2,1)S(1)}, u32[]{:S(2)}, u32[]{:S(2)}) collective-permute-start(bf16[264,768]{1,0:T(8,128)(2,1)S(1)} %shard_map.226), channel_id=1, source_target_pairs={{0,8},{4,12},{8,0},{12,4},{16,24},{20,28},{24,16},{28,20},{1,9},{5... | collective-permute-start | bytes 1216520 | tf_op jit(solution)/shard_map/ppermute | solution.py:453
  4.9 9.4 %collective-permute-done.3.got_ref = bf16[264,768]{1,0:T(8,128)(2,1)S(1)} collective-permute-done((bf16[264,768]{1,0:T(8,128)(2,1)S(1)}, bf16[264,768]{1,0:T(8,128)(2,1)S(1)}, u32[]{:S(2)}, u32[]{:S(2)}) %collective-permute-start.3) | collective-permute-done | bytes 405536 | tf_op jit(solution)/shard_map/ppermute | solution.py:453
  14.3 0.0 collective-permute-start.4
  14.3 0.0 copy-done
  14.3 0.0 copy-done.8
  14.3 0.0 copy-done.5
  14.3 0.0 copy-done.4
  14.3 0.0 copy-done.3
  14.3 0.0 copy-done.7
  14.3 0.0 copy-done.6
  14.3 7.4 %shard_map.222 = (bf16[256,768]{1,0:T(8,128)(2,1)S(1)}, bf16[256,768]{1,0:T(8,128)(2,1)S(1)}, bf16[576,768]{1,0:T(8,128)(2,1)S(1)}, bf16[192,768]{1,0:T(8,128)(2...) custom-call(bf16[256,768]{1,0:T(8,128)(2,1)} %tok_ref.1, ...), custom_call_target="tpu_custom_call" | custom-call | flops 6000000000 | bytes 12226816 | tf_op jit(solution)/shard_map/pallas_call | solution.py:441
  21.8 0.6 collective-permute-start
  22.3 1.3 %collective-permute-done.got_ref = bf16[256,768]{1,0:T(8,128)(2,1)S(1)} collective-permute-done((bf16[256,768]{1,0:T(8,128)(2,1)S(1)}, bf16[256,768]{1,0:T(8,128)(2,1)S(1)}, u32[]{:S(2)}, u32[]{:S(2)}) %collective-permute-start) | collective-permute-done | bytes 393248 | tf_op jit(solution)/shard_map/ppermute | solution.py:453
  23.7 0.1 shard_map.223.part_ref
  23.8 1.7 %collective-permute-start.1 = (bf16[256,768]{1,0:T(8,128)(2,1)S(1)}, bf16[256,768]{1,0:T(8,128)(2,1)S(1)}, u32[]{:S(2)}, u32[]{:S(2)}) collective-permute-start(bf16[256,768]{1,0:T(8,128)(2,1)S(1)} %shard_map.223.part_ref), channel_id=1, source_target_pairs={{0,2},{1,3},{2,0},{3,1},{4,6},{5,7},{6,4},{7,5},{8,10},{9,11},{10,... | collective-permute-start | bytes 1179656 | tf_op jit(solution)/shard_map/ppermute | solution.py:453
  25.5 0.0 collective-permute-done.4.swap_ref
  25.5 1.4 %shard_map.227 = (bf16[192,768]{1,0:T(8,128)(2,1)S(1)}, f32[192,768]{1,0:T(8,128)S(1)}, bf16[256,768]{1,0:T(8,128)(2,1)S(1)}, bf16[256,768]{1,0:T(8,128)(2,1)S(1)}) custom-call(bf16[264,768]{1,0:T(8,128)(2,1)S(1)} %collective-permute-done.3.got_ref, bf16[264,768]{1,0:T(8,128)(2,1)S(1)} %collective-permute-done.4.swap_ref, ...), custom_call_target="tpu_custom_call" | custom-call | flops 3000000000 | bytes 5637120 | tf_op jit(solution)/shard_map/pallas_call | solution.py:441
  26.9 2.7 %collective-permute-start.10 = (bf16[192,768]{1,0:T(8,128)(2,1)S(1)}, bf16[192,768]{1,0:T(8,128)(2,1)S(1)}, u32[]{:S(2)}, u32[]{:S(2)}) collective-permute-start(bf16[192,768]{1,0:T(8,128)(2,1)S(1)} %get-tuple-element.88), channel_id=1, source_target_pairs={{0,16},{4,20},{8,24},{12,28},{16,0},{20,4},{24,8},{28,12},{1,17},{... | collective-permute-start | bytes 884744 | tf_op jit(solution)/shard_map/ppermute | solution.py:453
  29.5 0.6 shard_map.228
  30.1 0.0 copy-start.1
  30.1 0.0 copy-start.2
  30.2 4.1 %shard_map.229 = (bf16[192,768]{1,0:T(8,128)(2,1)S(1)}, f32[192,768]{1,0:T(8,128)S(1)}) custom-call(bf16[264,768]{1,0:T(8,128)(2,1)S(1)} %collective-permute-done.3.got_ref, bf16[264,768]{1,0:T(8,128)(2,1)S(1)} %collective-permute-done.4.swap_ref, bf16[256,768]{1,0:T(8,128)(2,1)S(1)} %get-tuple-element.64.grad_ref, f32[6,128]{1,0:T(8,128)S(1)} %bitcast.35, ...), custom_call_target="tpu_custom_call" | custom-call | flops 5000000000 | bytes 4849920 | tf_op jit(solution)/shard_map/pallas_call | solution.py:441
  34.3 1.6 %collective-permute-start.5 = (bf16[192,768]{1,0:T(8,128)(2,1)S(1)}, bf16[192,768]{1,0:T(8,128)(2,1)S(1)}, u32[]{:S(2)}, u32[]{:S(2)}) collective-permute-start(bf16[192,768]{1,0:T(8,128)(2,1)S(1)} %get-tuple-element.75), channel_id=1, source_target_pairs={{0,4},{4,0},{8,12},{12,8},{16,20},{20,16},{24,28},{28,24},{1,5},{5... | collective-permute-start | bytes 884744 | tf_op jit(solution)/shard_map/ppermute | solution.py:453
  35.9 0.5 collective-permute-start.12
  36.4 0.0 collective-permute-done.1.got_ref
  36.4 0.0 copy-done.1
  36.4 0.0 copy-done.2
  36.4 0.3 shard_map.224.own_ref
  36.7 0.1 collective-permute-start.2
  36.8 6.4 %collective-permute-done.10 = bf16[192,768]{1,0:T(8,128)(2,1)S(1)} collective-permute-done((bf16[192,768]{1,0:T(8,128)(2,1)S(1)}, bf16[192,768]{1,0:T(8,128)(2,1)S(1)}, u32[]{:S(2)}, u32[]{:S(2)}) %collective-permute-start.10) | collective-permute-done | bytes 294944 | tf_op jit(solution)/shard_map/ppermute | solution.py:453
  43.2 1.6 %collective-permute-start.11 = (bf16[1,96,768]{2,1,0:T(8,128)(2,1)S(1)}, bf16[1,96,768]{2,1,0:T(8,128)(2,1)S(1)}, u32[]{:S(2)}, u32[]{:S(2)}) collective-permute-start(bf16[1,96,768]{2,1,0:T(8,128)(2,1)S(1)} %get-tuple-element.90), channel_id=1, source_target_pairs={{0,4},{4,0},{8,12},{12,8},{16,20},{20,16},{24,28},{28,24},{1,5},{5... | collective-permute-start | bytes 442376 | tf_op jit(solution)/shard_map/ppermute | solution.py:453
  44.8 0.0 collective-permute-done.5
  44.9 0.1 collective-permute-start.6
  45.0 5.6 %collective-permute-done.12 = bf16[192,768]{1,0:T(8,128)(2,1)S(1)} collective-permute-done((bf16[192,768]{1,0:T(8,128)(2,1)S(1)}, bf16[192,768]{1,0:T(8,128)(2,1)S(1)}, u32[]{:S(2)}, u32[]{:S(2)}) %collective-permute-start.12) | collective-permute-done | bytes 294944 | tf_op jit(solution)/shard_map/ppermute | solution.py:453
  50.6 0.4 collective-permute-start.13
  51.0 1.5 %collective-permute-start.7 = (bf16[4,8,96]{2,1,0:T(8,128)(2,1)S(1)}, bf16[4,8,96]{2,1,0:T(8,128)(2,1)S(1)}, u32[]{:S(2)}, u32[]{:S(2)}) collective-permute-start(bf16[4,8,96]{2,1,0:T(8,128)(2,1)S(1)} %get-tuple-element.80), channel_id=1, source_target_pairs={{0,4},{4,0},{8,12},{12,8},{16,20},{20,16},{24,28},{28,24},{1,5},{5... | collective-permute-start | bytes 18440 | tf_op jit(solution)/shard_map/ppermute | solution.py:453
  52.5 2.1 %collective-permute-done.7.got_ref = bf16[4,8,96]{2,1,0:T(8,128)(2,1)S(1)} collective-permute-done((bf16[4,8,96]{2,1,0:T(8,128)(2,1)S(1)}, bf16[4,8,96]{2,1,0:T(8,128)(2,1)S(1)}, u32[]{:S(2)}, u32[]{:S(2)}) %collective-permute-start.7) | collective-permute-done | bytes 6176 | tf_op jit(solution)/shard_map/ppermute | solution.py:453
  54.7 1.6 %collective-permute-start.8 = (bf16[2,8,96]{2,1,0:T(8,128)(2,1)S(1)}, bf16[2,8,96]{2,1,0:T(8,128)(2,1)S(1)}, u32[]{:S(2)}, u32[]{:S(2)}) collective-permute-start(bf16[2,8,96]{2,1,0:T(8,128)(2,1)S(1)} %get-tuple-element.82), channel_id=1, source_target_pairs={{0,8},{4,12},{8,0},{12,4},{16,24},{20,28},{24,16},{28,20},{1,9},{5... | collective-permute-start | bytes 9224 | tf_op jit(solution)/shard_map/ppermute | solution.py:453
  56.3 2.4 %collective-permute-done.8.got_ref = bf16[2,8,96]{2,1,0:T(8,128)(2,1)S(1)} collective-permute-done((bf16[2,8,96]{2,1,0:T(8,128)(2,1)S(1)}, bf16[2,8,96]{2,1,0:T(8,128)(2,1)S(1)}, u32[]{:S(2)}, u32[]{:S(2)}) %collective-permute-start.8) | collective-permute-done | bytes 3104 | tf_op jit(solution)/shard_map/ppermute | solution.py:453
  58.7 2.2 %collective-permute-start.9 = (bf16[1,8,96]{2,1,0:T(8,128)(2,1)S(1)}, bf16[1,8,96]{2,1,0:T(8,128)(2,1)S(1)}, u32[]{:S(2)}, u32[]{:S(2)}) collective-permute-start(bf16[1,8,96]{2,1,0:T(8,128)(2,1)S(1)} %get-tuple-element.84), channel_id=1, source_target_pairs={{0,16},{4,20},{8,24},{12,28},{16,0},{20,4},{24,8},{28,12},{1,17},{... | collective-permute-start | bytes 4616 | tf_op jit(solution)/shard_map/ppermute | solution.py:453
  60.9 2.3 %collective-permute-done.9.got_ref = bf16[1,8,96]{2,1,0:T(8,128)(2,1)S(1)} collective-permute-done((bf16[1,8,96]{2,1,0:T(8,128)(2,1)S(1)}, bf16[1,8,96]{2,1,0:T(8,128)(2,1)S(1)}, u32[]{:S(2)}, u32[]{:S(2)}) %collective-permute-start.9) | collective-permute-done | bytes 1568 | tf_op jit(solution)/shard_map/ppermute | solution.py:453
  63.2 0.7 shard_map.234
  63.9 0.0 collective-permute-start.14
  63.9 1.2 %collective-permute-done.14.got_ref = f32[8,96]{1,0:T(8,128)S(1)} collective-permute-done((f32[8,96]{1,0:T(8,128)S(1)}, f32[8,96]{1,0:T(8,128)S(1)}, u32[]{:S(2)}, u32[]{:S(2)}) %collective-permute-start.14) | collective-permute-done | bytes 3104 | tf_op jit(solution)/shard_map/ppermute | solution.py:453
  65.0 0.4 collective-permute-start.15
  65.4 3.2 %collective-permute-done.15.got_ref = f32[8,96]{1,0:T(8,128)S(1)} collective-permute-done((f32[8,96]{1,0:T(8,128)S(1)}, f32[8,96]{1,0:T(8,128)S(1)}, u32[]{:S(2)}, u32[]{:S(2)}) %collective-permute-start.15) | collective-permute-done | bytes 3104 | tf_op jit(solution)/shard_map/ppermute | solution.py:453
  68.7 0.6 shard_map.240
  69.2 0.0 collective-permute-done.2.got_ref
  69.2 1.0 %shard_map.225 = (bf16[256,768]{1,0:T(8,128)(2,1)}, bf16[256,768]{1,0:T(8,128)(2,1)}) custom-call(bf16[256,768]{1,0:T(8,128)(2,1)S(1)} %shard_map.224.own_ref, bf16[256,768]{1,0:T(8,128)(2,1)S(1)} %collective-permute-done.2.got_ref), custom_call_target="tpu_custom_call" | custom-call | bytes 1572864 | tf_op jit(solution)/shard_map/pallas_call | solution.py:441
  70.2 0.0 collective-permute-done.11.got_ref
  70.2 0.8 %shard_map.236 = f32[96,768]{1,0:T(8,128)} custom-call(f32[1,96,768]{2,1,0:T(8,128)S(1)} %get-tuple-element.89.keep_ref, bf16[1,96,768]{2,1,0:T(8,128)(2,1)S(1)} %collective-permute-done.11.got_ref), custom_call_target="tpu_custom_call" | custom-call | bytes 737280 | tf_op jit(solution)/shard_map/pallas_call | solution.py:441
  71.0 0.0 collective-permute-done.6.got_ref
  71.0 0.8 %shard_map.231 = (f32[96,576]{1,0:T(8,128)}, f32[192,96]{1,0:T(8,128)}) custom-call(f32[1,96,768]{2,1,0:T(8,128)S(1)} %get-tuple-element.76.keep_ref, bf16[1,96,768]{2,1,0:T(8,128)(2,1)S(1)} %collective-permute-done.6.got_ref), custom_call_target="tpu_custom_call" | custom-call | bytes 737280 | tf_op jit(solution)/shard_map/pallas_call | solution.py:441
  71.8 0.0 collective-permute-done.13.got_ref
  71.8 0.7 %shard_map.238 = f32[96,768]{1,0:T(8,128)} custom-call(f32[1,96,768]{2,1,0:T(8,128)S(1)} %get-tuple-element.94.keep_ref, bf16[1,96,768]{2,1,0:T(8,128)(2,1)S(1)} %collective-permute-done.13.got_ref), custom_call_target="tpu_custom_call" | custom-call | bytes 737280 | tf_op jit(solution)/shard_map/pallas_call | solution.py:441
  (6 shorter events, 0.2 us)
Async XLA Ops:
  0.6 13.6 %copy-start = (s32[256]{0:T(256)S(1)}, s32[256]{0:T(256)}, u32[]{:S(2)}) copy-start(s32[256]{0:T(256)} %param.16) | copy-start | bytes 3076
  0.7 13.6 %copy-start.8 = (f32[3,192]{1,0:T(4,128)S(1)}, f32[3,192]{1,0:T(4,128)}, u32[]{:S(2)}) copy-start(f32[3,192]{1,0:T(4,128)} %offsets_ref.3) | copy-start | bytes 6916
  0.7 13.6 %copy-start.5 = (f32[768]{0:T(1024)S(1)}, f32[768]{0:T(1024)}, u32[]{:S(2)}) copy-start(f32[768]{0:T(1024)} %param.26) | copy-start | bytes 9220
  0.7 13.6 %copy-start.4 = (f32[768]{0:T(1024)S(1)}, f32[768]{0:T(1024)}, u32[]{:S(2)}) copy-start(f32[768]{0:T(1024)} %param.20) | copy-start | bytes 9220
  0.7 13.6 %copy-start.3 = (f32[768]{0:T(1024)S(1)}, f32[768]{0:T(1024)}, u32[]{:S(2)}) copy-start(f32[768]{0:T(1024)} %param.19) | copy-start | bytes 9220
  0.7 13.6 %copy-start.7 = (f32[768]{0:T(1024)S(1)}, f32[768]{0:T(1024)}, u32[]{:S(2)}) copy-start(f32[768]{0:T(1024)} %param.18) | copy-start | bytes 9220
  0.7 13.6 %copy-start.6 = (f32[768]{0:T(1024)S(1)}, f32[768]{0:T(1024)}, u32[]{:S(2)}) copy-start(f32[768]{0:T(1024)} %param.17) | copy-start | bytes 9220
  1.8 12.5 %collective-permute-start.3 = (bf16[264,768]{1,0:T(8,128)(2,1)S(1)}, bf16[264,768]{1,0:T(8,128)(2,1)S(1)}, u32[]{:S(2)}, u32[]{:S(2)}) collective-permute-start(bf16[264,768]{1,0:T(8,128)(2,1)S(1)} %shard_map.226), channel_id=1, source_target_pairs={{0,8},{4,12},{8,0},{12,4},{16,24},{20,28},{24,16},{28,20},{1,9},{5... | collective-permute-start | bytes 1216520 | tf_op jit(solution)/shard_map/ppermute | solution.py:453
  14.3 11.2 %collective-permute-start.4 = (bf16[264,768]{1,0:T(8,128)(2,1)S(1)}, bf16[264,768]{1,0:T(8,128)(2,1)S(1)}, u32[]{:S(2)}, u32[]{:S(2)}) collective-permute-start(bf16[264,768]{1,0:T(8,128)(2,1)S(1)} %collective-permute-done.3.got_ref), channel_id=1, source_target_pairs={{0,1},{1,0},{2,3},{3,2},{4,5},{5,4},{6,7},{7,6},{8,9},{9,8},{10,11... | collective-permute-start | bytes 1216520 | tf_op jit(solution)/shard_map/ppermute | solution.py:453
  21.8 1.9 %collective-permute-start = (bf16[256,768]{1,0:T(8,128)(2,1)S(1)}, bf16[256,768]{1,0:T(8,128)(2,1)S(1)}, u32[]{:S(2)}, u32[]{:S(2)}) collective-permute-start(bf16[256,768]{1,0:T(8,128)(2,1)S(1)} %get-tuple-element.55), channel_id=1, source_target_pairs={{0,1},{1,0},{2,3},{3,2},{4,5},{5,4},{6,7},{7,6},{8,9},{9,8},{10,11... | collective-permute-start | bytes 1179656 | tf_op jit(solution)/shard_map/ppermute | solution.py:453
  23.8 12.6 %collective-permute-start.1 = (bf16[256,768]{1,0:T(8,128)(2,1)S(1)}, bf16[256,768]{1,0:T(8,128)(2,1)S(1)}, u32[]{:S(2)}, u32[]{:S(2)}) collective-permute-start(bf16[256,768]{1,0:T(8,128)(2,1)S(1)} %shard_map.223.part_ref), channel_id=1, source_target_pairs={{0,2},{1,3},{2,0},{3,1},{4,6},{5,7},{6,4},{7,5},{8,10},{9,11},{10,... | collective-permute-start | bytes 1179656 | tf_op jit(solution)/shard_map/ppermute | solution.py:453
  26.9 16.3 %collective-permute-start.10 = (bf16[192,768]{1,0:T(8,128)(2,1)S(1)}, bf16[192,768]{1,0:T(8,128)(2,1)S(1)}, u32[]{:S(2)}, u32[]{:S(2)}) collective-permute-start(bf16[192,768]{1,0:T(8,128)(2,1)S(1)} %get-tuple-element.88), channel_id=1, source_target_pairs={{0,16},{4,20},{8,24},{12,28},{16,0},{20,4},{24,8},{28,12},{1,17},{... | collective-permute-start | bytes 884744 | tf_op jit(solution)/shard_map/ppermute | solution.py:453
  30.1 6.2 %copy-start.1 = (f32[768]{0:T(1024)S(1)}, f32[768]{0:T(1024)}, u32[]{:S(2)}) copy-start(f32[768]{0:T(1024)} %param.24) | copy-start | bytes 9220
  30.1 6.2 %copy-start.2 = (f32[768]{0:T(1024)S(1)}, f32[768]{0:T(1024)}, u32[]{:S(2)}) copy-start(f32[768]{0:T(1024)} %param.28) | copy-start | bytes 9220
  34.3 10.5 %collective-permute-start.5 = (bf16[192,768]{1,0:T(8,128)(2,1)S(1)}, bf16[192,768]{1,0:T(8,128)(2,1)S(1)}, u32[]{:S(2)}, u32[]{:S(2)}) collective-permute-start(bf16[192,768]{1,0:T(8,128)(2,1)S(1)} %get-tuple-element.75), channel_id=1, source_target_pairs={{0,4},{4,0},{8,12},{12,8},{16,20},{20,16},{24,28},{28,24},{1,5},{5... | collective-permute-start | bytes 884744 | tf_op jit(solution)/shard_map/ppermute | solution.py:453
  35.9 14.7 %collective-permute-start.12 = (bf16[192,768]{1,0:T(8,128)(2,1)S(1)}, bf16[192,768]{1,0:T(8,128)(2,1)S(1)}, u32[]{:S(2)}, u32[]{:S(2)}) collective-permute-start(bf16[192,768]{1,0:T(8,128)(2,1)S(1)} %get-tuple-element.93), channel_id=1, source_target_pairs={{0,4},{4,0},{8,12},{12,8},{16,20},{20,16},{24,28},{28,24},{1,5},{5... | collective-permute-start | bytes 884744 | tf_op jit(solution)/shard_map/ppermute | solution.py:453
  36.7 32.5 %collective-permute-start.2 = (bf16[256,768]{1,0:T(8,128)(2,1)S(1)}, bf16[256,768]{1,0:T(8,128)(2,1)S(1)}, u32[]{:S(2)}, u32[]{:S(2)}) collective-permute-start(bf16[256,768]{1,0:T(8,128)(2,1)S(1)} %shard_map.224.own_ref), channel_id=1, source_target_pairs={{0,1},{1,0},{2,3},{3,2},{4,5},{5,4},{6,7},{7,6},{8,9},{9,8},{10,11... | collective-permute-start | bytes 1179656 | tf_op jit(solution)/shard_map/ppermute | solution.py:453
  43.2 27.0 %collective-permute-start.11 = (bf16[1,96,768]{2,1,0:T(8,128)(2,1)S(1)}, bf16[1,96,768]{2,1,0:T(8,128)(2,1)S(1)}, u32[]{:S(2)}, u32[]{:S(2)}) collective-permute-start(bf16[1,96,768]{2,1,0:T(8,128)(2,1)S(1)} %get-tuple-element.90), channel_id=1, source_target_pairs={{0,4},{4,0},{8,12},{12,8},{16,20},{20,16},{24,28},{28,24},{1,5},{5... | collective-permute-start | bytes 442376 | tf_op jit(solution)/shard_map/ppermute | solution.py:453
  44.9 26.1 %collective-permute-start.6 = (bf16[1,96,768]{2,1,0:T(8,128)(2,1)S(1)}, bf16[1,96,768]{2,1,0:T(8,128)(2,1)S(1)}, u32[]{:S(2)}, u32[]{:S(2)}) collective-permute-start(bf16[1,96,768]{2,1,0:T(8,128)(2,1)S(1)} %get-tuple-element.77), channel_id=1, source_target_pairs={{0,16},{4,20},{8,24},{12,28},{16,0},{20,4},{24,8},{28,12},{1,17},{... | collective-permute-start | bytes 442376 | tf_op jit(solution)/shard_map/ppermute | solution.py:453
  50.6 21.2 %collective-permute-start.13 = (bf16[1,96,768]{2,1,0:T(8,128)(2,1)S(1)}, bf16[1,96,768]{2,1,0:T(8,128)(2,1)S(1)}, u32[]{:S(2)}, u32[]{:S(2)}) collective-permute-start(bf16[1,96,768]{2,1,0:T(8,128)(2,1)S(1)} %get-tuple-element.95), channel_id=1, source_target_pairs={{0,16},{4,20},{8,24},{12,28},{16,0},{20,4},{24,8},{28,12},{1,17},{... | collective-permute-start | bytes 442376 | tf_op jit(solution)/shard_map/ppermute | solution.py:453
  51.0 3.7 %collective-permute-start.7 = (bf16[4,8,96]{2,1,0:T(8,128)(2,1)S(1)}, bf16[4,8,96]{2,1,0:T(8,128)(2,1)S(1)}, u32[]{:S(2)}, u32[]{:S(2)}) collective-permute-start(bf16[4,8,96]{2,1,0:T(8,128)(2,1)S(1)} %get-tuple-element.80), channel_id=1, source_target_pairs={{0,4},{4,0},{8,12},{12,8},{16,20},{20,16},{24,28},{28,24},{1,5},{5... | collective-permute-start | bytes 18440 | tf_op jit(solution)/shard_map/ppermute | solution.py:453
  54.7 4.1 %collective-permute-start.8 = (bf16[2,8,96]{2,1,0:T(8,128)(2,1)S(1)}, bf16[2,8,96]{2,1,0:T(8,128)(2,1)S(1)}, u32[]{:S(2)}, u32[]{:S(2)}) collective-permute-start(bf16[2,8,96]{2,1,0:T(8,128)(2,1)S(1)} %get-tuple-element.82), channel_id=1, source_target_pairs={{0,8},{4,12},{8,0},{12,4},{16,24},{20,28},{24,16},{28,20},{1,9},{5... | collective-permute-start | bytes 9224 | tf_op jit(solution)/shard_map/ppermute | solution.py:453
  58.7 4.5 %collective-permute-start.9 = (bf16[1,8,96]{2,1,0:T(8,128)(2,1)S(1)}, bf16[1,8,96]{2,1,0:T(8,128)(2,1)S(1)}, u32[]{:S(2)}, u32[]{:S(2)}) collective-permute-start(bf16[1,8,96]{2,1,0:T(8,128)(2,1)S(1)} %get-tuple-element.84), channel_id=1, source_target_pairs={{0,16},{4,20},{8,24},{12,28},{16,0},{20,4},{24,8},{28,12},{1,17},{... | collective-permute-start | bytes 4616 | tf_op jit(solution)/shard_map/ppermute | solution.py:453
  63.9 1.2 %collective-permute-start.14 = (f32[8,96]{1,0:T(8,128)S(1)}, f32[8,96]{1,0:T(8,128)S(1)}, u32[]{:S(2)}, u32[]{:S(2)}) collective-permute-start(f32[8,96]{1,0:T(8,128)S(1)} %get-tuple-element.97.own_ref), channel_id=1, source_target_pairs={{0,1},{1,0},{2,3},{3,2},{4,5},{5,4},{6,7},{7,6},{8,9},{9,8},{10,11... | collective-permute-start | bytes 9224 | tf_op jit(solution)/shard_map/ppermute | solution.py:453
  65.0 3.6 %collective-permute-start.15 = (f32[8,96]{1,0:T(8,128)S(1)}, f32[8,96]{1,0:T(8,128)S(1)}, u32[]{:S(2)}, u32[]{:S(2)}) collective-permute-start(f32[8,96]{1,0:T(8,128)S(1)} %shard_map.239.own_ref), channel_id=1, source_target_pairs={{0,2},{1,3},{2,0},{3,1},{4,6},{5,7},{6,4},{7,5},{8,10},{9,11},{10,... | collective-permute-start | bytes 9224 | tf_op jit(solution)/shard_map/ppermute | solution.py:453

commit v6 on v5

--- a/solution.py
+++ b/solution.py
@@ -392,11 +392,20 @@
     out_ref[...] = keep_ref[0] + got_ref[0].astype(F32)
 
 
-def split_kernel(keep_ref, got_ref, inlet_ref, outlet_ref):
+def split_kernel(
+    heads, third, keep_ref, got_ref, small_ref, norms_ref, far_ref,
+    inlet_ref, outlet_ref, norm_ref, bias_ref, thr_ref, offsets_ref,
+):
     total = keep_ref[0] + got_ref[0].astype(F32)
     columns = inlet_ref.shape[1]
     inlet_ref[...] = total[:, :columns]
     outlet_ref[...] = total[:, columns:].T
+    norm_ref[...] = (norms_ref[...] + far_ref[...])[:4]
+    small = small_ref[...]
+    bias_ref[...] = small[4:5]
+    thr_ref[...] = small[5:6, : thr_ref.shape[1]]
+    for head in range(heads):
+        offsets_ref[head : head + 1] = small[6:7, head * third : (head + 1) * third]
 
 
 def part_kernel(keep_ref, got_ref, out_ref):
@@ -411,24 +420,19 @@
     out_ref[...] = (base + part).astype(BF16)
 
 
-def pair_kernel(own_ref, got_ref, mixed_ref, grad_ref):
+def ends_kernel(
+    own_ref, got_ref, keep_c_ref, got_c_ref, keep_e_ref, got_e_ref, mixed_ref, grad_ref, contract_ref, expand_ref
+):
     first = core_bit() == 0
     own, got = own_ref[...], got_ref[...]
     mixed_ref[...] = jnp.where(first, own, got)
     grad_ref[...] = jnp.where(first, got, own)
-
-
-def small_kernel(heads, third, keep_ref, got_ref, norms_ref, bias_ref, thr_ref, offsets_ref):
-    total = keep_ref[0] + got_ref[0].astype(F32)
-    norms_ref[...] = total
-    bias_ref[...] = total[4:5]
-    thr_ref[...] = total[5:6, : thr_ref.shape[1]]
-    for head in range(heads):
-        offsets_ref[head : head + 1] = total[6:7, head * third : (head + 1) * third]
+    contract_ref[...] = keep_c_ref[0] + got_c_ref[0].astype(F32)
+    expand_ref[...] = keep_e_ref[0] + got_e_ref[0].astype(F32)
 
 
 def rows_kernel(own_ref, got_ref, out_ref):
-    out_ref[...] = (own_ref[...] + got_ref[...])[: out_ref.shape[0]]
+    out_ref[...] = own_ref[...] + got_ref[...]
 
 
 def call(kernel, outs, args, flops=0, scratch=(), limit=VMEM_LIMIT, places="", results=""):
@@ -523,7 +527,6 @@
         [part, far, tok, cot, seg, folded(outlet_bias), folded(contract_bias)], flops=1e6,
     )
     paired = swap(done, "tensor", n_tensor, 1)
-    mixed, input_grad = call(pair_kernel, [((n, width), BF16)] * 2, [done, paired], results="dd")
 
     def halve(bit, kept, arrived):
         shape = (kept.shape[0] // 2,) + kept.shape[1:]
@@ -544,22 +547,25 @@
         arrived = swap(away, "dp", n_dp, bit)
         bit *= 2
     third = offsets.shape[1] // n_dp
-    norms, bias_grad, thr_grad, offsets_grad = call(
-        functools.partial(small_kernel, heads, third),
-        [((8, block), F32), ((1, block), F32), ((1, units // n_dp), F32), ((heads, third), F32)], [kept, arrived],
-        results="vddd",
-    )
+    small, = call(add_kernel, [((8, block), F32)], [kept, arrived])
+    norms = small
     bit = 1
     while 2 * bit < n_tensor:
         norms, = call(rows_kernel, [((8, block), F32)], [norms, swap(norms, "tensor", n_tensor, bit)])
         bit *= 2
-    norm_grads, = call(rows_kernel, [((4, block), F32)], [norms, swap(norms, "tensor", n_tensor, bit)], results="d")
-
-    expand_grad, = call(add_kernel, [((block, units), F32)], reduce(expand_keep, expand_got, far_first), results="d")
-    contract_grad, = call(add_kernel, [((block, units), F32)], reduce(contract_keep, contract_got, 1), results="d")
-    inlet_grad, outlet_grad = call(
-        split_kernel, [((block, columns), F32), ((mine, block), F32)],
-        reduce(tail_keep, tail_got, 1), results="dd",
+    far_norms = swap(norms, "tensor", n_tensor, bit)
+
+    contract_parts = reduce(contract_keep, contract_got, 1)
+    expand_parts = reduce(expand_keep, expand_got, far_first)
+    mixed, input_grad, contract_grad, expand_grad = call(
+        ends_kernel, [((n, width), BF16), ((n, width), BF16), ((block, units), F32), ((block, units), F32)],
+        [done, paired] + contract_parts + expand_parts, results="dddd",
+    )
+    inlet_grad, outlet_grad, norm_grads, bias_grad, thr_grad, offsets_grad = call(
+        functools.partial(split_kernel, heads, third),
+        [((block, columns), F32), ((mine, block), F32), ((4, block), F32), ((1, block), F32), ((1, units // n_dp), F32),
+         ((heads, third), F32)],
+        reduce(tail_keep, tail_got, 1) + [small, norms, far_norms], results="dddddd",
     )
     return (
         mixed, input_grad, inlet_grad, offsets_grad, outlet_grad, expand_grad, thr_grad, contract_grad.T,

time: 72.7 us -> 70.3 us (0.967)
  Pallas kernels: 19.7 us -> 17.2 us
    pallas_call x19 -> x16, Pallas kernels: 19.7 us -> 17.2 us  [call(): pl.pallas_call(kernel, out_shape=[jax.ShapeDtypeStruct(shape, dtype) for...]
  transfers between devices with their start and end apart: 16 -> 16, of which waited for: 9 -> 9; matrix products, arithmetic and copies ran while one was open for 0% -> 0% of each run, Pallas kernels for 25% -> 21%
where the time goes in v6:
time: 70.3 us; the launch traced here: 70.1 us
  waiting for transfers between devices  34 us (48%)
  starting transfers between devices  18 us (26%)
  Pallas kernels  17.2 us (24%)
  between operations  0.86 us (1%)
    ppermute x16, waiting for transfers between devices, swap(): return lax.ppermute(value, axis, [(i, i ^ bit) for i in range(count)])  34 us
    ppermute x16, starting transfers between devices, swap(): return lax.ppermute(value, axis, [(i, i ^ bit) for i in range(count)])  18 us
    pallas_call x16, Pallas kernels, call(): pl.pallas_call(kernel, out_shape=[jax.ShapeDtypeStruct(shape, dtype) for...  17.2 us
  transfers between devices with their start and end apart: 16, of which 9 were waited for; matrix products, arithmetic and copies ran while one was open for 0% of the time, Pallas kernels for 21%

profile of v6, /device:TPU:0, one launch (start us, length us, event | category | flops | bytes accessed | tf_op | source)
XLA Modules:
  0.0 70.1 jit_solution(14587134355520821485)
XLA Ops:
  0.6 0.0 copy-start
  0.7 0.0 copy-start.8
  0.7 0.0 copy-start.5
  0.7 0.0 copy-start.4
  0.7 0.0 copy-start.3
  0.7 0.0 copy-start.7
  0.7 0.0 copy-start.6
  0.7 1.1 %shard_map.225 = bf16[264,768]{1,0:T(8,128)(2,1)S(1)} custom-call(bf16[256,768]{1,0:T(8,128)(2,1)} %tok_ref.1, bf16[256,768]{1,0:T(8,128)(2,1)} %cot_ref.1, s32[2,128]{1,0:T(2,128)} %bitcast.23), custom_call_target="tpu_custom_call" | custom-call | bytes 1192960 | tf_op jit(solution)/shard_map/pallas_call | solution.py:445
  1.8 3.1 %collective-permute-start.3 = (bf16[264,768]{1,0:T(8,128)(2,1)S(1)}, bf16[264,768]{1,0:T(8,128)(2,1)S(1)}, u32[]{:S(2)}, u32[]{:S(2)}) collective-permute-start(bf16[264,768]{1,0:T(8,128)(2,1)S(1)} %shard_map.225), channel_id=1, source_target_pairs={{0,8},{4,12},{8,0},{12,4},{16,24},{20,28},{24,16},{28,20},{1,9},{5... | collective-permute-start | bytes 1216520 | tf_op jit(solution)/shard_map/ppermute | solution.py:457
  4.9 9.4 %collective-permute-done.3.got_ref = bf16[264,768]{1,0:T(8,128)(2,1)S(1)} collective-permute-done((bf16[264,768]{1,0:T(8,128)(2,1)S(1)}, bf16[264,768]{1,0:T(8,128)(2,1)S(1)}, u32[]{:S(2)}, u32[]{:S(2)}) %collective-permute-start.3) | collective-permute-done | bytes 405536 | tf_op jit(solution)/shard_map/ppermute | solution.py:457
  14.3 0.0 collective-permute-start.4
  14.3 0.0 copy-done
  14.3 0.0 copy-done.8
  14.3 0.0 copy-done.5
  14.3 0.0 copy-done.4
  14.3 0.0 copy-done.3
  14.3 0.0 copy-done.7
  14.3 0.0 copy-done.6
  14.3 7.4 %shard_map.222 = (bf16[256,768]{1,0:T(8,128)(2,1)S(1)}, bf16[256,768]{1,0:T(8,128)(2,1)S(1)}, bf16[576,768]{1,0:T(8,128)(2,1)S(1)}, bf16[192,768]{1,0:T(8,128)(2...) custom-call(bf16[256,768]{1,0:T(8,128)(2,1)} %tok_ref.1, ...), custom_call_target="tpu_custom_call" | custom-call | flops 6000000000 | bytes 12226816 | tf_op jit(solution)/shard_map/pallas_call | solution.py:445
  21.8 0.6 collective-permute-start
  22.3 1.3 %collective-permute-done.got_ref = bf16[256,768]{1,0:T(8,128)(2,1)S(1)} collective-permute-done((bf16[256,768]{1,0:T(8,128)(2,1)S(1)}, bf16[256,768]{1,0:T(8,128)(2,1)S(1)}, u32[]{:S(2)}, u32[]{:S(2)}) %collective-permute-start) | collective-permute-done | bytes 393248 | tf_op jit(solution)/shard_map/ppermute | solution.py:457
  23.7 0.1 shard_map.223.part_ref
  23.8 1.7 %collective-permute-start.1 = (bf16[256,768]{1,0:T(8,128)(2,1)S(1)}, bf16[256,768]{1,0:T(8,128)(2,1)S(1)}, u32[]{:S(2)}, u32[]{:S(2)}) collective-permute-start(bf16[256,768]{1,0:T(8,128)(2,1)S(1)} %shard_map.223.part_ref), channel_id=1, source_target_pairs={{0,2},{1,3},{2,0},{3,1},{4,6},{5,7},{6,4},{7,5},{8,10},{9,11},{10,... | collective-permute-start | bytes 1179656 | tf_op jit(solution)/shard_map/ppermute | solution.py:457
  25.5 0.0 collective-permute-done.4.swap_ref
  25.5 1.4 %shard_map.226 = (bf16[192,768]{1,0:T(8,128)(2,1)S(1)}, f32[192,768]{1,0:T(8,128)S(1)}, bf16[256,768]{1,0:T(8,128)(2,1)S(1)}, bf16[256,768]{1,0:T(8,128)(2,1)S(1)}) custom-call(bf16[264,768]{1,0:T(8,128)(2,1)S(1)} %collective-permute-done.3.got_ref, bf16[264,768]{1,0:T(8,128)(2,1)S(1)} %collective-permute-done.4.swap_ref, ...), custom_call_target="tpu_custom_call" | custom-call | flops 3000000000 | bytes 5637120 | tf_op jit(solution)/shard_map/pallas_call | solution.py:445
  26.9 2.7 %collective-permute-start.7 = (bf16[192,768]{1,0:T(8,128)(2,1)S(1)}, bf16[192,768]{1,0:T(8,128)(2,1)S(1)}, u32[]{:S(2)}, u32[]{:S(2)}) collective-permute-start(bf16[192,768]{1,0:T(8,128)(2,1)S(1)} %get-tuple-element.73), channel_id=1, source_target_pairs={{0,16},{4,20},{8,24},{12,28},{16,0},{20,4},{24,8},{28,12},{1,17},{... | collective-permute-start | bytes 884744 | tf_op jit(solution)/shard_map/ppermute | solution.py:457
  29.5 0.6 shard_map.227
  30.1 0.0 copy-start.1
  30.1 0.0 copy-start.2
  30.2 4.1 %shard_map.231 = (bf16[192,768]{1,0:T(8,128)(2,1)S(1)}, f32[192,768]{1,0:T(8,128)S(1)}) custom-call(bf16[264,768]{1,0:T(8,128)(2,1)S(1)} %collective-permute-done.3.got_ref, bf16[264,768]{1,0:T(8,128)(2,1)S(1)} %collective-permute-done.4.swap_ref, bf16[256,768]{1,0:T(8,128)(2,1)S(1)} %get-tuple-element.64.grad_ref, f32[6,128]{1,0:T(8,128)S(1)} %bitcast.35, ...), custom_call_target="tpu_custom_call" | custom-call | flops 5000000000 | bytes 4849920 | tf_op jit(solution)/shard_map/pallas_call | solution.py:445
  34.3 1.6 %collective-permute-start.9 = (bf16[192,768]{1,0:T(8,128)(2,1)S(1)}, bf16[192,768]{1,0:T(8,128)(2,1)S(1)}, u32[]{:S(2)}, u32[]{:S(2)}) collective-permute-start(bf16[192,768]{1,0:T(8,128)(2,1)S(1)} %get-tuple-element.85), channel_id=1, source_target_pairs={{0,4},{4,0},{8,12},{12,8},{16,20},{20,16},{24,28},{28,24},{1,5},{5... | collective-permute-start | bytes 884744 | tf_op jit(solution)/shard_map/ppermute | solution.py:457
  35.9 0.5 collective-permute-start.5
  36.4 0.0 collective-permute-done.1.got_ref
  36.4 0.0 copy-done.1
  36.4 0.0 copy-done.2
  36.4 0.3 shard_map.224.own_ref
  36.7 0.1 collective-permute-start.2
  36.8 6.4 %collective-permute-done.7 = bf16[192,768]{1,0:T(8,128)(2,1)S(1)} collective-permute-done((bf16[192,768]{1,0:T(8,128)(2,1)S(1)}, bf16[192,768]{1,0:T(8,128)(2,1)S(1)}, u32[]{:S(2)}, u32[]{:S(2)}) %collective-permute-start.7) | collective-permute-done | bytes 294944 | tf_op jit(solution)/shard_map/ppermute | solution.py:457
  43.2 1.6 %collective-permute-start.8 = (bf16[1,96,768]{2,1,0:T(8,128)(2,1)S(1)}, bf16[1,96,768]{2,1,0:T(8,128)(2,1)S(1)}, u32[]{:S(2)}, u32[]{:S(2)}) collective-permute-start(bf16[1,96,768]{2,1,0:T(8,128)(2,1)S(1)} %get-tuple-element.75), channel_id=1, source_target_pairs={{0,4},{4,0},{8,12},{12,8},{16,20},{20,16},{24,28},{28,24},{1,5},{5... | collective-permute-start | bytes 442376 | tf_op jit(solution)/shard_map/ppermute | solution.py:457
  44.8 0.0 collective-permute-done.9
  44.9 0.1 collective-permute-start.10
  45.0 5.6 %collective-permute-done.5 = bf16[192,768]{1,0:T(8,128)(2,1)S(1)} collective-permute-done((bf16[192,768]{1,0:T(8,128)(2,1)S(1)}, bf16[192,768]{1,0:T(8,128)(2,1)S(1)}, u32[]{:S(2)}, u32[]{:S(2)}) %collective-permute-start.5) | collective-permute-done | bytes 294944 | tf_op jit(solution)/shard_map/ppermute | solution.py:457
  50.6 0.4 collective-permute-start.6
  51.0 1.5 %collective-permute-start.11 = (bf16[4,8,96]{2,1,0:T(8,128)(2,1)S(1)}, bf16[4,8,96]{2,1,0:T(8,128)(2,1)S(1)}, u32[]{:S(2)}, u32[]{:S(2)}) collective-permute-start(bf16[4,8,96]{2,1,0:T(8,128)(2,1)S(1)} %get-tuple-element.89), channel_id=1, source_target_pairs={{0,4},{4,0},{8,12},{12,8},{16,20},{20,16},{24,28},{28,24},{1,5},{5... | collective-permute-start | bytes 18440 | tf_op jit(solution)/shard_map/ppermute | solution.py:457
  52.5 2.1 %collective-permute-done.11.got_ref = bf16[4,8,96]{2,1,0:T(8,128)(2,1)S(1)} collective-permute-done((bf16[4,8,96]{2,1,0:T(8,128)(2,1)S(1)}, bf16[4,8,96]{2,1,0:T(8,128)(2,1)S(1)}, u32[]{:S(2)}, u32[]{:S(2)}) %collective-permute-start.11) | collective-permute-done | bytes 6176 | tf_op jit(solution)/shard_map/ppermute | solution.py:457
  54.7 1.6 %collective-permute-start.12 = (bf16[2,8,96]{2,1,0:T(8,128)(2,1)S(1)}, bf16[2,8,96]{2,1,0:T(8,128)(2,1)S(1)}, u32[]{:S(2)}, u32[]{:S(2)}) collective-permute-start(bf16[2,8,96]{2,1,0:T(8,128)(2,1)S(1)} %get-tuple-element.91), channel_id=1, source_target_pairs={{0,8},{4,12},{8,0},{12,4},{16,24},{20,28},{24,16},{28,20},{1,9},{5... | collective-permute-start | bytes 9224 | tf_op jit(solution)/shard_map/ppermute | solution.py:457
  56.3 2.4 %collective-permute-done.12.got_ref = bf16[2,8,96]{2,1,0:T(8,128)(2,1)S(1)} collective-permute-done((bf16[2,8,96]{2,1,0:T(8,128)(2,1)S(1)}, bf16[2,8,96]{2,1,0:T(8,128)(2,1)S(1)}, u32[]{:S(2)}, u32[]{:S(2)}) %collective-permute-start.12) | collective-permute-done | bytes 3104 | tf_op jit(solution)/shard_map/ppermute | solution.py:457
  58.7 2.2 %collective-permute-start.13 = (bf16[1,8,96]{2,1,0:T(8,128)(2,1)S(1)}, bf16[1,8,96]{2,1,0:T(8,128)(2,1)S(1)}, u32[]{:S(2)}, u32[]{:S(2)}) collective-permute-start(bf16[1,8,96]{2,1,0:T(8,128)(2,1)S(1)} %get-tuple-element.93), channel_id=1, source_target_pairs={{0,16},{4,20},{8,24},{12,28},{16,0},{20,4},{24,8},{28,12},{1,17},{... | collective-permute-start | bytes 4616 | tf_op jit(solution)/shard_map/ppermute | solution.py:457
  60.9 2.3 %collective-permute-done.13.got_ref = bf16[1,8,96]{2,1,0:T(8,128)(2,1)S(1)} collective-permute-done((bf16[1,8,96]{2,1,0:T(8,128)(2,1)S(1)}, bf16[1,8,96]{2,1,0:T(8,128)(2,1)S(1)}, u32[]{:S(2)}, u32[]{:S(2)}) %collective-permute-start.13) | collective-permute-done | bytes 1568 | tf_op jit(solution)/shard_map/ppermute | solution.py:457
  63.2 0.0 collective-permute-start.14
  63.2 1.2 %collective-permute-done.14.got_ref = f32[8,96]{1,0:T(8,128)S(1)} collective-permute-done((f32[8,96]{1,0:T(8,128)S(1)}, f32[8,96]{1,0:T(8,128)S(1)}, u32[]{:S(2)}, u32[]{:S(2)}) %collective-permute-start.14) | collective-permute-done | bytes 3104 | tf_op jit(solution)/shard_map/ppermute | solution.py:457
  64.4 0.4 collective-permute-start.15
  64.8 3.2 %collective-permute-done.15.far_ref = f32[8,96]{1,0:T(8,128)S(1)} collective-permute-done((f32[8,96]{1,0:T(8,128)S(1)}, f32[8,96]{1,0:T(8,128)S(1)}, u32[]{:S(2)}, u32[]{:S(2)}) %collective-permute-start.15) | collective-permute-done | bytes 3104 | tf_op jit(solution)/shard_map/ppermute | solution.py:457
  68.0 0.0 collective-permute-done.10.got_ref
  68.0 0.8 %shard_map.237 = (f32[96,576]{1,0:T(8,128)}, f32[192,96]{1,0:T(8,128)}, f32[4,96]{1,0:T(4,128)}, f32[1,96]{1,0:T(1,128)}, f32[1,96]{1,0:T(1,128)}, /*index=5*/f32[3,24]{1,0:T(4,128)}) custom-call(f32[1,96,768]{2,1,0:T(8,128)S(1)} %get-tuple-element.86.keep_ref, bf16[1,96,768]{2,1,0:T(8,128)(2,1)S(1)} %collective-permute-done.10.got_ref, ...), custom_call_target="tpu_custom_call" | custom-call | bytes 749088 | tf_op jit(solution)/shard_map/pallas_call | solution.py:445
  68.8 0.0 collective-permute-done.2.got_ref
  68.9 0.0 collective-permute-done.8.got_e_ref
  68.9 0.0 collective-permute-done.6.got_c_ref
  68.9 1.2 %shard_map.230 = (bf16[256,768]{1,0:T(8,128)(2,1)}, bf16[256,768]{1,0:T(8,128)(2,1)}, f32[96,768]{1,0:T(8,128)}, f32[96,768]{1,0:T(8,128)}) custom-call(bf16[256,768]{1,0:T(8,128)(2,1)S(1)} %shard_map.224.own_ref, bf16[256,768]{1,0:T(8,128)(2,1)S(1)} %collective-permute-done.2.got_ref, f32[1,96,768]{2,1,0:T(8,128)S(1)} %get-tuple-element.70.keep_c_ref, ...), custom_call_target="tpu_custom_call" | custom-call | bytes 3047424 | tf_op jit(solution)/shard_map/pallas_call | solution.py:445
  (7 shorter events, 0.2 us)
Async XLA Ops:
  0.6 13.6 %copy-start = (s32[256]{0:T(256)S(1)}, s32[256]{0:T(256)}, u32[]{:S(2)}) copy-start(s32[256]{0:T(256)} %param.16) | copy-start | bytes 3076
  0.7 13.6 %copy-start.8 = (f32[3,192]{1,0:T(4,128)S(1)}, f32[3,192]{1,0:T(4,128)}, u32[]{:S(2)}) copy-start(f32[3,192]{1,0:T(4,128)} %offsets_ref.3) | copy-start | bytes 6916
  0.7 13.6 %copy-start.5 = (f32[768]{0:T(1024)S(1)}, f32[768]{0:T(1024)}, u32[]{:S(2)}) copy-start(f32[768]{0:T(1024)} %param.26) | copy-start | bytes 9220
  0.7 13.6 %copy-start.4 = (f32[768]{0:T(1024)S(1)}, f32[768]{0:T(1024)}, u32[]{:S(2)}) copy-start(f32[768]{0:T(1024)} %param.20) | copy-start | bytes 9220
  0.7 13.6 %copy-start.3 = (f32[768]{0:T(1024)S(1)}, f32[768]{0:T(1024)}, u32[]{:S(2)}) copy-start(f32[768]{0:T(1024)} %param.19) | copy-start | bytes 9220
  0.7 13.6 %copy-start.7 = (f32[768]{0:T(1024)S(1)}, f32[768]{0:T(1024)}, u32[]{:S(2)}) copy-start(f32[768]{0:T(1024)} %param.18) | copy-start | bytes 9220
  0.7 13.6 %copy-start.6 = (f32[768]{0:T(1024)S(1)}, f32[768]{0:T(1024)}, u32[]{:S(2)}) copy-start(f32[768]{0:T(1024)} %param.17) | copy-start | bytes 9220
  1.8 12.5 %collective-permute-start.3 = (bf16[264,768]{1,0:T(8,128)(2,1)S(1)}, bf16[264,768]{1,0:T(8,128)(2,1)S(1)}, u32[]{:S(2)}, u32[]{:S(2)}) collective-permute-start(bf16[264,768]{1,0:T(8,128)(2,1)S(1)} %shard_map.225), channel_id=1, source_target_pairs={{0,8},{4,12},{8,0},{12,4},{16,24},{20,28},{24,16},{28,20},{1,9},{5... | collective-permute-start | bytes 1216520 | tf_op jit(solution)/shard_map/ppermute | solution.py:457
  14.3 11.2 %collective-permute-start.4 = (bf16[264,768]{1,0:T(8,128)(2,1)S(1)}, bf16[264,768]{1,0:T(8,128)(2,1)S(1)}, u32[]{:S(2)}, u32[]{:S(2)}) collective-permute-start(bf16[264,768]{1,0:T(8,128)(2,1)S(1)} %collective-permute-done.3.got_ref), channel_id=1, source_target_pairs={{0,1},{1,0},{2,3},{3,2},{4,5},{5,4},{6,7},{7,6},{8,9},{9,8},{10,11... | collective-permute-start | bytes 1216520 | tf_op jit(solution)/shard_map/ppermute | solution.py:457
  21.8 1.9 %collective-permute-start = (bf16[256,768]{1,0:T(8,128)(2,1)S(1)}, bf16[256,768]{1,0:T(8,128)(2,1)S(1)}, u32[]{:S(2)}, u32[]{:S(2)}) collective-permute-start(bf16[256,768]{1,0:T(8,128)(2,1)S(1)} %get-tuple-element.57), channel_id=1, source_target_pairs={{0,1},{1,0},{2,3},{3,2},{4,5},{5,4},{6,7},{7,6},{8,9},{9,8},{10,11... | collective-permute-start | bytes 1179656 | tf_op jit(solution)/shard_map/ppermute | solution.py:457
  23.8 12.6 %collective-permute-start.1 = (bf16[256,768]{1,0:T(8,128)(2,1)S(1)}, bf16[256,768]{1,0:T(8,128)(2,1)S(1)}, u32[]{:S(2)}, u32[]{:S(2)}) collective-permute-start(bf16[256,768]{1,0:T(8,128)(2,1)S(1)} %shard_map.223.part_ref), channel_id=1, source_target_pairs={{0,2},{1,3},{2,0},{3,1},{4,6},{5,7},{6,4},{7,5},{8,10},{9,11},{10,... | collective-permute-start | bytes 1179656 | tf_op jit(solution)/shard_map/ppermute | solution.py:457
  26.9 16.3 %collective-permute-start.7 = (bf16[192,768]{1,0:T(8,128)(2,1)S(1)}, bf16[192,768]{1,0:T(8,128)(2,1)S(1)}, u32[]{:S(2)}, u32[]{:S(2)}) collective-permute-start(bf16[192,768]{1,0:T(8,128)(2,1)S(1)} %get-tuple-element.73), channel_id=1, source_target_pairs={{0,16},{4,20},{8,24},{12,28},{16,0},{20,4},{24,8},{28,12},{1,17},{... | collective-permute-start | bytes 884744 | tf_op jit(solution)/shard_map/ppermute | solution.py:457
  30.1 6.2 %copy-start.1 = (f32[768]{0:T(1024)S(1)}, f32[768]{0:T(1024)}, u32[]{:S(2)}) copy-start(f32[768]{0:T(1024)} %param.24) | copy-start | bytes 9220
  30.1 6.2 %copy-start.2 = (f32[768]{0:T(1024)S(1)}, f32[768]{0:T(1024)}, u32[]{:S(2)}) copy-start(f32[768]{0:T(1024)} %param.28) | copy-start | bytes 9220
  34.3 10.5 %collective-permute-start.9 = (bf16[192,768]{1,0:T(8,128)(2,1)S(1)}, bf16[192,768]{1,0:T(8,128)(2,1)S(1)}, u32[]{:S(2)}, u32[]{:S(2)}) collective-permute-start(bf16[192,768]{1,0:T(8,128)(2,1)S(1)} %get-tuple-element.85), channel_id=1, source_target_pairs={{0,4},{4,0},{8,12},{12,8},{16,20},{20,16},{24,28},{28,24},{1,5},{5... | collective-permute-start | bytes 884744 | tf_op jit(solution)/shard_map/ppermute | solution.py:457
  35.9 14.7 %collective-permute-start.5 = (bf16[192,768]{1,0:T(8,128)(2,1)S(1)}, bf16[192,768]{1,0:T(8,128)(2,1)S(1)}, u32[]{:S(2)}, u32[]{:S(2)}) collective-permute-start(bf16[192,768]{1,0:T(8,128)(2,1)S(1)} %get-tuple-element.69), channel_id=1, source_target_pairs={{0,4},{4,0},{8,12},{12,8},{16,20},{20,16},{24,28},{28,24},{1,5},{5... | collective-permute-start | bytes 884744 | tf_op jit(solution)/shard_map/ppermute | solution.py:457
  36.7 32.1 %collective-permute-start.2 = (bf16[256,768]{1,0:T(8,128)(2,1)S(1)}, bf16[256,768]{1,0:T(8,128)(2,1)S(1)}, u32[]{:S(2)}, u32[]{:S(2)}) collective-permute-start(bf16[256,768]{1,0:T(8,128)(2,1)S(1)} %shard_map.224.own_ref), channel_id=1, source_target_pairs={{0,1},{1,0},{2,3},{3,2},{4,5},{5,4},{6,7},{7,6},{8,9},{9,8},{10,11... | collective-permute-start | bytes 1179656 | tf_op jit(solution)/shard_map/ppermute | solution.py:457
  43.2 25.6 %collective-permute-start.8 = (bf16[1,96,768]{2,1,0:T(8,128)(2,1)S(1)}, bf16[1,96,768]{2,1,0:T(8,128)(2,1)S(1)}, u32[]{:S(2)}, u32[]{:S(2)}) collective-permute-start(bf16[1,96,768]{2,1,0:T(8,128)(2,1)S(1)} %get-tuple-element.75), channel_id=1, source_target_pairs={{0,4},{4,0},{8,12},{12,8},{16,20},{20,16},{24,28},{28,24},{1,5},{5... | collective-permute-start | bytes 442376 | tf_op jit(solution)/shard_map/ppermute | solution.py:457
  44.9 23.1 %collective-permute-start.10 = (bf16[1,96,768]{2,1,0:T(8,128)(2,1)S(1)}, bf16[1,96,768]{2,1,0:T(8,128)(2,1)S(1)}, u32[]{:S(2)}, u32[]{:S(2)}) collective-permute-start(bf16[1,96,768]{2,1,0:T(8,128)(2,1)S(1)} %get-tuple-element.87), channel_id=1, source_target_pairs={{0,16},{4,20},{8,24},{12,28},{16,0},{20,4},{24,8},{28,12},{1,17},{... | collective-permute-start | bytes 442376 | tf_op jit(solution)/shard_map/ppermute | solution.py:457
  50.6 18.3 %collective-permute-start.6 = (bf16[1,96,768]{2,1,0:T(8,128)(2,1)S(1)}, bf16[1,96,768]{2,1,0:T(8,128)(2,1)S(1)}, u32[]{:S(2)}, u32[]{:S(2)}) collective-permute-start(bf16[1,96,768]{2,1,0:T(8,128)(2,1)S(1)} %get-tuple-element.71), channel_id=1, source_target_pairs={{0,16},{4,20},{8,24},{12,28},{16,0},{20,4},{24,8},{28,12},{1,17},{... | collective-permute-start | bytes 442376 | tf_op jit(solution)/shard_map/ppermute | solution.py:457
  51.0 3.7 %collective-permute-start.11 = (bf16[4,8,96]{2,1,0:T(8,128)(2,1)S(1)}, bf16[4,8,96]{2,1,0:T(8,128)(2,1)S(1)}, u32[]{:S(2)}, u32[]{:S(2)}) collective-permute-start(bf16[4,8,96]{2,1,0:T(8,128)(2,1)S(1)} %get-tuple-element.89), channel_id=1, source_target_pairs={{0,4},{4,0},{8,12},{12,8},{16,20},{20,16},{24,28},{28,24},{1,5},{5... | collective-permute-start | bytes 18440 | tf_op jit(solution)/shard_map/ppermute | solution.py:457
  54.7 4.1 %collective-permute-start.12 = (bf16[2,8,96]{2,1,0:T(8,128)(2,1)S(1)}, bf16[2,8,96]{2,1,0:T(8,128)(2,1)S(1)}, u32[]{:S(2)}, u32[]{:S(2)}) collective-permute-start(bf16[2,8,96]{2,1,0:T(8,128)(2,1)S(1)} %get-tuple-element.91), channel_id=1, source_target_pairs={{0,8},{4,12},{8,0},{12,4},{16,24},{20,28},{24,16},{28,20},{1,9},{5... | collective-permute-start | bytes 9224 | tf_op jit(solution)/shard_map/ppermute | solution.py:457
  58.7 4.5 %collective-permute-start.13 = (bf16[1,8,96]{2,1,0:T(8,128)(2,1)S(1)}, bf16[1,8,96]{2,1,0:T(8,128)(2,1)S(1)}, u32[]{:S(2)}, u32[]{:S(2)}) collective-permute-start(bf16[1,8,96]{2,1,0:T(8,128)(2,1)S(1)} %get-tuple-element.93), channel_id=1, source_target_pairs={{0,16},{4,20},{8,24},{12,28},{16,0},{20,4},{24,8},{28,12},{1,17},{... | collective-permute-start | bytes 4616 | tf_op jit(solution)/shard_map/ppermute | solution.py:457
  63.2 1.2 %collective-permute-start.14 = (f32[8,96]{1,0:T(8,128)S(1)}, f32[8,96]{1,0:T(8,128)S(1)}, u32[]{:S(2)}, u32[]{:S(2)}) collective-permute-start(f32[8,96]{1,0:T(8,128)S(1)} %shard_map.235.own_ref.small_ref), channel_id=1, source_target_pairs={{0,1},{1,0},{2,3},{3,2},{4,5},{5,4},{6,7},{7,6},{8,9},{9,8},{10,11... | collective-permute-start | bytes 9224 | tf_op jit(solution)/shard_map/ppermute | solution.py:457
  64.4 3.6 %collective-permute-start.15 = (f32[8,96]{1,0:T(8,128)S(1)}, f32[8,96]{1,0:T(8,128)S(1)}, u32[]{:S(2)}, u32[]{:S(2)}) collective-permute-start(f32[8,96]{1,0:T(8,128)S(1)} %shard_map.236.norms_ref), channel_id=1, source_target_pairs={{0,2},{1,3},{2,0},{3,1},{4,6},{5,7},{6,4},{7,5},{8,10},{9,11},{10,... | collective-permute-start | bytes 9224 | tf_op jit(solution)/shard_map/ppermute | solution.py:457
